TPU v7x, 32 devices: a whole 2x2x4 slice. The times are simulated.
32 devices in a mesh: dp: 8 (over y, x, core), seq: 4 (over z).
Axes of the slice: x: 2, y: 2, z: 4, core: 2. Of those that a mesh axis runs over, the one named last changes fastest.
Arguments:
- char_ids: int32 [8, 512, 50], P('dp', 'seq'), may hold values from 0 to 261
- segment_ids: int32 [8, 512], P('dp'), may hold values from 0 to 3, never falling along the last dimension, each value on 1 to 256 neighbouring positions
- pad_mask: int32 [8, 512], P('dp'), may hold values 0 or 1
- cotangent: bfloat16 [8, 512, 768], P('dp', 'seq'), may hold values from -6 to 6
- char_table: bfloat16 [262, 16], replicated, may hold values from -6 to 6
- conv_weight: bfloat16 [7, 16, 2048], replicated, may hold values from -0.5 to 0.5
- conv_bias: bfloat16 [2048], replicated, may hold values from -2 to 2
- hw_weight: bfloat16 [2, 2048, 4096], P(None, 'dp'), may hold values from -0.125 to 0.125
- hw_bias: bfloat16 [2, 4096], P(None, 'dp'), may hold values from -3 to 3
- proj_weight: bfloat16 [2048, 768], P('dp'), may hold values from -0.125 to 0.125
- pos_table: bfloat16 [512, 768], P(None, 'dp'), may hold values from -6 to 6
- qkv_weight: bfloat16 [768, 2304], P('dp'), may hold values from -0.3125 to 0.3125
- out_weight: bfloat16 [768, 768], P('dp'), may hold values from -0.875 to 0.875
- ff_in_weight: bfloat16 [768, 3072], P('dp'), may hold values from -0.21875 to 0.21875
- ff_out_weight: bfloat16 [3072, 768], P('dp'), may hold values from -0.109375 to 0.109375
- ff_in_bias: bfloat16 [3072], P('dp'), may hold values from -2 to 2
- d_biases: bfloat16 [5, 768], P(None, 'dp'), may hold values from -2 to 2
- norm_gain: bfloat16 [3, 768], P(None, 'dp'), may hold values from 0.5 to 1.5
- norm_shift: bfloat16 [3, 768], P(None, 'dp'), may hold values from -2 to 2
Outputs:
- output: bfloat16 [8, 512, 768], P('dp', 'seq')
- char_table_grad: float32 [262, 16], replicated
- conv_weight_grad: float32 [7, 16, 2048], replicated
- conv_bias_grad: float32 [2048], replicated
- hw_weight_grad: float32 [2, 2048, 4096], P(None, 'dp')
- hw_bias_grad: float32 [2, 4096], P(None, 'dp')
- proj_weight_grad: float32 [2048, 768], P('dp')
- pos_table_grad: float32 [512, 768], P(None, 'dp')
- qkv_weight_grad: float32 [768, 2304], P('dp')
- out_weight_grad: float32 [768, 768], P('dp')
- ff_in_weight_grad: float32 [768, 3072], P('dp')
- ff_out_weight_grad: float32 [3072, 768], P('dp')
- ff_in_bias_grad: float32 [3072], P('dp')
- d_biases_grad: float32 [5, 768], P(None, 'dp')
- norm_gain_grad: float32 [3, 768], P(None, 'dp')
- norm_shift_grad: float32 [3, 768], P(None, 'dp')
Inputs may be any that keep to these rules, and one draw needn't show every extreme that they name: `segment_ids`: segment numbers never fall along a row; one segment spans 1 to 256 words.
All inputs are finite; a program needn't handle non-finite values. No bound on the sum of `pad_mask` on one device may be relied on, other than what follows from the above.
Results may differ from a plain program's by a relative error of at most 0.028.
The roundings to bfloat16 on the way count: a program that leaves them out, or rounds other values in their place, can miss the bound.
Values may be sent and summed in bfloat16 or wider, within the bound.
No kernel may reach another device: no remote copies, remote signals or barrier semaphores. Data moves between devices by JAX's collectives and lax.ppermute only.
A program may use at most 448 MiB of HBM per device.

v0:
```python
import math

import jax
import jax.numpy as jnp
import numpy as np
from jax import lax
from jax.sharding import PartitionSpec as P

HDIM = 64


eps_norm = 1e-12
masked_score = -1e30
width_shares = (1, 1, 2, 4, 8, 16, 32)


def filter_widths(filters):
    per_share = filters // 64
    return np.repeat(
        np.arange(1, len(width_shares) + 1),
        [per_share * share_count for share_count in width_shares],
    )


def layer_norm(inputs, gain_row, shift_row):
    centred = inputs - jnp.mean(inputs, axis=-1, keepdims=True)
    spread = jnp.mean(centred * centred, axis=-1, keepdims=True)
    return centred * lax.rsqrt(spread + eps_norm) * gain_row + shift_row


def highway_mix(gate_values, carried):
    filters = carried.shape[-1]
    opened = jax.nn.sigmoid(gate_values[:, filters:])
    return opened * carried + (1.0 - opened) * jax.nn.relu(gate_values[:, :filters])


def gelu_exact(inputs):
    return jax.nn.gelu(inputs, approximate=False)


def product(left_side, right_side):
    return jnp.dot(left_side, right_side, preferred_element_type=jnp.float32)


def product_tn(left_side, right_side):
    return lax.dot_general(
        left_side, right_side, (((0,), (0,)), ((), ())), preferred_element_type=jnp.float32
    )


def product_nt(left_side, right_side):
    return lax.dot_general(
        left_side, right_side, (((1,), (1,)), ((), ())), preferred_element_type=jnp.float32
    )


def char_windows(word_ids, char_rows, tap_count):
    word_count, char_len = word_ids.shape
    char_count = char_rows.shape[0]
    onehot = (
        word_ids.reshape(-1)[:, None] == jnp.arange(char_count, dtype=jnp.int32)[None, :]
    ).astype(jnp.bfloat16)
    vectors = product(onehot, char_rows).astype(jnp.bfloat16).reshape(word_count, char_len, -1)
    padded = jnp.pad(vectors, ((0, 0), (0, tap_count - 1), (0, 0)))
    char_taps = jnp.stack(
        [padded[:, tap_index : tap_index + char_len, :] for tap_index in range(tap_count)], axis=2
    )
    return (onehot, char_taps.reshape(word_count * char_len, -1))


def shards(
    char_ids,
    segment_ids,
    pad_mask,
    cotangent,
    char_table,
    conv_weight,
    conv_bias,
    hw_weight,
    hw_bias,
    proj_weight,
    pos_table,
    qkv_weight,
    out_weight,
    ff_in_weight,
    ff_out_weight,
    ff_in_bias,
    d_biases,
    norm_gain,
    norm_shift,
):
    (
        highway_full,
        highway_bias,
        proj_full,
        pos_full,
        qkv_full,
        out_full,
        inner_full,
        outer_full,
        inner_bias,
        bias_full,
        gain_full,
        shift_full,
    ) = (
        lax.all_gather(hw_weight, "dp", axis=1, tiled=True),
        lax.all_gather(hw_bias, "dp", axis=1, tiled=True),
        lax.all_gather(proj_weight, "dp", axis=0, tiled=True),
        lax.all_gather(pos_table, "dp", axis=1, tiled=True),
        lax.all_gather(qkv_weight, "dp", axis=0, tiled=True),
        lax.all_gather(out_weight, "dp", axis=0, tiled=True),
        lax.all_gather(ff_in_weight, "dp", axis=0, tiled=True),
        lax.all_gather(ff_out_weight, "dp", axis=0, tiled=True),
        lax.all_gather(ff_in_bias, "dp", axis=0, tiled=True),
        lax.all_gather(d_biases, "dp", axis=1, tiled=True),
        lax.all_gather(norm_gain, "dp", axis=1, tiled=True),
        lax.all_gather(norm_shift, "dp", axis=1, tiled=True),
    )
    seqs_here, local_len, char_len = char_ids.shape
    tap_count, char_dim, filters = conv_weight.shape
    model_dim = cotangent.shape[2]
    seq_len = segment_ids.shape[1]
    head_count = model_dim // HDIM
    highway_depth = highway_full.shape[0]
    word_count = seqs_here * local_len
    score_scale = HDIM ** (-0.5)
    bias_rows = bias_full.astype(jnp.float32)
    gain_rows = gain_full.astype(jnp.float32)
    shift_rows = shift_full.astype(jnp.float32)
    widths = filter_widths(filters)
    tap_mask = np.arange(tap_count)[:, None] < widths[None, :]
    masked_kernel = (conv_weight * jnp.asarray(tap_mask, jnp.bfloat16)[:, None, :]).reshape(
        tap_count * char_dim, filters
    )
    valid_place = jnp.asarray(np.arange(char_len)[:, None] <= char_len - widths[None, :])
    word_block = math.gcd(word_count, 32)
    block_count = word_count // word_block
    id_blocks = char_ids.reshape(block_count, word_block, char_len)

    def embed_forward(block_ids):
        unused, char_taps = char_windows(block_ids, char_table, tap_count)
        conv_out = (product(char_taps, masked_kernel) + conv_bias.astype(jnp.float32)).reshape(
            word_block, char_len, filters
        )
        conv_out = jnp.where(valid_place[None], conv_out, masked_score)
        return (jnp.max(conv_out, axis=1), jnp.argmax(conv_out, axis=1))

    pooled, top_place = lax.map(embed_forward, id_blocks)
    pooled = pooled.reshape(word_count, filters)
    hidden = jax.nn.relu(pooled)
    carried_list = []
    gates_list = []
    for highway_layer in range(highway_depth):
        carried_list.append(hidden)
        gate_values = product(
            hidden.astype(jnp.bfloat16), highway_full[highway_layer]
        ) + highway_bias[highway_layer].astype(jnp.float32)
        gates_list.append(gate_values)
        hidden = highway_mix(gate_values, hidden)
    top_hidden = hidden.astype(jnp.bfloat16)
    projected = product(top_hidden, proj_full) + bias_rows[0]
    row_start = lax.axis_index("seq") * local_len
    pos_rows = lax.dynamic_slice_in_dim(pos_full, row_start, local_len, 0).astype(jnp.float32)
    summed = (projected.reshape(seqs_here, local_len, model_dim) + pos_rows[None]).reshape(
        word_count, model_dim
    )
    embedded = layer_norm(summed, gain_rows[0], shift_rows[0])
    embedded_b = embedded.astype(jnp.bfloat16)
    qkv_shift = jnp.concatenate([bias_rows[1], jnp.zeros_like(bias_rows[1]), bias_rows[2]])
    qkv = (product(embedded_b, qkv_full) + qkv_shift).astype(jnp.bfloat16)
    queries = qkv[:, :model_dim].reshape(seqs_here, local_len, head_count, HDIM)
    keys_local = qkv[:, model_dim : 2 * model_dim].reshape(seqs_here, local_len, model_dim)
    values_local = qkv[:, 2 * model_dim :].reshape(seqs_here, local_len, model_dim)
    keys_full, values_full = (
        lax.all_gather(keys_local, "seq", axis=1, tiled=True),
        lax.all_gather(values_local, "seq", axis=1, tiled=True),
    )
    query_segs = lax.dynamic_slice_in_dim(segment_ids, row_start, local_len, 1)
    query_pos = row_start + jnp.arange(local_len, dtype=jnp.int32)
    same_segment = query_segs[:, :, None] == segment_ids[:, None, :]
    open_key = (pad_mask[:, None, :] == 0) | (
        query_pos[:, None] == jnp.arange(seq_len, dtype=jnp.int32)[None, :]
    )[None]
    allowed = (same_segment & open_key)[:, None]

    def score_of(key_rows):
        raw_scores = (
            jnp.einsum(
                "sqhd,skhd->shqk",
                queries,
                key_rows.reshape(seqs_here, seq_len, head_count, HDIM),
                preferred_element_type=jnp.float32,
            )
            * score_scale
        )
        return jnp.where(allowed, raw_scores, masked_score)

    scores = score_of(keys_full)
    row_top = jnp.max(scores, axis=-1, keepdims=True)
    exp_scores = jnp.exp(scores - row_top)
    denominator = jnp.sum(exp_scores, axis=-1, keepdims=True)
    attn_probs = (exp_scores / denominator).astype(jnp.bfloat16)
    log_total = row_top + jnp.log(denominator)
    attended = (
        jnp.einsum(
            "shqk,skhd->sqhd",
            attn_probs,
            values_full.reshape(seqs_here, seq_len, head_count, HDIM),
            preferred_element_type=jnp.float32,
        )
        .reshape(word_count, model_dim)
        .astype(jnp.bfloat16)
    )
    attn_out = product(attended, out_full) + bias_rows[3]
    first_input = embedded + attn_out
    first_norm = layer_norm(first_input, gain_rows[1], shift_rows[1])
    first_b = first_norm.astype(jnp.bfloat16)
    ffn_up = product(first_b, inner_full) + inner_bias.astype(jnp.float32)
    ffn_act = gelu_exact(ffn_up).astype(jnp.bfloat16)
    ffn_down = product(ffn_act, outer_full) + bias_rows[4]
    second = first_norm + ffn_down
    result = layer_norm(second, gain_rows[2], shift_rows[2])
    grad_out = cotangent.reshape(word_count, model_dim).astype(jnp.float32)
    unused, norm_back = jax.vjp(layer_norm, second, gain_rows[2], shift_rows[2])
    d_second, gain_grad2, shift_grad2 = norm_back(grad_out)
    grad_down = d_second.astype(jnp.bfloat16)
    outer_grad = product_tn(ffn_act, grad_down)
    bias_grad4 = jnp.sum(grad_down.astype(jnp.float32), axis=0)
    unused, gelu_back = jax.vjp(gelu_exact, ffn_up)
    grad_up = gelu_back(product_nt(grad_down, outer_full))[0].astype(jnp.bfloat16)
    inner_grad = product_tn(first_b, grad_up)
    inner_bias_grad = jnp.sum(grad_up.astype(jnp.float32), axis=0)
    d_first = d_second + product_nt(grad_up, inner_full)
    unused, norm_back = jax.vjp(layer_norm, first_input, gain_rows[1], shift_rows[1])
    d_res, gain_grad1, shift_grad1 = norm_back(d_first)
    grad_attn = d_res.astype(jnp.bfloat16)
    out_grad = product_tn(attended, grad_attn)
    bias_grad3 = jnp.sum(grad_attn.astype(jnp.float32), axis=0)
    grad_attended = (
        product_nt(grad_attn, out_full)
        .astype(jnp.bfloat16)
        .reshape(seqs_here, local_len, head_count, HDIM)
    )
    keys_back, values_back = (keys_full, values_full)
    probs_again = jnp.exp(score_of(keys_back) - log_total)
    probs_again_b = probs_again.astype(jnp.bfloat16)
    key_heads = keys_back.reshape(seqs_here, seq_len, head_count, HDIM)
    value_heads = values_back.reshape(seqs_here, seq_len, head_count, HDIM)
    d_probs = jnp.einsum(
        "sqhd,skhd->shqk", grad_attended, value_heads, preferred_element_type=jnp.float32
    )
    grad_scores = (
        probs_again * (d_probs - jnp.sum(probs_again * d_probs, axis=-1, keepdims=True))
    ).astype(jnp.bfloat16)
    d_queries = (
        jnp.einsum("shqk,skhd->sqhd", grad_scores, key_heads, preferred_element_type=jnp.float32)
        * score_scale
    )
    d_keys_all = (
        jnp.einsum("shqk,sqhd->skhd", grad_scores, queries, preferred_element_type=jnp.float32)
        * score_scale
    )
    d_values_all = jnp.einsum(
        "shqk,sqhd->skhd", probs_again_b, grad_attended, preferred_element_type=jnp.float32
    )
    d_keys, d_values = (
        lax.psum_scatter(
            d_keys_all.reshape(seqs_here, seq_len, model_dim).astype(jnp.bfloat16),
            "seq",
            scatter_dimension=1,
            tiled=True,
        ).astype(jnp.float32),
        lax.psum_scatter(
            d_values_all.reshape(seqs_here, seq_len, model_dim).astype(jnp.bfloat16),
            "seq",
            scatter_dimension=1,
            tiled=True,
        ).astype(jnp.float32),
    )
    grad_qkv = jnp.concatenate(
        [
            d_queries.reshape(word_count, model_dim),
            d_keys.reshape(word_count, model_dim),
            d_values.reshape(word_count, model_dim),
        ],
        axis=1,
    ).astype(jnp.bfloat16)
    qkv_grad = product_tn(embedded_b, grad_qkv)
    bias_grad1 = jnp.sum(grad_qkv[:, :model_dim].astype(jnp.float32), axis=0)
    bias_grad2 = jnp.sum(grad_qkv[:, 2 * model_dim :].astype(jnp.float32), axis=0)
    d_embedded = d_res + product_nt(grad_qkv, qkv_full)
    unused, norm_back = jax.vjp(layer_norm, summed, gain_rows[0], shift_rows[0])
    d_summed, gain_grad0, shift_grad0 = norm_back(d_embedded)
    pos_local = jnp.sum(d_summed.reshape(seqs_here, local_len, model_dim), axis=0)
    pos_grad = lax.dynamic_update_slice_in_dim(
        jnp.zeros((seq_len, model_dim), jnp.float32), pos_local, row_start, 0
    )
    grad_proj = d_summed.astype(jnp.bfloat16)
    proj_grad = product_tn(top_hidden, grad_proj)
    bias_grad0 = jnp.sum(grad_proj.astype(jnp.float32), axis=0)
    d_hidden = product_nt(grad_proj, proj_full)
    kernel_grads = [None] * highway_depth
    shift_grads = [None] * highway_depth
    for highway_layer in reversed(range(highway_depth)):
        carried = carried_list[highway_layer]
        unused, mix_back = jax.vjp(highway_mix, gates_list[highway_layer], carried)
        d_gates, d_carried = mix_back(d_hidden)
        grad_gates = d_gates.astype(jnp.bfloat16)
        kernel_grads[highway_layer] = product_tn(carried.astype(jnp.bfloat16), grad_gates)
        shift_grads[highway_layer] = jnp.sum(grad_gates.astype(jnp.float32), axis=0)
        d_hidden = d_carried + product_nt(grad_gates, highway_full[highway_layer])
    grad_pooled = jnp.where(pooled > 0, d_hidden, 0.0).astype(jnp.bfloat16)

    def embed_backward(running, inputs):
        weight_sum, bias_sum, table_sum = running
        block_ids, place_block, grad_block = inputs
        onehot, char_taps = char_windows(block_ids, char_table, tap_count)
        grad_conv = jnp.where(
            jnp.arange(char_len, dtype=jnp.int32)[None, :, None] == place_block[:, None, :],
            grad_block[:, None, :],
            jnp.zeros((), jnp.bfloat16),
        ).reshape(word_block * char_len, filters)
        weight_sum = weight_sum + product_tn(char_taps, grad_conv)
        bias_sum = bias_sum + jnp.sum(grad_block.astype(jnp.float32), axis=0)
        d_taps = product_nt(grad_conv, masked_kernel).reshape(
            word_block, char_len, tap_count, char_dim
        )
        spread = jnp.zeros((word_block, char_len + tap_count - 1, char_dim), jnp.float32)
        for tap_index in range(tap_count):
            spread = spread.at[:, tap_index : tap_index + char_len].add(d_taps[:, :, tap_index])
        grad_chars = (
            spread[:, :char_len].reshape(word_block * char_len, char_dim).astype(jnp.bfloat16)
        )
        table_sum = table_sum + product_tn(onehot, grad_chars)
        return ((weight_sum, bias_sum, table_sum), None)

    start_sums = (
        jnp.zeros((tap_count * char_dim, filters), jnp.float32),
        jnp.zeros((filters,), jnp.float32),
        jnp.zeros(char_table.shape, jnp.float32),
    )
    conv_sums, unused = lax.scan(
        embed_backward,
        start_sums,
        (id_blocks, top_place, grad_pooled.reshape(block_count, word_block, filters)),
    )
    conv_weight_grad = (
        conv_sums[0] * jnp.asarray(np.repeat(tap_mask, char_dim, axis=0), jnp.float32)
    ).reshape(tap_count, char_dim, filters)
    table_total, conv_total, conv_bias_total = lax.psum(
        (conv_sums[2], conv_weight_grad, conv_sums[1]), ("dp", "seq")
    )
    weight_grads = (
        jnp.stack(kernel_grads),
        jnp.stack(shift_grads),
        proj_grad,
        pos_grad,
        qkv_grad,
        out_grad,
        inner_grad,
        outer_grad,
        inner_bias_grad,
        jnp.stack([bias_grad0, bias_grad1, bias_grad2, bias_grad3, bias_grad4]),
        jnp.stack([gain_grad0, gain_grad1, gain_grad2]),
        jnp.stack([shift_grad0, shift_grad1, shift_grad2]),
    )
    sliced = (
        lax.psum_scatter(weight_grads[0], "dp", scatter_dimension=1, tiled=True),
        lax.psum_scatter(weight_grads[1], "dp", scatter_dimension=1, tiled=True),
        lax.psum_scatter(weight_grads[2], "dp", scatter_dimension=0, tiled=True),
        lax.psum_scatter(weight_grads[3], "dp", scatter_dimension=1, tiled=True),
        lax.psum_scatter(weight_grads[4], "dp", scatter_dimension=0, tiled=True),
        lax.psum_scatter(weight_grads[5], "dp", scatter_dimension=0, tiled=True),
        lax.psum_scatter(weight_grads[6], "dp", scatter_dimension=0, tiled=True),
        lax.psum_scatter(weight_grads[7], "dp", scatter_dimension=0, tiled=True),
        lax.psum_scatter(weight_grads[8], "dp", scatter_dimension=0, tiled=True),
        lax.psum_scatter(weight_grads[9], "dp", scatter_dimension=1, tiled=True),
        lax.psum_scatter(weight_grads[10], "dp", scatter_dimension=1, tiled=True),
        lax.psum_scatter(weight_grads[11], "dp", scatter_dimension=1, tiled=True),
    )
    summed_grads = (
        lax.psum(sliced[0].astype(jnp.bfloat16), "seq").astype(jnp.float32),
        lax.psum(sliced[1].astype(jnp.bfloat16), "seq").astype(jnp.float32),
        lax.psum(sliced[2].astype(jnp.bfloat16), "seq").astype(jnp.float32),
        lax.psum(sliced[3].astype(jnp.bfloat16), "seq").astype(jnp.float32),
        lax.psum(sliced[4].astype(jnp.bfloat16), "seq").astype(jnp.float32),
        lax.psum(sliced[5].astype(jnp.bfloat16), "seq").astype(jnp.float32),
        lax.psum(sliced[6].astype(jnp.bfloat16), "seq").astype(jnp.float32),
        lax.psum(sliced[7].astype(jnp.bfloat16), "seq").astype(jnp.float32),
        lax.psum(sliced[8].astype(jnp.bfloat16), "seq").astype(jnp.float32),
        lax.psum(sliced[9].astype(jnp.bfloat16), "seq").astype(jnp.float32),
        lax.psum(sliced[10].astype(jnp.bfloat16), "seq").astype(jnp.float32),
        lax.psum(sliced[11].astype(jnp.bfloat16), "seq").astype(jnp.float32),
    )
    output = result.astype(jnp.bfloat16).reshape(seqs_here, local_len, model_dim)
    return (output, table_total, conv_total, conv_bias_total) + tuple(summed_grads)


def solution(mesh):
    placed = (
        P("dp", "seq", None),
        P("dp", None),
        P("dp", None),
        P("dp", "seq", None),
        P(),
        P(),
        P(),
        P(None, "dp", None),
        P(None, "dp"),
        P("dp", None),
        P(None, "dp"),
        P("dp", None),
        P("dp", None),
        P("dp", None),
        P("dp", None),
        P("dp"),
        P(None, "dp"),
        P(None, "dp"),
        P(None, "dp"),
    )
    return jax.shard_map(
        shards,
        mesh=mesh,
        in_specs=placed,
        out_specs=(
            P("dp", "seq", None),
            P(),
            P(),
            P(),
            P(None, "dp", None),
            P(None, "dp"),
            P("dp", None),
            P(None, "dp"),
            P("dp", None),
            P("dp", None),
            P("dp", None),
            P("dp", None),
            P("dp"),
            P(None, "dp"),
            P(None, "dp"),
            P(None, "dp"),
        ),
        check_vma=False,
    )
```

profile of v0, /device:TPU:0, one launch (start us, length us, event | category | flops | bytes accessed | tf_op | source)
XLA Modules:
  0.0 1733.0 jit_solution(7577704498146748608)
XLA Ops:
  12.2 151.9 %while.42 = (s32[]{:T(128)}, f32[4,32,2048]{2,1,0:T(8,128)S(1)}, s32[4,32,2048]{2,1,0:T(8,128)}, s32[4,32,50]{2,1,0:T(8,128)S(1)}, bf16[262,16]{0,1:T(8,128)(2,1...) while((s32[]{:T(128)}, f32[4,32,2048]{2,1,0:T(8,128)S(1)}, ...), condition=%wide.region_2.3_spmd.clone.clone, body=%wide.region_0.2_spmd.sunk.clone.sunk.clone | while | flops 783319424 | bytes 57710120 | solution.py:148
  26.2 12.8 reshape.884
  39.0 12.2 iota_reduce_fusion.3
  63.7 12.3 reshape.884
  75.9 13.0 iota_reduce_fusion.3
  101.4 12.4 reshape.884
  113.7 12.4 iota_reduce_fusion.3
  138.6 12.6 reshape.884
  249.7 20.4 %all-gather.1 = bf16[512,768]{1,0:T(8,128)(2,1)S(1)} all-gather(bf16[128,768]{1,0:T(8,128)(2,1)S(1)} %get-tuple-element.525), channel_id=3, replica_groups=mesh['dp'=8,'seq'=4] {'seq'}, dimensions={0}, use_global_device_ids=true | all-gather | bytes 983040 | tf_op jit(solution)/shard_map/all_gather | solution.py:175
  271.2 18.1 %all-gather = bf16[512,768]{1,0:T(8,128)(2,1)S(1)} all-gather(bf16[128,768]{1,0:T(8,128)(2,1)S(1)} %get-tuple-element.527), channel_id=2, replica_groups=mesh['dp'=8,'seq'=4] {'seq'}, dimensions={0}, use_global_device_ids=true | all-gather | bytes 983040 | tf_op jit(solution)/shard_map/all_gather | solution.py:176
  319.6 32.2 %all-gather.23.cloned.1.call-done = bf16[3072,768]{1,0:T(8,128)(2,1)} async-done(((bf16[384,768]{1,0:T(8,128)(2,1)}), bf16[3072,768]{1,0:T(8,128)(2,1)}) %all-gather.23.cloned.1.call-update) | async-done | bytes 4718608 | tf_op jit(solution)/shard_map/all_gather | solution.py:113
  388.5 13.2 reduce-scatter.42.cloned.1.call-done
  403.3 23.9 %reduce-scatter.40.cloned.1.call-done = bf16[128,768]{1,0:T(8,128)(2,1)} async-done(((bf16[512,768]{1,0:T(8,128)(2,1)}), bf16[128,768]{1,0:T(8,128)(2,1)}) %reduce-scatter.40.cloned.1.call-update) | async-done | bytes 196624
  474.9 13.8 convolution_bitcast_fusion.1
  488.8 13.5 convolution_bitcast_fusion
  502.2 45.5 %pad_maximum_fusion = f32[2,2048,4096]{2,1,0:T(8,128)} fusion(f32[1,2048,4096]{2,1,0:T(8,128)} %convolution_bitcast_fusion, f32[1,2048,4096]{2,1,0:T(8,128)} %convolution_bitcast_fusion.1), kind=kLoop, calls=%fused_computation.60 | loop fusion | flops 16777216 | bytes 134217728 | tf_op jit(solution)/shard_map/stack | solution.py:354
  581.8 67.5 %reduce-scatter.32.cloned.1.call-done = f32[96,2304]{1,0:T(8,128)} async-done(((f32[768,2304]{1,0:T(8,128)}), f32[96,2304]{1,0:T(8,128)}) %reduce-scatter.32.cloned.1.call-update) | async-done | bytes 884752 | tf_op jit(solution)/shard_map/reduce_scatter | solution.py:372
  651.3 78.4 %reduce-scatter.36.cloned.1.call-done = f32[96,3072]{1,0:T(8,128)} async-done(((f32[768,3072]{1,0:T(8,128)}), f32[96,3072]{1,0:T(8,128)}) %reduce-scatter.36.cloned.1.call-update) | async-done | bytes 1179664 | tf_op jit(solution)/shard_map/reduce_scatter | solution.py:374
  731.9 78.1 %reduce-scatter.38.cloned.1.call-done = f32[384,768]{1,0:T(8,128)} async-done(((f32[3072,768]{1,0:T(8,128)}), f32[384,768]{1,0:T(8,128)}) %reduce-scatter.38.cloned.1.call-update) | async-done | bytes 1179664 | tf_op jit(solution)/shard_map/reduce_scatter | solution.py:375
  812.1 385.5 %reduce-scatter.26.cloned.1.call-done = f32[2,256,4096]{2,1,0:T(8,128)} async-done(((f32[2,2048,4096]{2,1,0:T(8,128)}), f32[2,256,4096]{2,1,0:T(8,128)}) %reduce-scatter.26.cloned.1.call-update) | async-done | bytes 8388624 | tf_op jit(solution)/shard_map/reduce_scatter | solution.py:368
  1204.4 293.9 %while.43 = (s32[]{:T(128)}, f32[112,2048]{1,0:T(8,128)S(1)}, f32[2048]{0:T(1024)S(1)}, f32[262,16]{0,1:T(8,128)}, s32[4,32,50]{2,1,0:T(8,128)}, /*index=5*/bf16...) while((s32[]{:T(128)}, f32[112,2048]{1,0:T(8,128)S(1)}, ...), condition=%wide.region_22.23_spmd.clone.clone, body=%wide.region_20.22_spmd.clone.sunk.clone | while | flops 1509560320 | bytes 38898288 | solution.py:342
  1501.8 24.6 %all-reduce.7 = bf16[3072]{0:T(1024)(128)(2,1)S(1)} all-reduce(f32[3072]{0:T(1024)S(1)} %copy-done.79), channel_id=14, replica_groups=mesh['dp'=8,'seq'=4] {'dp'}, use_global_device_ids=true, to_apply=%region_45.46.clone | all-reduce | flops 3072 | bytes 18432
  1526.5 47.3 %all-reduce.8 = (f32[262,16]{0,1:T(8,128)}, f32[2048]{0:T(1024)}) all-reduce(f32[262,16]{0,1:T(8,128)S(1)} %copy-done.61, f32[2048]{0:T(1024)S(1)} %get-tuple-element.379), channel_id=1, replica_groups=mesh['dp'=8,'seq'=4] {'dp','seq'}, use_global_device_ids=true, to_apply=%region_23.24 | all-reduce | flops 6240 | bytes 49920 | tf_op jit(solution)/shard_map/psum | solution.py:350
  1605.3 118.4 %all-reduce.14.cloned.1.call-done = f32[7,16,2048]{2,1,0:T(8,128)} async-done(((f32[7,16,2048]{2,1,0:T(8,128)}), f32[7,16,2048]{2,1,0:T(8,128)}) %all-reduce.14.cloned.1.call-update) | async-done | bytes 917520 | tf_op jit(solution)/shard_map/psum | solution.py:350
  (648 shorter events, 647.0 us)
Async XLA Ops:
  7.2 217.5 %all-gather.13.cloned.1.call-start = ((), (), s32[]{:S(2)}) async-start(), calls=%async_computation.13 | async-start | bytes 37748736 | tf_op jit(solution)/shard_map/all_gather | solution.py:106
  8.0 234.5 %all-gather.15.cloned.1.call-start = ((), (), s32[]{:S(2)}) async-start(), calls=%async_computation.14 | async-start | bytes 3538944 | tf_op jit(solution)/shard_map/all_gather | solution.py:108
  8.7 236.9 %all-gather.17.cloned.1.call-start = ((), (), s32[]{:S(2)}) async-start(), calls=%async_computation.15 | async-start | bytes 3981312 | tf_op jit(solution)/shard_map/all_gather | solution.py:110
  9.5 286.6 %all-gather.19.cloned.1.call-start = ((), (), s32[]{:S(2)}) async-start(), calls=%async_computation.16 | async-start | bytes 1327104 | tf_op jit(solution)/shard_map/all_gather | solution.py:111
  10.0 301.1 %all-gather.21.cloned.1.call-start = ((), (), s32[]{:S(2)}) async-start(), calls=%async_computation.17 | async-start | bytes 5308416 | tf_op jit(solution)/shard_map/all_gather | solution.py:112
  10.6 341.2 %all-gather.23.cloned.1.call-start = ((), (), s32[]{:S(2)}) async-start(), calls=%async_computation.18 | async-start | bytes 5308416 | tf_op jit(solution)/shard_map/all_gather | solution.py:113
  11.2 390.5 %reduce-scatter.42.cloned.1.call-start = ((), (), s32[]{:S(2)}) async-start(), calls=%async_computation.28 | async-start | bytes 983040
  164.1 58.9 %copy-start.8 = (f32[4,32,2048]{2,1,0:T(8,128)}, f32[4,32,2048]{2,1,0:T(8,128)S(1)}, u32[]{:S(2)}) copy-start(f32[4,32,2048]{2,1,0:T(8,128)S(1)} %get-tuple-element.375) | copy-start | bytes 3145732
  164.2 58.9 %copy-start.84 = (s32[1,512]{1,0:T(1,128)S(1)}, s32[1,512]{1,0:T(1,128)}, u32[]{:S(2)}) copy-start(s32[1,512]{1,0:T(1,128)} %param.41) | copy-start | bytes 6148
  165.2 66.7 %copy-start.10 = (f32[4,32,2048]{2,1,0:T(8,128)}, f32[4,32,2048]{2,1,0:T(8,128)S(1)}, u32[]{:S(2)}) copy-start(f32[4,32,2048]{2,1,0:T(8,128)S(1)} %broadcast_maximum_fusion) | copy-start | bytes 3145732
  378.3 48.9 %reduce-scatter.40.cloned.1.call-start = ((), (), s32[]{:S(2)}) async-start(), calls=%async_computation.27 | async-start | bytes 983040
  385.7 183.6 %reduce-scatter.34.cloned.1.call-start = ((), (), s32[]{:S(2)}) async-start(), calls=%async_computation.24 | async-start | bytes 2654208 | tf_op jit(solution)/shard_map/reduce_scatter | solution.py:373
  387.8 183.2 %reduce-scatter.30.cloned.1.call-start = ((), (), s32[]{:S(2)}) async-start(), calls=%async_computation.22 | async-start | bytes 1769472 | tf_op jit(solution)/shard_map/reduce_scatter | solution.py:371
  437.2 142.6 %reduce-scatter.28.cloned.1.call-start = ((), (), s32[]{:S(2)}) async-start(), calls=%async_computation.21 | async-start | bytes 7077888 | tf_op jit(solution)/shard_map/reduce_scatter | solution.py:370
  440.9 208.4 %reduce-scatter.32.cloned.1.call-start = ((), (), s32[]{:S(2)}) async-start(), calls=%async_computation.23 | async-start | bytes 7962624 | tf_op jit(solution)/shard_map/reduce_scatter | solution.py:372
  445.2 284.5 %reduce-scatter.36.cloned.1.call-start = ((), (), s32[]{:S(2)}) async-start(), calls=%async_computation.25 | async-start | bytes 10616832 | tf_op jit(solution)/shard_map/reduce_scatter | solution.py:374
  451.5 358.4 %reduce-scatter.38.cloned.1.call-start = ((), (), s32[]{:S(2)}) async-start(), calls=%async_computation.26 | async-start | bytes 10616832 | tf_op jit(solution)/shard_map/reduce_scatter | solution.py:375
  457.7 739.9 %reduce-scatter.26.cloned.1.call-start = ((), (), s32[]{:S(2)}) async-start(), calls=%async_computation.20 | async-start | bytes 75497472 | tf_op jit(solution)/shard_map/reduce_scatter | solution.py:368
  547.9 1025.9 %reduce-scatter.50.cloned.1.call-start = ((), (), s32[]{:S(2)}) async-start(), calls=%async_computation.32 | async-start | bytes 442368
  552.3 1022.3 %reduce-scatter.48.cloned.1.call-start = ((), (), s32[]{:S(2)}) async-start(), calls=%async_computation.31 | async-start | bytes 442368
  555.0 1020.5 %reduce-scatter.46.cloned.1.call-start = ((), (), s32[]{:S(2)}) async-start(), calls=%async_computation.30 | async-start | bytes 442368
  556.3 1020.1 %reduce-scatter.44.cloned.1.call-start = ((), (), s32[]{:S(2)}) async-start(), calls=%async_computation.29 | async-start | bytes 2359296
  558.4 1033.9 %all-reduce.16.cloned.1.call-start = ((), (), s32[]{:S(2)}) async-start(), calls=%async_computation.33 | async-start | bytes 12910592 | tf_op jit(solution)/shard_map/psum | solution.py:382
  1203.7 520.1 %all-reduce.14.cloned.1.call-start = ((), (), s32[]{:S(2)}) async-start(), calls=%async_computation.19 | async-start | bytes 1835008 | tf_op jit(solution)/shard_map/psum | solution.py:350
  (104 other events, 735.1 us)
Sparse Core Ops, SparseCore 0:
  9.9 163.4 all-gather.12
  175.3 32.3 all-gather.14
  209.7 34.8 all-gather.16
  246.3 24.0 all-gather.18
  272.2 38.9 all-gather.20
  312.9 38.8 all-gather.22
  378.4 23.2 reduce-scatter.41
  404.6 22.5 reduce-scatter.39
  430.5 41.7 reduce-scatter.33
  475.8 38.4 reduce-scatter.29
  518.0 61.7 reduce-scatter.27
  583.8 65.4 reduce-scatter.31
  653.2 76.4 reduce-scatter.35
  733.5 76.4 reduce-scatter.37
  813.8 383.7 reduce-scatter.25
  1200.5 34.0 reduce-scatter.49
  1237.5 34.0 reduce-scatter.47
  1274.6 34.0 reduce-scatter.45
  1312.0 41.5 reduce-scatter.43
  1357.7 231.7 all-reduce.15
  1595.2 128.4 all-reduce.13
where the time goes:
time: 1740 us; the launch traced here: 1730 us
  waiting for transfers between devices  820 us (47%)
  local copies, waits for them, and re-layouts  308 us (18%)
  matrix products  212 us (12%)
  other arithmetic  196 us (11%)
  blocking collectives  179 us (10%)
    reduce_scatter x1, waiting for transfers between devices, shards(): lax.psum_scatter(weight_grads[0], 'dp', scatter_dimension=1, tiled=True)  385 us
    scatter-add x28, local copies, waits for them, and re-layouts, embed_backward(): spread.at[:, tap_index:tap_index + char_len].add(d_taps[:, :, tap_index])  136 us
    psum x1, waiting for transfers between devices, shards(): lax.psum((conv_sums[2], conv_weight_grad, conv_sums[1]), ('dp', 'seq'))  118 us
    reduce_scatter x1, waiting for transfers between devices, shards(): lax.psum_scatter(weight_grads[6], 'dp', scatter_dimension=0, tiled=True)  78.4 us
    reduce_scatter x1, waiting for transfers between devices, shards(): lax.psum_scatter(weight_grads[7], 'dp', scatter_dimension=0, tiled=True)  78.1 us
    dot_general x19, matrix products, product(): return jnp.dot(left_side, right_side, preferred_element_type=jnp.float32)  72.1 us
    dot_general x15, matrix products, product_tn(): lax.dot_general(left_side, right_side, (((0,), (0,)), ((), ())), preferre...  71.2 us
    reduce_scatter x1, waiting for transfers between devices, shards(): lax.psum_scatter(weight_grads[4], 'dp', scatter_dimension=0, tiled=True)  67.5 us
  transfers between devices with their start and end apart: 21, of which 10 were waited for; matrix products, arithmetic and copies ran while one was open for 39% of the time, Pallas kernels for 0%

commit v1 on v0

--- a/solution.py
+++ b/solution.py
@@ -1,9 +1,12 @@
+import functools
 import math
 
 import jax
 import jax.numpy as jnp
 import numpy as np
 from jax import lax
+from jax.experimental import pallas as pl
+from jax.experimental.pallas import tpu as pltpu
 from jax.sharding import PartitionSpec as P
 
 HDIM = 64
@@ -396,6 +399,1089 @@
     return (output, table_total, conv_total, conv_bias_total) + tuple(summed_grads)
 
 
+PLANE = 8
+DEPTH = 4
+CORE_PARTNER = 1
+GROUP = 8
+
+f32 = jnp.float32
+bf16 = jnp.bfloat16
+
+
+def swap(value, axis_name, size, offset):
+    return lax.ppermute(value, axis_name, [(at, at ^ offset) for at in range(size)])
+
+
+def plane_swap(value, offset):
+    return swap(value, "dp", PLANE, offset)
+
+
+def plane_gather(block):
+    even = [block] + [plane_swap(block, offset) for offset in (2, 4, 6)]
+    odd = [plane_swap(piece, CORE_PARTNER) for piece in even]
+    return [piece for pair in zip(even, odd) for piece in pair]
+
+
+def plane_reduce(keep, send):
+    arrived = plane_swap(send, CORE_PARTNER)
+    total = keep[0].astype(f32) + arrived[0].astype(f32)
+    others = [
+        plane_swap((keep[i].astype(f32) + arrived[i].astype(f32)).astype(bf16), 2 * i)
+        for i in range(1, PLANE // 2)
+    ]
+    for piece in others:
+        total = total + piece.astype(f32)
+    return total
+
+
+def line_total(block):
+    first = lax.ppermute(block, "seq", [(0, 1), (3, 2)])
+    paired = block + first
+    second = lax.ppermute(paired, "seq", [(1, 2), (2, 1)])
+    whole = paired + second
+    return whole, lax.ppermute(whole, "seq", [(1, 0), (2, 3)])
+
+
+def line_sum(block):
+    whole, third = line_total(block)
+    place = lax.axis_index("seq")
+    return jnp.where((place == 1) | (place == 2), whole, third)
+
+
+def nn(left_side, right_side):
+    return jnp.dot(left_side, right_side, preferred_element_type=f32)
+
+
+def nt(left_side, right_side):
+    return lax.dot_general(
+        left_side, right_side, (((1,), (1,)), ((), ())), preferred_element_type=f32
+    )
+
+
+def tn(left_side, right_side):
+    return lax.dot_general(
+        left_side, right_side, (((0,), (0,)), ((), ())), preferred_element_type=f32
+    )
+
+
+VMEM = pltpu.VMEM
+SMEM_SPEC = pl.BlockSpec(memory_space=pltpu.SMEM)
+
+
+def whole(count):
+    return [pl.BlockSpec(memory_space=pltpu.VMEM)] * count
+
+
+def call(body, out_shapes, scalar, operands, scratch=(), name=None):
+    return pl.pallas_call(
+        body,
+        out_shape=[jax.ShapeDtypeStruct(s, t) for s, t in out_shapes],
+        in_specs=[SMEM_SPEC] + whole(len(operands)),
+        out_specs=whole(len(out_shapes)),
+        scratch_shapes=list(scratch),
+        name=name,
+        compiler_params=pltpu.CompilerParams(vmem_limit_bytes=58 * 1024 * 1024),
+    )(scalar, *operands)
+
+
+def lookup_body(char_len, d_ref, ids_ref, table_ref, extra_ref, x_ref):
+    words = ids_ref.shape[0]
+    rows, lanes = table_ref.shape
+    width = lanes // GROUP
+    groups = x_ref.shape[1] // lanes
+    lane = lax.broadcasted_iota(jnp.int32, (rows, lanes), 1) // width
+    entry = lax.broadcasted_iota(jnp.int32, (words, rows), 1)
+    total = jnp.zeros((groups * words, lanes), f32)
+    for place in range(GROUP):
+        pieces = []
+        for group in range(groups):
+            at = GROUP * group + place
+            if at < char_len:
+                hit = ids_ref[:, at : at + 1] == entry
+                pieces.append(jnp.where(hit, 1.0, 0.0).astype(bf16))
+            else:
+                pieces.append(jnp.zeros((words, rows), bf16))
+        own = jnp.where(lane == place, table_ref[...].astype(f32), 0.0).astype(bf16)
+        total = total + nn(jnp.concatenate(pieces, axis=0), own)
+    for group in range(groups):
+        x_ref[:words, group * lanes : (group + 1) * lanes] = total[
+            group * words : (group + 1) * words
+        ].astype(bf16)
+    x_ref[words:, :] = extra_ref[...]
+
+
+def fill_taps(taps_ref, weight_ref):
+    depth, filters = weight_ref.shape
+    char_dim = taps_ref.shape[0] // (2 * GROUP)
+    taps_ref[...] = jnp.zeros_like(taps_ref)
+    for place in range(GROUP):
+        taps_ref[
+            place * char_dim : place * char_dim + depth, place * filters : (place + 1) * filters
+        ] = weight_ref[...]
+
+
+def conv_body(char_len, first_masked, words, d_ref, *refs):
+    blocks = refs[:PLANE]
+    (weight_ref, last_ref, bias_ref, h_ref, hb_ref, at_ref, x_ref, ba_ref, bb_ref) = refs[
+        PLANE : PLANE + 9
+    ]
+    taps_ref, extra_ref = refs[PLANE + 9 :]
+    d = d_ref[0]
+    filters = weight_ref.shape[1]
+    held = blocks[0].shape[1]
+    lanes = taps_ref.shape[0] // 2
+    fill_taps(taps_ref, weight_ref)
+    for k in range(PLANE):
+        rows = pl.ds(pl.multiple_of((d ^ k) * words, words), words)
+        x_ref[rows, :held] = blocks[k][:words, :]
+        x_ref[rows, held:] = jnp.zeros((words, x_ref.shape[1] - held), bf16)
+        extra_ref[d ^ k] = blocks[k][words:, : 2 * filters].astype(f32)
+    for half, out in ((0, ba_ref), (PLANE // 2, bb_ref)):
+        source = extra_ref[half + d // 2]
+        out[...] = jnp.where(d % 2 == 0, source[:, :filters], source[:, filters:])
+    last = last_ref[...]
+
+    def one(step, carry):
+        rows = pl.ds(pl.multiple_of(step * words, words), words)
+        best = None
+        for group in range(-(-char_len // GROUP)):
+            count = min(GROUP, char_len - GROUP * group)
+            values = nn(
+                x_ref[rows, group * lanes : (group + 2) * lanes], taps_ref[:, : count * filters]
+            )
+            for place in range(count):
+                at = GROUP * group + place
+                value = values[:, place * filters : (place + 1) * filters]
+                if at >= first_masked:
+                    value = jnp.where(at <= last, value, masked_score)
+                if best is None:
+                    best, where = value, jnp.zeros(value.shape, jnp.int32)
+                else:
+                    where = jnp.where(value > best, at, where)
+                    best = jnp.maximum(value, best)
+        pooled = jnp.maximum(best + bias_ref[...], 0.0)
+        h_ref[rows, :] = pooled
+        hb_ref[rows, :] = pooled.astype(bf16)
+        at_ref[rows, :] = where
+        return carry
+
+    lax.fori_loop(0, PLANE, one, 0)
+
+
+def highway_body(layer, d_ref, *refs):
+    blocks = refs[:PLANE]
+    w_ref, ba_ref, bb_ref, h_ref, open_ref, ra_ref, hn_ref, hb_ref = refs[PLANE:]
+    d = d_ref[0]
+    a = ba_ref[layer : layer + 1, :]
+    b = bb_ref[layer : layer + 1, :]
+    for k in range(PLANE):
+        a = a + nn(blocks[k][...], w_ref[d ^ k, 0, 0])
+        b = b + nn(blocks[k][...], w_ref[d ^ k, 0, 1])
+    opened = jax.nn.sigmoid(b)
+    ra = jnp.maximum(a, 0.0)
+    mixed = opened * h_ref[...] + (1.0 - opened) * ra
+    open_ref[...] = opened
+    ra_ref[...] = ra
+    hn_ref[...] = mixed
+    hb_ref[...] = mixed.astype(bf16)
+
+
+def highway(layer, dvec, blocks, weights, bias_a, bias_b, hidden):
+    words, filters = hidden.shape
+    part = words // 4
+    row = pl.BlockSpec((part, filters), lambda i: (i, 0))
+    depth, parts = weights.shape[1:3]
+    return pl.pallas_call(
+        functools.partial(highway_body, layer),
+        grid=(4,),
+        out_shape=[jax.ShapeDtypeStruct((words, filters), t) for t in (f32, f32, f32, bf16)],
+        in_specs=[SMEM_SPEC]
+        + [row] * PLANE
+        + [
+            pl.BlockSpec((PLANE, 1, parts, filters, filters), lambda i: (0, layer, 0, 0, 0)),
+            pl.BlockSpec(bias_a.shape, lambda i: (0, 0)),
+            pl.BlockSpec(bias_b.shape, lambda i: (0, 0)),
+            row,
+        ],
+        out_specs=[row] * 4,
+        name=f"highway{layer}",
+        compiler_params=pltpu.CompilerParams(vmem_limit_bytes=58 * 1024 * 1024),
+    )(dvec, *blocks, weights, bias_a, bias_b, hidden)
+
+
+def project_body(d_ref, h_ref, w_ref, keep_ref, send_ref):
+    d = d_ref[0]
+    words = keep_ref.shape[1]
+    for i in range(PLANE // 2):
+        for odd, out in ((0, keep_ref), (1, send_ref)):
+            rows = pl.ds(pl.multiple_of((d ^ odd ^ (2 * i)) * words, words), words)
+            out[i] = nn(h_ref[rows, :], w_ref[...]).astype(out.dtype)
+
+
+def unproject_body(words, d_ref, *refs):
+    blocks = refs[:PLANE]
+    w_ref, h_ref, dh_ref, dw_ref, sum_ref = refs[PLANE:]
+    d = d_ref[0]
+    total, rest = None, None
+    for k in range(PLANE):
+        rows = pl.ds(pl.multiple_of((d ^ k) * words, words), words)
+        grad = blocks[k][:words, :]
+        dh_ref[rows, :] = nt(grad, w_ref[...])
+        piece = tn(h_ref[rows, :], grad)
+        total = piece if total is None else total + piece
+        block = blocks[k][...].astype(f32)
+        rest = block if rest is None else rest + block
+    dw_ref[...] = total.astype(dw_ref.dtype)
+    sum_ref[: words + 16, :] = rest
+    sum_ref[words + 16 :, :] = jnp.broadcast_to(over_words(rest[:words]), (16, rest.shape[1]))
+
+
+def highway_back_body(
+    d_ref, dh_ref, open_ref, ra_ref, h_ref, w_ref, ga_ref, gb_ref, dc_ref, sum_ref, keep_ref, send_ref
+):
+    d = d_ref[0]
+    dh = dh_ref[...]
+    opened = open_ref[...]
+    ra = ra_ref[...]
+    closed = 1.0 - opened
+    ga = jnp.where(ra > 0.0, dh * closed, 0.0).astype(bf16)
+    gb = (dh * (h_ref[...] - ra) * (opened * closed)).astype(bf16)
+    ga_ref[...] = ga
+    gb_ref[...] = gb
+    dc_ref[...] = dh * opened
+    filters = ga.shape[1]
+
+    @pl.when(pl.program_id(0) == 0)
+    def first():
+        sum_ref[...] = jnp.zeros_like(sum_ref)
+
+    sum_ref[:, :filters] += jnp.sum(
+        ga.astype(f32).reshape(-1, 8, filters), axis=0
+    )
+    sum_ref[:, filters:] += jnp.sum(
+        gb.astype(f32).reshape(-1, 8, filters), axis=0
+    )
+    for i in range(PLANE // 2):
+        for odd, out in ((1, send_ref), (0, keep_ref)):
+            j = d ^ odd ^ (2 * i)
+            out[i] = (nt(ga, w_ref[j, 0, 0]) + nt(gb, w_ref[j, 0, 1])).astype(out.dtype)
+
+
+def highway_back(layer, dvec, d_hidden, opened, ra, hidden, weights):
+    words, filters = hidden.shape
+    part = words // 4
+    row = pl.BlockSpec((part, filters), lambda i: (i, 0))
+    half = PLANE // 2
+    blocks = pl.BlockSpec((half, part, filters), lambda i: (0, i, 0))
+    parts = weights.shape[2]
+    return pl.pallas_call(
+        highway_back_body,
+        grid=(4,),
+        out_shape=[
+            jax.ShapeDtypeStruct((words, filters), bf16),
+            jax.ShapeDtypeStruct((words, filters), bf16),
+            jax.ShapeDtypeStruct((words, filters), f32),
+            jax.ShapeDtypeStruct((8, 2 * filters), f32),
+            jax.ShapeDtypeStruct((half, words, filters), f32),
+            jax.ShapeDtypeStruct((half, words, filters), bf16),
+        ],
+        in_specs=[SMEM_SPEC]
+        + [row] * 4
+        + [pl.BlockSpec((PLANE, 1, parts, filters, filters), lambda i: (0, layer, 0, 0, 0))],
+        out_specs=[row, row, row, pl.BlockSpec((8, 2 * filters), lambda i: (0, 0)), blocks, blocks],
+        name=f"highway_back{layer}",
+        compiler_params=pltpu.CompilerParams(vmem_limit_bytes=58 * 1024 * 1024),
+    )(dvec, d_hidden, opened, ra, hidden, weights)
+
+
+def highway_grad_body(d_ref, *refs):
+    blocks = refs[:PLANE]
+    ga_ref, gb_ref, sum_ref, out_ref = refs[PLANE:]
+    d = d_ref[0]
+    filters = ga_ref.shape[1]
+    row = jnp.sum(sum_ref[...], axis=0, keepdims=True)
+    pad = out_ref.shape[1] - filters
+    tail = jnp.where(
+        lax.broadcasted_iota(jnp.int32, (pad, 2 * filters), 0) == 0, row, 0.0
+    ).astype(bf16)
+    for k in range(PLANE):
+        out_ref[d ^ k, :filters, :filters] = tn(blocks[k][...], ga_ref[...]).astype(bf16)
+        out_ref[d ^ k, :filters, filters:] = tn(blocks[k][...], gb_ref[...]).astype(bf16)
+        out_ref[d ^ k, filters:, :] = tail
+
+
+def spread_groups(char_len, filters, grad, at, spread_ref, group):
+    count = min(GROUP, char_len - GROUP * group)
+    for place in range(count):
+        hit = at == GROUP * group + place
+        spread_ref[:, place * filters : (place + 1) * filters] = jnp.where(hit, grad, 0.0).astype(
+            bf16
+        )
+    return count
+
+
+def char_back_body(char_len, words, d_ref, h_ref, at_ref, dh_ref, weight_ref, gp_ref, keep_ref, send_ref, taps_ref, spread_ref, chars_ref):
+    d = d_ref[0]
+    filters = h_ref.shape[1]
+    lanes = taps_ref.shape[0] // 2
+    held = keep_ref.shape[2]
+    fill_taps(taps_ref, weight_ref)
+    chars_ref[...] = jnp.zeros_like(chars_ref)
+
+    def one(step, carry):
+        rows = pl.ds(pl.multiple_of(step * 2 * words, 2 * words), 2 * words)
+        grad = jnp.where(h_ref[rows, :] > 0.0, dh_ref[rows, :], 0.0).astype(bf16)
+        gp_ref[rows, :] = grad
+        grad = grad.astype(f32)
+        at = at_ref[rows, :]
+        for group in range(-(-char_len // GROUP)):
+            count = spread_groups(char_len, filters, grad, at, spread_ref, group)
+            piece = nt(spread_ref[:, : count * filters], taps_ref[:, : count * filters])
+            chars_ref[rows, group * lanes : (group + 2) * lanes] += piece
+        return carry
+
+    lax.fori_loop(0, PLANE // 2, one, 0)
+    for i in range(PLANE // 2):
+        for odd, out in ((1, send_ref), (0, keep_ref)):
+            rows = pl.ds(pl.multiple_of((d ^ odd ^ (2 * i)) * words, words), words)
+            out[i] = chars_ref[rows, :held].astype(out.dtype)
+
+
+def conv_grad_body(char_len, d_ref, x_ref, at_ref, gp_ref, dw_ref, spread_ref, xt_ref):
+    filters = gp_ref.shape[1]
+    lanes = 128
+    depth = dw_ref.shape[0] - 8
+    char_dim = lanes // GROUP
+    grad = gp_ref[...].astype(f32)
+    at = at_ref[...]
+    groups = -(-char_len // GROUP)
+    dw_ref[...] = jnp.zeros_like(dw_ref)
+    for group in range(groups):
+        count = spread_groups(char_len, filters, grad, at, spread_ref, group)
+        piece = tn(x_ref[:, group * lanes : (group + 2) * lanes], spread_ref[:, : count * filters])
+        for place in range(count):
+            dw_ref[:depth, :] += piece[
+                place * char_dim : place * char_dim + depth,
+                place * filters : (place + 1) * filters,
+            ]
+    total = jnp.sum(grad.reshape(-1, 8, filters), axis=0)
+    dw_ref[depth:, :] = jnp.broadcast_to(jnp.sum(total, axis=0, keepdims=True), (8, filters))
+
+
+def table_grad_body(char_len, d_ref, ids_ref, chars_ref, out_ref):
+    words = ids_ref.shape[1]
+    lanes = 128
+    width = lanes // GROUP
+    rows = out_ref.shape[0] * GROUP
+    groups = -(-char_len // GROUP)
+    entry = lax.broadcasted_iota(jnp.int32, (rows, words), 0)
+    lane = lax.broadcasted_iota(jnp.int32, (rows, lanes), 1) // width
+    stacked = jnp.concatenate(
+        [chars_ref[:, group * lanes : (group + 1) * lanes] for group in range(groups)], axis=0
+    ).astype(bf16)
+    total = jnp.zeros((rows, lanes), f32)
+    for place in range(GROUP):
+        pieces = []
+        for group in range(groups):
+            at = GROUP * group + place
+            if at < char_len:
+                pieces.append(jnp.where(ids_ref[at : at + 1, :] == entry, 1.0, 0.0).astype(bf16))
+            else:
+                pieces.append(jnp.zeros((rows, words), bf16))
+        found = nn(jnp.concatenate(pieces, axis=1), stacked)
+        total = total + jnp.where(lane == place, found, 0.0)
+    step = width
+    while step < lanes:
+        total = total + pltpu.roll(total, step, 1)
+        step *= 2
+    part = out_ref.shape[0]
+    fold = jnp.zeros(out_ref.shape, f32)
+    lane = lax.broadcasted_iota(jnp.int32, out_ref.shape, 1) // width
+    for place in range(GROUP):
+        fold = fold + jnp.where(lane == place, total[place * part : (place + 1) * part], 0.0)
+    out_ref[...] = fold
+
+
+def pack_highway_body(carry_ref, gate_ref, out_ref):
+    out_ref[0, :, 0] = carry_ref[...]
+    out_ref[0, :, 1] = gate_ref[...]
+
+
+def pack_highway(weights):
+    layers, rows, columns = weights.shape
+    own = columns // (2 * PLANE)
+    block = (layers, rows, own)
+    return pl.pallas_call(
+        pack_highway_body,
+        grid=(PLANE,),
+        out_shape=jax.ShapeDtypeStruct((PLANE, layers, 2, rows, own), bf16),
+        in_specs=[
+            pl.BlockSpec(block, lambda j: (0, 0, j)),
+            pl.BlockSpec(block, lambda j: (0, 0, PLANE + j)),
+        ],
+        out_specs=pl.BlockSpec((1, layers, 2, rows, own), lambda j: (j, 0, 0, 0, 0)),
+        name="pack_highway",
+    )(weights, weights)
+
+
+def pack_encoder_body(qkv_ref, out_ref, inner_ref, outer_ref, small_ref, packed_ref):
+    dim = packed_ref.shape[1]
+    at = 0
+    for ref in (qkv_ref, out_ref, inner_ref, outer_ref, small_ref):
+        rows = ref.shape[0]
+        for start in range(0, ref.shape[1], dim):
+            packed_ref[at : at + rows, :] = ref[:, start : start + dim]
+            at += rows
+
+
+def finish_highway_body(flag_ref, whole_ref, third_ref, *refs):
+    mid = flag_ref[0] == 1
+    refs[-1][0] = jnp.where(mid, whole_ref[0].astype(f32), third_ref[0].astype(f32))
+
+
+def finish_highway(layer, layers, flag, total, third, previous):
+    own = total.shape[2] // 2
+    block = pl.BlockSpec((1, own, own), lambda half, j: (j, 0, half))
+    shape = jax.ShapeDtypeStruct((layers, own, 2 * PLANE * own), f32)
+    operands = [flag, total, third]
+    specs = [SMEM_SPEC, block, block]
+    aliases = {}
+    if previous is not None:
+        operands.append(previous)
+        specs.append(pl.BlockSpec(memory_space=pl.ANY))
+        aliases = {3: 0}
+    return pl.pallas_call(
+        finish_highway_body,
+        grid=(2, PLANE),
+        out_shape=shape,
+        in_specs=specs,
+        out_specs=pl.BlockSpec((1, own, own), lambda half, j: (layer, 0, half * PLANE + j)),
+        input_output_aliases=aliases,
+        name=f"finish_highway{layer}",
+    )(*operands)
+
+
+def normalize(value):
+    mean = jnp.mean(value, axis=-1, keepdims=True)
+    centred = value - mean
+    spread = jnp.mean(centred * centred, axis=-1, keepdims=True)
+    scale = lax.rsqrt(spread + eps_norm)
+    return centred * scale, scale
+
+
+def normalize_back(grad, normal, scale, gain):
+    moved = grad * gain
+    return (
+        moved
+        - jnp.mean(moved, axis=-1, keepdims=True)
+        - normal * jnp.mean(moved * normal, axis=-1, keepdims=True)
+    ) * scale
+
+
+def over_words(value):
+    return jnp.sum(value, axis=0, keepdims=True)
+
+
+def encoder_body(
+    head_count,
+    in_parts,
+    flag_ref,
+    emb_ref,
+    e1_ref,
+    e2_ref,
+    e3_ref,
+    small_ref,
+    qseg_ref,
+    kseg_ref,
+    kpad_ref,
+    cot_ref,
+    w_hbm,
+    result_ref,
+    d_own_ref,
+    d_send_ref,
+    embs_ref,
+    gq_ref,
+    gk_ref,
+    gv_ref,
+    att_ref,
+    gattn_ref,
+    first_ref,
+    act_ref,
+    gup_ref,
+    gdown_ref,
+    stats_ref,
+    w_ref,
+    q_ref,
+    k_ref,
+    v_ref,
+    p_ref,
+    up_ref,
+    gatt_ref,
+    sems,
+):
+    words, dim = emb_ref.shape
+    part = dim // PLANE
+    wide = act_ref.shape[1] // PLANE
+    cuts = [0, 3 * part, 4 * part, (4 + in_parts) * part, (4 + in_parts) * part + wide]
+    copies = [
+        pltpu.make_async_copy(
+            w_hbm.at[:, low:high, :], w_ref.at[:, low:high, :], sems.at[i]
+        )
+        for i, (low, high) in enumerate(zip(cuts, cuts[1:]))
+    ]
+    for copy in copies:
+        copy.start()
+    pair = 2 * HDIM
+    scale = HDIM ** (-0.5)
+
+    def square(i):
+        return w_ref[:, i * part : (i + 1) * part, :].reshape(dim, dim)
+
+    def small(i):
+        return small_ref[i : i + 1, :]
+
+    emb = emb_ref[...]
+    emb_b = emb.astype(bf16)
+    embs_ref[:words] = emb_b
+    for i, ref in enumerate((e1_ref, e2_ref, e3_ref)):
+        embs_ref[(i + 1) * words : (i + 2) * words] = ref[...]
+    copies[0].wait()
+    q_ref[...] = (nn(emb_b, square(0)) + small(1)).astype(bf16)
+    k_ref[...] = nn(embs_ref[...], square(1)).astype(bf16)
+    v_ref[...] = (nn(embs_ref[...], square(2)) + small(2)).astype(bf16)
+    keys = k_ref.shape[0]
+    row = lax.broadcasted_iota(jnp.int32, (words, keys), 0)
+    column = lax.broadcasted_iota(jnp.int32, (words, keys), 1)
+    allowed = (qseg_ref[...] == kseg_ref[...]) & ((kpad_ref[...] == 0) | (row == column))
+    low_lane = lax.broadcasted_iota(jnp.int32, (1, pair), 1) < HDIM
+
+    def of_head(value, side):
+        keep = low_lane if side == 0 else jnp.logical_not(low_lane)
+        return jnp.where(keep, value.astype(f32), 0.0).astype(bf16)
+
+    for at in range(head_count // 2):
+        cols = slice(at * pair, (at + 1) * pair)
+        outs = []
+        for side in range(2):
+            scores = nt(of_head(q_ref[:, cols], side), k_ref[:, cols]) * scale
+            scores = jnp.where(allowed, scores, masked_score)
+            top = jnp.max(scores, axis=-1, keepdims=True)
+            raised = jnp.exp(scores - top)
+            probs = raised / jnp.sum(raised, axis=-1, keepdims=True)
+            p_ref[2 * at + side] = probs
+            outs.append(nn(probs.astype(bf16), v_ref[:, cols]))
+        att_ref[:, cols] = jnp.where(low_lane, outs[0], outs[1]).astype(bf16)
+    copies[1].wait()
+    attn_out = nn(att_ref[...], square(3)) + small(3)
+    normal1, scale1 = normalize(emb + attn_out)
+    first = normal1 * small(6) + small(9)
+    first_b = first.astype(bf16)
+    first_ref[...] = first_b
+    copies[2].wait()
+    half_root = math.sqrt(0.5)
+    for i in range(in_parts):
+        cols = slice(i * dim, (i + 1) * dim)
+        up = nn(first_b, square(4 + i)) + small(11 + i)
+        up_ref[:, cols] = up
+        act_ref[:, cols] = (0.5 * up * (1.0 + lax.erf(up * half_root))).astype(bf16)
+    copies[3].wait()
+    low = cuts[3]
+    outer = w_ref[:, low : low + wide, :].reshape(PLANE * wide, dim)
+    second = first + (nn(act_ref[...], outer) + small(4))
+    normal2, scale2 = normalize(second)
+    result_ref[...] = (normal2 * small(7) + small(10)).astype(bf16)
+
+    grad = cot_ref[...].astype(f32)
+    d_second = normalize_back(grad, normal2, scale2, small(7))
+    stats_ref[...] = jnp.zeros_like(stats_ref)
+    stats_ref[7:8] = over_words(grad * normal2)
+    stats_ref[10:11] = over_words(grad)
+    gdown = d_second.astype(bf16)
+    gdown_ref[...] = gdown
+    stats_ref[4:5] = over_words(gdown.astype(f32))
+    d_first = d_second
+    density = 1.0 / math.sqrt(2.0 * math.pi)
+    per = dim // wide
+    for i in range(in_parts):
+        cols = slice(i * dim, (i + 1) * dim)
+        block = w_ref[i * per : (i + 1) * per, low : low + wide, :].reshape(dim, dim)
+        up = up_ref[:, cols]
+        slope = 0.5 * (1.0 + lax.erf(up * half_root)) + up * (
+            density * jnp.exp(-0.5 * up * up)
+        )
+        gup = (nt(gdown, block) * slope).astype(bf16)
+        gup_ref[:, cols] = gup
+        stats_ref[11 + i : 12 + i] = over_words(gup.astype(f32))
+        d_first = d_first + nt(gup, square(4 + i))
+    stats_ref[6:7] = over_words(d_first * normal1)
+    stats_ref[9:10] = over_words(d_first)
+    d_res = normalize_back(d_first, normal1, scale1, small(6))
+    gattn = d_res.astype(bf16)
+    gattn_ref[...] = gattn
+    stats_ref[3:4] = over_words(gattn.astype(f32))
+    gatt_ref[...] = nt(gattn, square(3)).astype(bf16)
+    for at in range(head_count // 2):
+        cols = slice(at * pair, (at + 1) * pair)
+        dq, dk, dv = [], None, None
+        for side in range(2):
+            gatt = of_head(gatt_ref[:, cols], side)
+            probs = p_ref[2 * at + side]
+            d_probs = nt(gatt, v_ref[:, cols])
+            inner = jnp.sum(probs * d_probs, axis=-1, keepdims=True)
+            gscore = (probs * (d_probs - inner)).astype(bf16)
+            dq.append(nn(gscore, k_ref[:, cols]))
+            more_k = tn(gscore, of_head(q_ref[:, cols], side))
+            more_v = tn(probs.astype(bf16), gatt)
+            dk = more_k if dk is None else dk + more_k
+            dv = more_v if dv is None else dv + more_v
+        gq_ref[:, cols] = (jnp.where(low_lane, dq[0], dq[1]) * scale).astype(bf16)
+        gk_ref[:, cols] = (dk * scale).astype(bf16)
+        gv_ref[:, cols] = dv.astype(bf16)
+    stats_ref[1:2] = over_words(gq_ref[...].astype(f32))
+    stats_ref[2:3] = over_words(gv_ref[...].astype(f32))
+    for i in range(DEPTH):
+        rows = slice(i * words, (i + 1) * words)
+        piece = nt(gk_ref[rows, :], square(1)) + nt(gv_ref[rows, :], square(2))
+        if i == 0:
+            d_own_ref[...] = d_res + nt(gq_ref[...], square(0)) + piece
+        else:
+            d_send_ref[i - 1] = piece.astype(bf16)
+
+
+def encoder_grad_body(
+    flag_ref,
+    embs_ref,
+    gq_ref,
+    gk_ref,
+    gv_ref,
+    att_ref,
+    gattn_ref,
+    first_ref,
+    act_ref,
+    gup_ref,
+    gdown_ref,
+    stats_ref,
+    out_hbm,
+    out_ref,
+    sems,
+):
+    words, dim = gq_ref.shape
+    part = dim // PLANE
+    wide = act_ref.shape[1] // PLANE
+    in_parts = gup_ref.shape[1] // dim
+    pieces = []
+
+    def put(low, high, value):
+        out_ref[:, low:high, :] = value.reshape(PLANE, high - low, dim)
+
+    def send(low, high):
+        copy = pltpu.make_async_copy(
+            out_ref.at[:, low:high, :], out_hbm.at[:, low:high, :], sems.at[len(pieces)]
+        )
+        copy.start()
+        pieces.append(copy)
+
+    low = (4 + in_parts) * part
+    per = dim // wide
+    for i in range(in_parts):
+        cols = slice(i * dim, (i + 1) * dim)
+        out_ref[i * per : (i + 1) * per, low : low + wide, :] = (
+            tn(act_ref[:, cols], gdown_ref[...]).astype(bf16).reshape(per, wide, dim)
+        )
+    tail = jnp.broadcast_to(stats_ref[...].astype(bf16)[None], (PLANE,) + stats_ref.shape)
+    out_ref[:, low + wide :, :] = tail
+    send(low, out_ref.shape[1])
+    for i in range(in_parts):
+        cols = slice(i * dim, (i + 1) * dim)
+        put((4 + i) * part, (5 + i) * part, tn(first_ref[...], gup_ref[:, cols]).astype(bf16))
+    send(4 * part, low)
+    put(3 * part, 4 * part, tn(att_ref[...], gattn_ref[...]).astype(bf16))
+    put(0, part, tn(embs_ref[:words, :], gq_ref[...]).astype(bf16))
+    put(part, 2 * part, tn(embs_ref[...], gk_ref[...]).astype(bf16))
+    put(2 * part, 3 * part, tn(embs_ref[...], gv_ref[...]).astype(bf16))
+    send(0, 4 * part)
+    for copy in pieces:
+        copy.wait()
+
+
+def encoder(flag, embedded, others, small, query_segs, key_segs, key_pads, cotangent, weights):
+    words, dim = embedded.shape
+    keys = DEPTH * words
+    head_count = dim // HDIM
+    part = dim // PLANE
+    in_parts = 4
+    ff_dim = in_parts * dim
+    vmem = pl.BlockSpec(memory_space=pltpu.VMEM)
+    hbm = pl.BlockSpec(memory_space=pl.ANY)
+    shapes = [
+        ((words, dim), bf16),
+        ((words, dim), f32),
+        ((DEPTH - 1, words, dim), bf16),
+        ((keys, dim), bf16),
+        ((words, dim), bf16),
+        ((keys, dim), bf16),
+        ((keys, dim), bf16),
+        ((words, dim), bf16),
+        ((words, dim), bf16),
+        ((words, dim), bf16),
+        ((words, ff_dim), bf16),
+        ((words, ff_dim), bf16),
+        ((words, dim), bf16),
+        ((16, dim), f32),
+    ]
+    outs = pl.pallas_call(
+        functools.partial(encoder_body, head_count, in_parts),
+        out_shape=[jax.ShapeDtypeStruct(s, t) for s, t in shapes],
+        in_specs=[SMEM_SPEC] + [vmem] * 9 + [hbm],
+        out_specs=[vmem] * len(shapes),
+        scratch_shapes=[
+            VMEM(weights.shape, bf16),
+            VMEM((words, dim), bf16),
+            VMEM((keys, dim), bf16),
+            VMEM((keys, dim), bf16),
+            VMEM((head_count, words, keys), f32),
+            VMEM((words, ff_dim), f32),
+            VMEM((words, dim), bf16),
+            pltpu.SemaphoreType.DMA((4,)),
+        ],
+        name="encoder",
+        compiler_params=pltpu.CompilerParams(vmem_limit_bytes=58 * 1024 * 1024),
+    )(flag, embedded, *others, small, query_segs, key_segs, key_pads, cotangent, weights)
+    result, d_own, d_send = outs[:3]
+    rows = (4 + in_parts) * part + ff_dim // PLANE + 16
+    grads = pl.pallas_call(
+        encoder_grad_body,
+        out_shape=jax.ShapeDtypeStruct((PLANE, rows, dim), bf16),
+        in_specs=[SMEM_SPEC] + [vmem] * 11,
+        out_specs=hbm,
+        scratch_shapes=[VMEM((PLANE, rows, dim), bf16), pltpu.SemaphoreType.DMA((3,))],
+        name="encoder_grad",
+        compiler_params=pltpu.CompilerParams(vmem_limit_bytes=58 * 1024 * 1024),
+    )(flag, *outs[3:])
+    return result, d_own, d_send, grads
+
+
+def round_up(value, multiple):
+    return -(-value // multiple) * multiple
+
+
+def plane_shards(
+    char_ids,
+    segment_ids,
+    pad_mask,
+    cotangent,
+    char_table,
+    conv_weight,
+    conv_bias,
+    hw_weight,
+    hw_bias,
+    proj_weight,
+    pos_table,
+    qkv_weight,
+    out_weight,
+    ff_in_weight,
+    ff_out_weight,
+    ff_in_bias,
+    d_biases,
+    norm_gain,
+    norm_shift,
+):
+    d = lax.axis_index("dp")
+    z = lax.axis_index("seq")
+    dvec = d.astype(jnp.int32)[None]
+    words, char_len = char_ids.shape[1:]
+    all_words = PLANE * words
+    tap_count, char_dim, filters = conv_weight.shape
+    chars = char_table.shape[0]
+    own = filters // PLANE
+    depth = hw_weight.shape[0]
+    model_dim = cotangent.shape[2]
+    seq_len = segment_ids.shape[1]
+    head_count = model_dim // HDIM
+    part = model_dim // PLANE
+    ff_dim = ff_out_weight.shape[0] * PLANE
+    lanes = GROUP * char_dim
+    held = round_up(char_len * char_dim, lanes)
+    score_scale = HDIM ** (-0.5)
+
+    ids = char_ids.reshape(words, char_len)
+    table_rows = round_up(chars, 128)
+    table = jnp.pad(jnp.tile(char_table, (1, GROUP)), ((0, table_rows - chars), (0, 0)))
+    extra = jnp.pad(hw_bias, ((0, 16 - depth), (0, held - hw_bias.shape[1])))
+    (own_x,) = call(
+        functools.partial(lookup_body, char_len),
+        [((words + 16, held), bf16)],
+        dvec,
+        (ids, table, extra),
+        name="lookup",
+    )
+    x_blocks = plane_gather(own_x)
+
+    hw_cols = lax.all_to_all(pack_highway(hw_weight), "dp", 0, 0)
+
+    small = jnp.concatenate(
+        [d_biases.reshape(-1), norm_gain.reshape(-1), norm_shift.reshape(-1), ff_in_bias]
+    )
+    small_rows = round_up(small.shape[0], model_dim) // model_dim
+    small = jnp.pad(small, (0, small_rows * model_dim - small.shape[0])).reshape(-1, model_dim)
+    pos_here = lax.dynamic_slice_in_dim(pos_table, z * words, words, 0).reshape(-1, model_dim)
+    pos_rows = pos_here.shape[0]
+    tail_rows = round_up(small_rows + pos_rows, 16)
+    tail = jnp.pad(
+        jnp.concatenate([small, pos_here], axis=0), ((0, tail_rows - small_rows - pos_rows), (0, 0))
+    )
+    in_parts = ff_in_weight.shape[1] // model_dim
+    weight_rows = (4 + in_parts) * part + ff_dim // PLANE
+    packed = pl.pallas_call(
+        pack_encoder_body,
+        out_shape=jax.ShapeDtypeStruct((weight_rows + tail_rows, model_dim), bf16),
+        name="pack_encoder",
+    )(qkv_weight, out_weight, ff_in_weight, ff_out_weight, tail)
+    gathered = lax.all_gather(packed, "dp", axis=0, tiled=False)
+    at = weight_rows
+    small = gathered[:, at : at + small_rows].reshape(PLANE, -1)
+    at += small_rows
+    pos_full = (
+        gathered[:, at : at + pos_rows]
+        .reshape(PLANE, words, part)
+        .transpose(1, 0, 2)
+        .reshape(words, model_dim)
+    )
+
+    def rows_of(start, count):
+        piece = small[:, start : start + count * part].reshape(PLANE, count, part)
+        return piece.transpose(1, 0, 2).reshape(count, model_dim).astype(f32)
+
+    inner_bias = small[:, 11 * part : 11 * part + ff_dim // PLANE].reshape(in_parts, model_dim)
+    small_full = jnp.concatenate(
+        [
+            rows_of(0, 5),
+            rows_of(5 * part, 3),
+            rows_of(8 * part, 3),
+            inner_bias.astype(f32),
+            jnp.zeros((16 - 11 - in_parts, model_dim), f32),
+        ],
+        axis=0,
+    )
+
+    widths = filter_widths(filters)
+    tap_mask = jnp.asarray(np.arange(tap_count)[:, None] < widths[None, :])
+    masked_kernel = jnp.where(tap_mask[:, None, :], conv_weight, 0).reshape(
+        tap_count * char_dim, filters
+    )
+    own_kernel = lax.dynamic_slice_in_dim(masked_kernel, d * own, own, 1)
+    last_place = jnp.asarray((char_len - widths)[None, :], jnp.int32)
+    own_last = lax.dynamic_slice_in_dim(last_place, d * own, own, 1)
+    own_bias = lax.dynamic_slice_in_dim(conv_bias.astype(f32)[None, :], d * own, own, 1)
+    taps_shape = VMEM((2 * lanes, GROUP * own), bf16)
+    hidden0, hidden0_b, top_at, x_all, bias_a, bias_b = call(
+        functools.partial(conv_body, char_len, char_len - tap_count + 1, words),
+        [
+            ((all_words, own), f32),
+            ((all_words, own), bf16),
+            ((all_words, own), jnp.int32),
+            ((all_words, held + lanes), bf16),
+            ((16, own), f32),
+            ((16, own), f32),
+        ],
+        dvec,
+        (*x_blocks, own_kernel, own_last, own_bias),
+        [taps_shape, VMEM((PLANE, 16, 2 * own), f32)],
+        name="conv",
+    )
+
+    hidden, hidden_b = hidden0, hidden0_b
+    saved = []
+    for layer in range(depth):
+        blocks = plane_gather(hidden_b)
+        opened, ra, following, following_b = highway(
+            layer, dvec, blocks, hw_cols, bias_a, bias_b, hidden
+        )
+        saved.append((blocks, opened, ra, hidden))
+        hidden, hidden_b = following, following_b
+    half = PLANE // 2
+    keep, send = call(
+        project_body,
+        [((half, words, model_dim), f32), ((half, words, model_dim), bf16)],
+        dvec,
+        (hidden_b, proj_weight),
+        name="project",
+    )
+    projected = plane_reduce(keep, send) + small_full[0]
+
+    summed = projected + pos_full.astype(f32)
+    normal0, scale0 = normalize(summed)
+    embedded = normal0 * small_full[5] + small_full[8]
+    embedded_b = embedded.astype(bf16)
+    others = [swap(embedded_b, "seq", DEPTH, offset) for offset in range(1, DEPTH)]
+
+    def by_offset(row):
+        pieces = row.reshape(DEPTH, words)
+        return jnp.concatenate(
+            [lax.dynamic_index_in_dim(pieces, z ^ offset, 0) for offset in range(DEPTH)], axis=1
+        )
+
+    key_segs, key_pads = by_offset(segment_ids), by_offset(pad_mask)
+    result, d_own, d_send, enc_grads = encoder(
+        dvec,
+        embedded,
+        others,
+        small_full,
+        key_segs[0, :words, None],
+        key_segs,
+        key_pads,
+        cotangent.reshape(words, model_dim),
+        gathered,
+    )
+    d_embedded = d_own
+    for offset in range(1, DEPTH):
+        d_embedded = d_embedded + swap(d_send[offset - 1], "seq", DEPTH, offset).astype(f32)
+    enc_slice = lax.psum_scatter(enc_grads, "dp", scatter_dimension=0, tiled=True)[0]
+    d_summed = normalize_back(d_embedded, normal0, scale0, small_full[5])
+    grad_proj = jnp.concatenate(
+        [
+            d_summed.astype(bf16),
+            over_words(d_embedded * normal0).astype(bf16),
+            over_words(d_embedded).astype(bf16),
+            jnp.zeros((14, model_dim), bf16),
+        ],
+        axis=0,
+    )
+
+    gp_blocks = plane_gather(grad_proj)
+    d_hidden, proj_grad, top_sums = call(
+        functools.partial(unproject_body, words),
+        [((all_words, own), f32), ((own, model_dim), bf16), ((words + 32, model_dim), f32)],
+        dvec,
+        (*gp_blocks, proj_weight, hidden_b),
+        name="unproject",
+    )
+    hw_slices = [None] * depth
+    for layer in reversed(range(depth)):
+        blocks, opened, ra, hidden = saved[layer]
+        ga, gb, d_carry, sums, keep, send = highway_back(
+            layer, dvec, d_hidden, opened, ra, hidden, hw_cols
+        )
+        d_hidden = d_carry + plane_reduce(keep, send)
+        (cols_grad,) = call(
+            highway_grad_body,
+            [((PLANE, own + 16, 2 * own), bf16)],
+            dvec,
+            (*blocks, ga, gb, sums),
+            name=f"highway_grad{layer}",
+        )
+        hw_slices[layer] = lax.all_to_all(cols_grad, "dp", 0, 0)
+
+    grad_pooled, keep, send = call(
+        functools.partial(char_back_body, char_len, words),
+        [
+            ((all_words, own), bf16),
+            ((half, words, held), f32),
+            ((half, words, held), bf16),
+        ],
+        dvec,
+        (hidden0, top_at, d_hidden, own_kernel),
+        [
+            taps_shape,
+            VMEM((2 * words, GROUP * own), bf16),
+            VMEM((all_words, held + lanes), f32),
+        ],
+        name="char_back",
+    )
+    char_grads = plane_reduce(keep, send)
+    (conv_part,) = call(
+        functools.partial(conv_grad_body, char_len),
+        [((tap_count * char_dim + 8, own), f32)],
+        dvec,
+        (x_all, top_at, grad_pooled),
+        [VMEM((all_words, GROUP * own), bf16), VMEM((2 * lanes, all_words), bf16)],
+        name="conv_grad",
+    )
+    fold_rows = round_up(-(-chars // GROUP), 8)
+    (table_part,) = call(
+        functools.partial(table_grad_body, char_len),
+        [((fold_rows, lanes), f32)],
+        dvec,
+        (ids.T, char_grads),
+        name="table_grad",
+    )
+    ends = jnp.concatenate(
+        [conv_part, jnp.pad(table_part, ((0, 0), (0, own - lanes)))], axis=0
+    )
+    ends = ends + swap(ends, "seq", DEPTH, 1)
+    ends = ends + swap(ends, "seq", DEPTH, 2)
+    end_blocks = jnp.stack(plane_gather(ends))
+    ordered = [lax.dynamic_index_in_dim(end_blocks, d ^ j, 0, False) for j in range(PLANE)]
+    conv_rows = tap_count * char_dim
+    conv_total = jnp.concatenate([piece[:conv_rows] for piece in ordered], axis=1)
+    conv_total = jnp.where(
+        tap_mask[:, None, :], conv_total.reshape(tap_count, char_dim, filters), 0.0
+    )
+    conv_bias_total = jnp.concatenate([piece[conv_rows] for piece in ordered])
+    table_total = sum(piece[conv_rows + 8 :, :lanes] for piece in ordered)
+    table_total = (
+        table_total.reshape(fold_rows, GROUP, char_dim)
+        .transpose(1, 0, 2)
+        .reshape(GROUP * fold_rows, char_dim)[:chars]
+    )
+
+    top_own = lax.dynamic_slice_in_dim(top_sums, d * part, part, 1).astype(bf16)
+    top_own = jnp.pad(top_own, ((0, 0), (0, 128 - part)))
+    top_all = lax.dynamic_update_slice_in_dim(
+        jnp.zeros((seq_len, 128), bf16), top_own[:words], z * words, 0
+    )
+    top_total = line_sum(jnp.concatenate([top_all, top_own[words:]], axis=0))[:, :part].astype(f32)
+    pos_total = top_total[:seq_len]
+    gain0, shift0, bias0 = top_total[seq_len], top_total[seq_len + 1], top_total[seq_len + 16]
+    proj_total = line_sum(proj_grad).astype(f32)
+    enc_total = line_sum(enc_slice).astype(f32)
+    qkv_total = jnp.concatenate([enc_total[i * part : (i + 1) * part] for i in range(3)], axis=1)
+    out_total = enc_total[3 * part : 4 * part]
+    at = 4 * part
+    inner_total = jnp.concatenate(
+        [enc_total[at + i * part : at + (i + 1) * part] for i in range(in_parts)], axis=1
+    )
+    at += in_parts * part
+    outer_total = enc_total[at : at + ff_dim // PLANE]
+    small_total = enc_total[weight_rows:]
+    own_small = lax.dynamic_slice_in_dim(small_total, d * part, part, 1)
+    bias_total = jnp.concatenate([bias0[None], own_small[1:5]], axis=0)
+    gain_total = jnp.concatenate([gain0[None], own_small[6:8]], axis=0)
+    shift_total = jnp.concatenate([shift0[None], own_small[9:11]], axis=0)
+    inner_bias_total = lax.dynamic_slice_in_dim(
+        small_total[11 : 11 + in_parts].reshape(-1), d * (ff_dim // PLANE), ff_dim // PLANE, 0
+    )
+
+    flag = ((z == 1) | (z == 2)).astype(jnp.int32)[None]
+    hw_total, hw_bias_totals = None, [None] * depth
+    for layer in reversed(range(depth)):
+        whole_sum, third = line_total(hw_slices[layer])
+        hw_total = finish_highway(layer, depth, flag, whole_sum, third, hw_total)
+        row = jnp.where(flag[0] == 1, whole_sum[:, own], third[:, own])
+        row = row.reshape(PLANE, 2, own).transpose(1, 0, 2).reshape(-1)
+        hw_bias_totals[layer] = lax.dynamic_slice_in_dim(row, d * 2 * own, 2 * own, 0).astype(f32)
+
+    output = result.reshape(1, words, model_dim)
+    return (
+        output,
+        table_total,
+        conv_total,
+        conv_bias_total,
+        hw_total,
+        jnp.stack(hw_bias_totals),
+        proj_total,
+        pos_total,
+        qkv_total,
+        out_total,
+        inner_total,
+        outer_total,
+        inner_bias_total,
+        bias_total,
+        gain_total,
+        shift_total,
+    )
+
+
 def solution(mesh):
     placed = (
         P("dp", "seq", None),
@@ -418,8 +1504,10 @@
         P(None, "dp"),
         P(None, "dp"),
     )
+    plane, depth = mesh.shape["dp"], mesh.shape["seq"]
+    step = plane_shards if (plane, depth) == (PLANE, DEPTH) else shards
     return jax.shard_map(
-        shards,
+        step,
         mesh=mesh,
         in_specs=placed,
         out_specs=(

time: 1740 us -> 780 us (0.45)
  waiting for transfers between devices: 820 us -> 390 us
  local copies, waits for them, and re-layouts: 308 us -> 24.9 us
  matrix products: 212 us -> 0 us
  blocking collectives: 179 us -> 0 us
  Pallas kernels: 0 us -> 154 us
  other arithmetic: 196 us -> 57.1 us
  starting transfers between devices: 0.85 us -> 131 us
    reduce_scatter x7 -> x1, waiting for transfers between devices: 617 us -> 0.01 us  [plane_shards(): lax.psum_scatter(enc_grads, 'dp', scatter_dimension=0, tiled=True)[0]]
    ppermute x0 -> x74, waiting for transfers between devices: none -> 372 us  [the longest x59 263 us: swap(): lax.ppermute(value, axis_name, [(at, at ^ offset) for at in range(size)])]
    dot_general x51 -> x0, matrix products: 212 us -> none  [the longest x19 72.1 us: product(): return jnp.dot(left_side, right_side, preferred_element_type=jnp.float32)]
    pallas_call x0 -> x19, Pallas kernels: none -> 154 us  [the longest x9 60.3 us: call(): pl.pallas_call(body, out_shape=[jax.ShapeDtypeStruct(s, t) for s, t in ou...]
    scatter-add x28 -> x0, local copies, waits for them, and re-layouts: 136 us -> none  [embed_backward(): spread.at[:, tap_index:tap_index + char_len].add(d_taps[:, :, tap_index])]
    psum x2 -> x0, waiting for transfers between devices: 118 us -> none  [the longest x1 118 us: shards(): lax.psum((conv_sums[2], conv_weight_grad, conv_sums[1]), ('dp', 'seq'))]
    ppermute x0 -> x74, starting transfers between devices: none -> 117 us  [the longest x59 90.7 us: swap(): lax.ppermute(value, axis_name, [(at, at ^ offset) for at in range(size)])]
    another operation x8 -> x1, other arithmetic: 95.4 us -> 0.6 us  [plane_shards(): jnp.stack(hw_bias_totals)]
  transfers between devices with their start and end apart: 21 -> 79, of which waited for: 10 -> 40; matrix products, arithmetic and copies ran while one was open for 39% -> 8% of each run, Pallas kernels for 0% -> 15%
where the time goes in v1:
time: 780 us; the launch traced here: 773 us
  waiting for transfers between devices  390 us (50%)
  Pallas kernels  154 us (20%)
  starting transfers between devices  131 us (17%)
  other arithmetic  57.1 us (7%)
  local copies, waits for them, and re-layouts  24.9 us (3%)
  between operations  15.4 us (2%)
    ppermute x59, waiting for transfers between devices, swap(): lax.ppermute(value, axis_name, [(at, at ^ offset) for at in range(size)])  263 us
    ppermute x5, waiting for transfers between devices, line_total(): return (whole, lax.ppermute(whole, 'seq', [(1, 0), (2, 3)]))  95.7 us
    ppermute x59, starting transfers between devices, swap(): lax.ppermute(value, axis_name, [(at, at ^ offset) for at in range(size)])  90.7 us
    pallas_call x9, Pallas kernels, call(): pl.pallas_call(body, out_shape=[jax.ShapeDtypeStruct(s, t) for s, t in ou...  60.3 us
    pallas_call x1, Pallas kernels, encoder(): pl.pallas_call(functools.partial(encoder_body, head_count, in_parts), out...  24.1 us
    pallas_call x2, Pallas kernels, finish_highway(): pl.pallas_call(finish_highway_body, grid=(2, PLANE), out_shape=shape, in_...  20.7 us
    all_to_all x2, waiting for transfers between devices, plane_shards(): hw_slices[layer] = lax.all_to_all(cols_grad, 'dp', 0, 0)  18.4 us
    pallas_call x2, Pallas kernels, highway_back(): pl.pallas_call(highway_back_body, grid=(4,), out_shape=[jax.ShapeDtypeStr...  16.2 us
  transfers between devices with their start and end apart: 79, of which 40 were waited for; matrix products, arithmetic and copies ran while one was open for 8% of the time, Pallas kernels for 15%

profile of v1, /device:TPU:0, one launch (start us, length us, event | category | flops | bytes accessed | tf_op | source)
XLA Modules:
  0.0 772.6 jit_solution(7851532528230846427)
XLA Ops:
  36.4 64.8 %collective-permute-done.1.refs_2_ = bf16[144,896]{1,0:T(8,128)(2,1)S(1)} collective-permute-done((bf16[144,896]{1,0:T(8,128)(2,1)}, bf16[144,896]{1,0:T(8,128)(2,1)S(1)}, u32[]{:S(2)}, u32[]{:S(2)}) %collective-permute-start.1) | collective-permute-done | bytes 258080 | tf_op jit(solution)/shard_map/ppermute | solution.py:412
  102.1 10.8 %collective-permute-done.5.refs_6_ = bf16[144,896]{1,0:T(8,128)(2,1)S(1)} collective-permute-done((bf16[144,896]{1,0:T(8,128)(2,1)}, bf16[144,896]{1,0:T(8,128)(2,1)S(1)}, u32[]{:S(2)}, u32[]{:S(2)}) %collective-permute-start.5) | collective-permute-done | bytes 258080 | tf_op jit(solution)/shard_map/ppermute | solution.py:412
  117.0 12.1 %conv.1 = (f32[1024,256]{1,0:T(8,128)}, bf16[1024,256]{1,0:T(8,128)(2,1)}, s32[1024,256]{1,0:T(8,128)}, bf16[1024,1024]{1,0:T(8,128)(2,1)}, f32[16,256]{1,0:T(8,128)}, /*index=5*/f32[16,256]{1,0:T(8,128)}) custom-call(s32[1]{0:T(128)} %bitcast.d_ref.flag_ref, bf16[144,896]{1,0:T(8,128)(2,1)} %lookup.1.refs_0_, bf16[144,896]{1,0:T(8,128)(2,1)} %copy-done.31, ...), custom_call_target="tpu_custom_call" | custom-call | tf_op jit(solution)/shard_map/conv/pallas_call | solution.py:476
  132.6 33.8 %collective-permute-done.10.refs_4_ = bf16[1024,256]{1,0:T(8,128)(2,1)S(1)} collective-permute-done((bf16[1024,256]{1,0:T(8,128)(2,1)}, bf16[1024,256]{1,0:T(8,128)(2,1)S(1)}, u32[]{:S(2)}, u32[]{:S(2)}) %collective-permute-start.10) | collective-permute-done | bytes 524320 | tf_op jit(solution)/shard_map/ppermute | solution.py:412
  182.0 11.5 %collective-permute-done.15.refs_2_ = bf16[1024,256]{1,0:T(8,128)(2,1)S(1)} collective-permute-done((bf16[1024,256]{1,0:T(8,128)(2,1)}, bf16[1024,256]{1,0:T(8,128)(2,1)S(1)}, u32[]{:S(2)}, u32[]{:S(2)}) %collective-permute-start.15) | collective-permute-done | bytes 524320 | tf_op jit(solution)/shard_map/ppermute | solution.py:412
  194.0 10.0 %collective-permute-done.19.refs_6_ = bf16[1024,256]{1,0:T(8,128)(2,1)S(1)} collective-permute-done((bf16[1024,256]{1,0:T(8,128)(2,1)}, bf16[1024,256]{1,0:T(8,128)(2,1)S(1)}, u32[]{:S(2)}, u32[]{:S(2)}) %collective-permute-start.19) | collective-permute-done | bytes 524320 | tf_op jit(solution)/shard_map/ppermute | solution.py:412
  245.8 9.8 %collective-permute-done.26.e2_ref = bf16[128,768]{1,0:T(8,128)(2,1)S(1)} collective-permute-done((bf16[128,768]{1,0:T(8,128)(2,1)S(1)}, bf16[128,768]{1,0:T(8,128)(2,1)S(1)}, u32[]{:S(2)}, u32[]{:S(2)}) %collective-permute-start.26) | collective-permute-done | bytes 196640 | tf_op jit(solution)/shard_map/ppermute | solution.py:412
  256.3 24.1 %encoder.1 = (bf16[128,768]{1,0:T(8,128)(2,1)}, f32[128,768]{1,0:T(8,128)}, bf16[3,128,768]{2,1,0:T(8,128)(2,1)}, bf16[512,768]{1,0:T(8,128)(2,1)}, bf16[128,768...) custom-call(s32[1]{0:T(128)} %bitcast.d_ref.flag_ref, ...), custom_call_target="tpu_custom_call" | custom-call | tf_op jit(solution)/shard_map/encoder/pallas_call | solution.py:1132
  280.4 9.1 %encoder_grad.1 = bf16[8,1168,768]{2,1,0:T(8,128)(2,1)} custom-call(s32[1]{0:T(128)} %bitcast.d_ref.flag_ref, bf16[512,768]{1,0:T(8,128)(2,1)} %get-tuple-element.99.embs_ref, bf16[128,768]{1,0:T(8,128)(2,1)} %get-tuple-element.100.gq_ref, bf16[512,768]{1,0:T(8,128)(2,1)} %get-tuple-element.101.gk_ref, bf16[512,768]{1,0:T(8,128)(2,1)} %get-tuple-element.102.gv_ref, ...), custom_call_target="tpu_custom_call" | custom-call | tf_op jit(solution)/shard_map/encoder_grad/pallas_call | solution.py:1152
  298.7 10.3 %collective-permute-done.29 = bf16[128,768]{1,0:T(8,128)(2,1)S(1)} collective-permute-done((bf16[128,768]{1,0:T(8,128)(2,1)S(1)}, bf16[128,768]{1,0:T(8,128)(2,1)S(1)}, u32[]{:S(2)}, u32[]{:S(2)}) %collective-permute-start.29) | collective-permute-done | bytes 196640 | tf_op jit(solution)/shard_map/ppermute | solution.py:412
  356.4 12.8 %collective-permute-done.39 = bf16[1024,256]{1,0:T(8,128)(2,1)} collective-permute-done((bf16[1024,256]{1,0:T(8,128)(2,1)}, bf16[1024,256]{1,0:T(8,128)(2,1)}, u32[]{:S(2)}, u32[]{:S(2)}) %collective-permute-start.39) | collective-permute-done | bytes 524320 | tf_op jit(solution)/shard_map/ppermute | solution.py:412
  371.2 13.7 %collective-permute-done.41 = bf16[1024,256]{1,0:T(8,128)(2,1)} collective-permute-done((bf16[1024,256]{1,0:T(8,128)(2,1)}, bf16[1024,256]{1,0:T(8,128)(2,1)}, u32[]{:S(2)}, u32[]{:S(2)}) %collective-permute-start.41) | collective-permute-done | bytes 524320 | tf_op jit(solution)/shard_map/ppermute | solution.py:412
  396.0 18.3 %all-to-all-done.2 = bf16[8,272,512]{2,1,0:T(8,128)(2,1)S(1)} async-done(((bf16[8,272,512]{2,1,0:T(8,128)(2,1)}), bf16[8,272,512]{2,1,0:T(8,128)(2,1)S(1)}, u32[]{:S(2)}, u32[]{:S(2)}) %all-to-all-start.2) | async-done | bytes 2228256 | tf_op jit(solution)/shard_map/all_to_all | solution.py:1373
  436.2 32.4 %collective-permute-done.43 = bf16[1024,256]{1,0:T(8,128)(2,1)S(1)} collective-permute-done((bf16[1024,256]{1,0:T(8,128)(2,1)S(1)}, bf16[1024,256]{1,0:T(8,128)(2,1)S(1)}, u32[]{:S(2)}, u32[]{:S(2)}) %collective-permute-start.43) | collective-permute-done | bytes 524320 | tf_op jit(solution)/shard_map/ppermute | solution.py:412
  468.6 11.7 %collective-permute-done.45 = bf16[1024,256]{1,0:T(8,128)(2,1)S(1)} collective-permute-done((bf16[1024,256]{1,0:T(8,128)(2,1)S(1)}, bf16[1024,256]{1,0:T(8,128)(2,1)S(1)}, u32[]{:S(2)}, u32[]{:S(2)}) %collective-permute-start.45) | collective-permute-done | bytes 524320 | tf_op jit(solution)/shard_map/ppermute | solution.py:412
  483.1 11.7 %char_back.1 = (bf16[1024,256]{1,0:T(8,128)(2,1)}, f32[4,128,896]{2,1,0:T(8,128)}, bf16[4,128,896]{2,1,0:T(8,128)(2,1)}) custom-call(s32[1]{0:T(128)} %bitcast.d_ref.flag_ref, f32[1024,256]{1,0:T(8,128)} %get-tuple-element.66.refs_11_.h_ref, s32[1024,256]{1,0:T(8,128)} %get-tuple-element.74.at_ref, f32[1024,256]{1,0:T(8,128)} %fusion.2.dh_ref, ...), custom_call_target="tpu_custom_call" | custom-call | tf_op jit(solution)/shard_map/char_back/pallas_call | solution.py:476
  519.0 9.7 %conv_grad.1 = f32[120,256]{1,0:T(8,128)} custom-call(s32[1]{0:T(128)} %bitcast.d_ref.flag_ref, bf16[1024,1024]{1,0:T(8,128)(2,1)} %get-tuple-element.73.x_ref, s32[1024,256]{1,0:T(8,128)} %get-tuple-element.74.at_ref, bf16[1024,256]{1,0:T(8,128)(2,1)} %get-tuple-element.88.gp_ref), custom_call_target="tpu_custom_call" | custom-call | tf_op jit(solution)/shard_map/conv_grad/pallas_call | solution.py:476
  538.5 43.4 %collective-permute-start.50 = (f32[160,256]{1,0:T(8,128)}, f32[160,256]{1,0:T(8,128)}, u32[]{:S(2)}, u32[]{:S(2)}) collective-permute-start(f32[160,256]{1,0:T(8,128)} %select_maximum_fusion), channel_id=1, source_target_pairs={{0,1},{1,0},{2,3},{3,2},{4,5},{5,4},{6,7},{7,6},{8,9},{9,8},{10,11... | collective-permute-start | bytes 491528 | tf_op jit(solution)/shard_map/ppermute | solution.py:412
  618.2 12.4 %collective-permute-done.71 = bf16[1168,768]{1,0:T(8,128)(2,1)S(1)} collective-permute-done((bf16[1168,768]{1,0:T(8,128)(2,1)}, bf16[1168,768]{1,0:T(8,128)(2,1)S(1)}, u32[]{:S(2)}, u32[]{:S(2)}) %collective-permute-start.71) | collective-permute-done | bytes 1794080 | tf_op jit(solution)/shard_map/ppermute | solution.py:438
  640.7 14.9 %collective-permute-done.64.third_ref = bf16[8,272,512]{2,1,0:T(8,128)(2,1)} collective-permute-done((bf16[8,272,512]{2,1,0:T(8,128)(2,1)S(1)}, bf16[8,272,512]{2,1,0:T(8,128)(2,1)}, u32[]{:S(2)}, u32[]{:S(2)}) %collective-permute-start.64) | collective-permute-done | bytes 2228256 | tf_op jit(solution)/shard_map/ppermute | solution.py:442
  656.6 10.4 %finish_highway1.1.refs_0_ = f32[2,256,4096]{2,1,0:T(8,128)} custom-call(s32[1]{0:T(128)} %bitcast.69.flag_ref, bf16[8,272,512]{2,1,0:T(8,128)(2,1)} %copy-done.2, bf16[8,272,512]{2,1,0:T(8,128)(2,1)} %collective-permute-done.64.third_ref), custom_call_target="tpu_custom_call" | custom-call | tf_op jit(solution)/shard_map/finish_highway1/pallas_call | solution.py:853
  667.0 57.1 %collective-permute-done.61.third_ref = bf16[8,272,512]{2,1,0:T(8,128)(2,1)} collective-permute-done((bf16[8,272,512]{2,1,0:T(8,128)(2,1)}, bf16[8,272,512]{2,1,0:T(8,128)(2,1)}, u32[]{:S(2)}, u32[]{:S(2)}) %collective-permute-start.61) | collective-permute-done | bytes 2228256 | tf_op jit(solution)/shard_map/ppermute | solution.py:442
  725.2 10.4 %finish_highway0.1 = f32[2,256,4096]{2,1,0:T(8,128)} custom-call(s32[1]{0:T(128)} %bitcast.69.flag_ref, bf16[8,272,512]{2,1,0:T(8,128)(2,1)} %add.360.whole_ref, bf16[8,272,512]{2,1,0:T(8,128)(2,1)} %collective-permute-done.61.third_ref, f32[2,256,4096]{2,1,0:T(8,128)} %finish_highway1.1.refs_0_), custom_call_target="tpu_custom_call", output_to_operand_aliasing={{}: (3, {})} | custom-call | tf_op jit(solution)/shard_map/finish_highway0/pallas_call | solution.py:853
  736.2 21.0 %collective-permute-done.73 = bf16[1168,768]{1,0:T(8,128)(2,1)} collective-permute-done((bf16[1168,768]{1,0:T(8,128)(2,1)}, bf16[1168,768]{1,0:T(8,128)(2,1)}, u32[]{:S(2)}, u32[]{:S(2)}) %collective-permute-start.73) | collective-permute-done | bytes 1794080 | tf_op jit(solution)/shard_map/ppermute | solution.py:442
  (419 shorter events, 280.8 us)
Async XLA Ops:
  7.2 218.0 %all-gather.3.cloned.1.call-start = ((), (), s32[]{:S(2)}) async-start(), calls=%async_computation.5 | async-start | bytes 16367616 | tf_op jit(solution)/shard_map/all_gather | solution.py:1240
  21.5 149.2 %all-to-all-start = ((bf16[8,2,2,256,256]{4,3,2,1,0:T(8,128)(2,1)}), bf16[8,2,2,256,256]{4,3,2,1,0:T(8,128)(2,1)}, u32[]{:S(2)}, u32[]{:S(2)}) async-start(bf16[8,2,2,256,256]{4,3,2,1,0:T(8,128)(2,1)} %pack_highway.1), calls=%async_computation | async-start | bytes 8388608 | tf_op jit(solution)/shard_map/all_to_all | solution.py:1220
  26.8 562.9 %reduce-scatter.2.cloned.1.call-start = ((), (), s32[]{:S(2)}) async-start(), calls=%async_computation.4 | async-start | bytes 16146432 | tf_op jit(solution)/shard_map/reduce_scatter | solution.py:1339
  32.4 68.8 %collective-permute-start.1 = (bf16[144,896]{1,0:T(8,128)(2,1)}, bf16[144,896]{1,0:T(8,128)(2,1)S(1)}, u32[]{:S(2)}, u32[]{:S(2)}) collective-permute-start(bf16[144,896]{1,0:T(8,128)(2,1)} %lookup.1.refs_0_), channel_id=1, source_target_pairs={{0,8},{4,12},{8,0},{12,4},{16,24},{20,28},{24,16},{28,20},{1,9},{5... | collective-permute-start | bytes 774152 | tf_op jit(solution)/shard_map/ppermute | solution.py:412
  34.7 67.3 %collective-permute-start.3 = (bf16[144,896]{1,0:T(8,128)(2,1)}, bf16[144,896]{1,0:T(8,128)(2,1)S(1)}, u32[]{:S(2)}, u32[]{:S(2)}) collective-permute-start(bf16[144,896]{1,0:T(8,128)(2,1)} %lookup.1.refs_0_), channel_id=1, source_target_pairs={{0,16},{4,20},{8,24},{12,28},{16,0},{20,4},{24,8},{28,12},{1,17},{... | collective-permute-start | bytes 774152 | tf_op jit(solution)/shard_map/ppermute | solution.py:412
  36.3 76.6 %collective-permute-start.5 = (bf16[144,896]{1,0:T(8,128)(2,1)}, bf16[144,896]{1,0:T(8,128)(2,1)S(1)}, u32[]{:S(2)}, u32[]{:S(2)}) collective-permute-start(bf16[144,896]{1,0:T(8,128)(2,1)} %lookup.1.refs_0_), channel_id=1, source_target_pairs={{0,24},{4,28},{8,16},{12,20},{16,8},{20,12},{24,0},{28,4},{1,25},{... | collective-permute-start | bytes 774152 | tf_op jit(solution)/shard_map/ppermute | solution.py:412
  36.3 79.8 %collective-permute-start = (bf16[144,896]{1,0:T(8,128)(2,1)}, bf16[144,896]{1,0:T(8,128)(2,1)S(1)}, u32[]{:S(2)}, u32[]{:S(2)}) collective-permute-start(bf16[144,896]{1,0:T(8,128)(2,1)} %lookup.1.refs_0_), channel_id=1, source_target_pairs={{0,4},{4,0},{8,12},{12,8},{16,20},{20,16},{24,28},{28,24},{1,5},{5... | collective-permute-start | bytes 774152 | tf_op jit(solution)/shard_map/ppermute | solution.py:412
  129.1 37.3 %collective-permute-start.10 = (bf16[1024,256]{1,0:T(8,128)(2,1)}, bf16[1024,256]{1,0:T(8,128)(2,1)S(1)}, u32[]{:S(2)}, u32[]{:S(2)}) collective-permute-start(bf16[1024,256]{1,0:T(8,128)(2,1)} %get-tuple-element.63.refs_0_), channel_id=1, source_target_pairs={{0,16},{4,20},{8,24},{12,28},{16,0},{20,4},{24,8},{28,12},{1,17},{... | collective-permute-start | bytes 1572872 | tf_op jit(solution)/shard_map/ppermute | solution.py:412
  129.7 36.8 %collective-permute-start.12 = (bf16[1024,256]{1,0:T(8,128)(2,1)}, bf16[1024,256]{1,0:T(8,128)(2,1)S(1)}, u32[]{:S(2)}, u32[]{:S(2)}) collective-permute-start(bf16[1024,256]{1,0:T(8,128)(2,1)} %get-tuple-element.63.refs_0_), channel_id=1, source_target_pairs={{0,24},{4,28},{8,16},{12,20},{16,8},{20,12},{24,0},{28,4},{1,25},{... | collective-permute-start | bytes 1572872 | tf_op jit(solution)/shard_map/ppermute | solution.py:412
  345.2 39.7 %collective-permute-start.41 = (bf16[1024,256]{1,0:T(8,128)(2,1)}, bf16[1024,256]{1,0:T(8,128)(2,1)}, u32[]{:S(2)}, u32[]{:S(2)}) collective-permute-start(bf16[1024,256]{1,0:T(8,128)(2,1)} %get-tuple-element.173), channel_id=1, source_target_pairs={{0,24},{4,28},{8,16},{12,20},{16,8},{20,12},{24,0},{28,4},{1,25},{... | collective-permute-start | bytes 1572872 | tf_op jit(solution)/shard_map/ppermute | solution.py:412
  352.6 61.7 %all-to-all-start.2 = ((bf16[8,272,512]{2,1,0:T(8,128)(2,1)}), bf16[8,272,512]{2,1,0:T(8,128)(2,1)S(1)}, u32[]{:S(2)}, u32[]{:S(2)}) async-start(bf16[8,272,512]{2,1,0:T(8,128)(2,1)} %highway_grad1.1), calls=%async_computation.2 | async-start | bytes 4456448 | tf_op jit(solution)/shard_map/all_to_all | solution.py:1373
  414.3 85.6 %collective-permute-start.62 = (bf16[8,272,512]{2,1,0:T(8,128)(2,1)S(1)}, bf16[8,272,512]{2,1,0:T(8,128)(2,1)}, u32[]{:S(2)}, u32[]{:S(2)}) collective-permute-start(bf16[8,272,512]{2,1,0:T(8,128)(2,1)S(1)} %all-to-all-done.2), channel_id=1, source_target_pairs={{0,1},{3,2},{4,5},{7,6},{8,9},{11,10},{12,13},{15,14},{16,17},{19,... | collective-permute-start | bytes 6684680 | tf_op jit(solution)/shard_map/ppermute | solution.py:438
  425.4 79.5 %all-to-all-start.1 = ((bf16[8,272,512]{2,1,0:T(8,128)(2,1)}), bf16[8,272,512]{2,1,0:T(8,128)(2,1)}, u32[]{:S(2)}, u32[]{:S(2)}) async-start(bf16[8,272,512]{2,1,0:T(8,128)(2,1)} %highway_grad0.1), calls=%async_computation.1 | async-start | bytes 4456448 | tf_op jit(solution)/shard_map/all_to_all | solution.py:1373
  432.6 36.0 %collective-permute-start.43 = (bf16[1024,256]{1,0:T(8,128)(2,1)S(1)}, bf16[1024,256]{1,0:T(8,128)(2,1)S(1)}, u32[]{:S(2)}, u32[]{:S(2)}) collective-permute-start(bf16[1024,256]{1,0:T(8,128)(2,1)S(1)} %get-tuple-element.169), channel_id=1, source_target_pairs={{0,8},{4,12},{8,0},{12,4},{16,24},{20,28},{24,16},{28,20},{1,9},{5... | collective-permute-start | bytes 1572872 | tf_op jit(solution)/shard_map/ppermute | solution.py:412
  436.1 44.2 %collective-permute-start.45 = (bf16[1024,256]{1,0:T(8,128)(2,1)S(1)}, bf16[1024,256]{1,0:T(8,128)(2,1)S(1)}, u32[]{:S(2)}, u32[]{:S(2)}) collective-permute-start(bf16[1024,256]{1,0:T(8,128)(2,1)S(1)} %get-tuple-element.170), channel_id=1, source_target_pairs={{0,24},{4,28},{8,16},{12,20},{16,8},{20,12},{24,0},{28,4},{1,25},{... | collective-permute-start | bytes 1572872 | tf_op jit(solution)/shard_map/ppermute | solution.py:412
  502.8 99.7 %collective-permute-start.63 = (bf16[8,272,512]{2,1,0:T(8,128)(2,1)S(1)}, bf16[8,272,512]{2,1,0:T(8,128)(2,1)}, u32[]{:S(2)}, u32[]{:S(2)}) collective-permute-start(bf16[8,272,512]{2,1,0:T(8,128)(2,1)S(1)} %add.361), channel_id=1, source_target_pairs={{1,2},{2,1},{5,6},{6,5},{9,10},{10,9},{13,14},{14,13},{17,18},{18,... | collective-permute-start | bytes 6684680 | tf_op jit(solution)/shard_map/ppermute | solution.py:440
  504.9 101.9 %collective-permute-start.59 = (bf16[8,272,512]{2,1,0:T(8,128)(2,1)}, bf16[8,272,512]{2,1,0:T(8,128)(2,1)}, u32[]{:S(2)}, u32[]{:S(2)}) collective-permute-start(bf16[8,272,512]{2,1,0:T(8,128)(2,1)} %all-to-all-done.1), channel_id=1, source_target_pairs={{0,1},{3,2},{4,5},{7,6},{8,9},{11,10},{12,13},{15,14},{16,17},{19,... | collective-permute-start | bytes 6684680 | tf_op jit(solution)/shard_map/ppermute | solution.py:438
  528.7 53.2 %collective-permute-start.70 = (bf16[544,128]{1,0:T(8,128)(2,1)S(1)}, bf16[544,128]{1,0:T(8,128)(2,1)S(1)}, u32[]{:S(2)}, u32[]{:S(2)}) collective-permute-start(bf16[544,128]{1,0:T(8,128)(2,1)S(1)} %add.368), channel_id=1, source_target_pairs={{1,0},{2,3},{5,4},{6,7},{9,8},{10,11},{13,12},{14,15},{17,16},{18,... | collective-permute-start | bytes 417800 | tf_op jit(solution)/shard_map/ppermute | solution.py:442
  530.1 52.6 %collective-permute-start.66 = (bf16[256,768]{1,0:T(8,128)(2,1)S(1)}, bf16[256,768]{1,0:T(8,128)(2,1)}, u32[]{:S(2)}, u32[]{:S(2)}) collective-permute-start(bf16[256,768]{1,0:T(8,128)(2,1)S(1)} %add.364), channel_id=1, source_target_pairs={{1,2},{2,1},{5,6},{6,5},{9,10},{10,9},{13,14},{14,13},{17,18},{18,... | collective-permute-start | bytes 1179656 | tf_op jit(solution)/shard_map/ppermute | solution.py:440
  538.5 47.1 %collective-permute-start.50 = (f32[160,256]{1,0:T(8,128)}, f32[160,256]{1,0:T(8,128)}, u32[]{:S(2)}, u32[]{:S(2)}) collective-permute-start(f32[160,256]{1,0:T(8,128)} %select_maximum_fusion), channel_id=1, source_target_pairs={{0,1},{1,0},{2,3},{3,2},{4,5},{5,4},{6,7},{7,6},{8,9},{9,8},{10,11... | collective-permute-start | bytes 491528 | tf_op jit(solution)/shard_map/ppermute | solution.py:412
  589.7 40.9 %collective-permute-start.71 = (bf16[1168,768]{1,0:T(8,128)(2,1)}, bf16[1168,768]{1,0:T(8,128)(2,1)S(1)}, u32[]{:S(2)}, u32[]{:S(2)}) collective-permute-start(bf16[1168,768]{1,0:T(8,128)(2,1)} %bitcast.158), channel_id=1, source_target_pairs={{0,1},{3,2},{4,5},{7,6},{8,9},{11,10},{12,13},{15,14},{16,17},{19,... | collective-permute-start | bytes 5382152 | tf_op jit(solution)/shard_map/ppermute | solution.py:438
  605.5 50.1 %collective-permute-start.64 = (bf16[8,272,512]{2,1,0:T(8,128)(2,1)S(1)}, bf16[8,272,512]{2,1,0:T(8,128)(2,1)}, u32[]{:S(2)}, u32[]{:S(2)}) collective-permute-start(bf16[8,272,512]{2,1,0:T(8,128)(2,1)S(1)} %add.362.whole_ref), channel_id=1, source_target_pairs={{1,0},{2,3},{5,4},{6,7},{9,8},{10,11},{13,12},{14,15},{17,16},{18,... | collective-permute-start | bytes 6684680 | tf_op jit(solution)/shard_map/ppermute | solution.py:442
  633.9 90.3 %collective-permute-start.61 = (bf16[8,272,512]{2,1,0:T(8,128)(2,1)}, bf16[8,272,512]{2,1,0:T(8,128)(2,1)}, u32[]{:S(2)}, u32[]{:S(2)}) collective-permute-start(bf16[8,272,512]{2,1,0:T(8,128)(2,1)} %add.360.whole_ref), channel_id=1, source_target_pairs={{1,0},{2,3},{5,4},{6,7},{9,8},{10,11},{13,12},{14,15},{17,16},{18,... | collective-permute-start | bytes 6684680 | tf_op jit(solution)/shard_map/ppermute | solution.py:442
  637.2 120.0 %collective-permute-start.73 = (bf16[1168,768]{1,0:T(8,128)(2,1)}, bf16[1168,768]{1,0:T(8,128)(2,1)}, u32[]{:S(2)}, u32[]{:S(2)}) collective-permute-start(bf16[1168,768]{1,0:T(8,128)(2,1)} %add.370), channel_id=1, source_target_pairs={{1,0},{2,3},{5,4},{6,7},{9,8},{10,11},{13,12},{14,15},{17,16},{18,... | collective-permute-start | bytes 5382152 | tf_op jit(solution)/shard_map/ppermute | solution.py:442
  (110 other events, 1159.5 us)
Sparse Core Ops, SparseCore 0:
  15.0 155.8 all-gather.2
  289.7 139.0 reduce-scatter.1

commit v2 on v1

--- a/solution.py
+++ b/solution.py
@@ -416,36 +416,42 @@
     return swap(value, "dp", PLANE, offset)
 
 
-def plane_gather(block):
+def plane_gather(block, before=()):
     even = [block] + [plane_swap(block, offset) for offset in (2, 4, 6)]
+    if before:
+        even[1] = tie(even[1], *before)
     odd = [plane_swap(piece, CORE_PARTNER) for piece in even]
     return [piece for pair in zip(even, odd) for piece in pair]
 
 
+def tie(value, *after):
+    return lax.optimization_barrier((value, *after))[0]
+
+
+def plane_parts(keep, send):
+    arrived = plane_swap(send, CORE_PARTNER)
+    own = keep[0].astype(f32) + arrived[0].astype(f32)
+    return [own] + [
+        (keep[i].astype(f32) + arrived[i].astype(f32)).astype(bf16) for i in range(1, PLANE // 2)
+    ]
+
+
+def plane_total(parts, after=()):
+    total = tie(parts[0], *after)
+    for i, part in enumerate(parts[1:], 1):
+        total = total + plane_swap(part, 2 * i).astype(f32)
+    return total
+
+
 def plane_reduce(keep, send):
-    arrived = plane_swap(send, CORE_PARTNER)
-    total = keep[0].astype(f32) + arrived[0].astype(f32)
-    others = [
-        plane_swap((keep[i].astype(f32) + arrived[i].astype(f32)).astype(bf16), 2 * i)
-        for i in range(1, PLANE // 2)
-    ]
-    for piece in others:
-        total = total + piece.astype(f32)
-    return total
-
-
-def line_total(block):
-    first = lax.ppermute(block, "seq", [(0, 1), (3, 2)])
-    paired = block + first
-    second = lax.ppermute(paired, "seq", [(1, 2), (2, 1)])
-    whole = paired + second
-    return whole, lax.ppermute(whole, "seq", [(1, 0), (2, 3)])
-
-
-def line_sum(block):
-    whole, third = line_total(block)
-    place = lax.axis_index("seq")
-    return jnp.where((place == 1) | (place == 2), whole, third)
+    return plane_total(plane_parts(keep, send))
+
+
+LINE_STEPS = ([(0, 1), (3, 2)], [(1, 2), (2, 1)], [(1, 0), (2, 3)])
+
+
+def line_step(value, step):
+    return lax.ppermute(value, "seq", LINE_STEPS[step])
 
 
 def nn(left_side, right_side):
@@ -472,7 +478,11 @@
     return [pl.BlockSpec(memory_space=pltpu.VMEM)] * count
 
 
-def call(body, out_shapes, scalar, operands, scratch=(), name=None):
+def cost(flops, moved):
+    return pl.CostEstimate(flops=int(flops), transcendentals=0, bytes_accessed=int(moved))
+
+
+def call(body, out_shapes, scalar, operands, scratch=(), name=None, flops=0):
     return pl.pallas_call(
         body,
         out_shape=[jax.ShapeDtypeStruct(s, t) for s, t in out_shapes],
@@ -480,11 +490,34 @@
         out_specs=whole(len(out_shapes)),
         scratch_shapes=list(scratch),
         name=name,
+        cost_estimate=cost(
+            flops,
+            sum(x.size * x.dtype.itemsize for x in operands)
+            + sum(math.prod(s) * jnp.dtype(t).itemsize for s, t in out_shapes),
+        ),
         compiler_params=pltpu.CompilerParams(vmem_limit_bytes=58 * 1024 * 1024),
     )(scalar, *operands)
 
 
-def lookup_body(char_len, d_ref, ids_ref, table_ref, extra_ref, x_ref):
+EXTRA_ROWS = 32
+VECTOR_ROW = 2
+POS_ROW = 16
+
+
+def lookup_body(
+    char_len,
+    z_ref,
+    ids_ref,
+    table_ref,
+    gate_ref,
+    biases_ref,
+    gain_ref,
+    shift_ref,
+    inner_ref,
+    pos_ref,
+    x_ref,
+    extra_ref,
+):
     words = ids_ref.shape[0]
     rows, lanes = table_ref.shape
     width = lanes // GROUP
@@ -507,39 +540,56 @@
         x_ref[:words, group * lanes : (group + 1) * lanes] = total[
             group * words : (group + 1) * words
         ].astype(bf16)
-    x_ref[words:, :] = extra_ref[...]
-
-
-def fill_taps(taps_ref, weight_ref):
-    depth, filters = weight_ref.shape
+    extra_ref[...] = jnp.zeros_like(extra_ref)
+    at = 0
+    for ref in (gate_ref, biases_ref, gain_ref, shift_ref, inner_ref):
+        extra_ref[at : at + ref.shape[0], : ref.shape[1]] = ref[...].astype(f32)
+        at += ref.shape[0]
+    per = EXTRA_ROWS - POS_ROW
+    part = pos_ref.shape[1]
+    for i in range(words // per):
+        rows = pl.ds(pl.multiple_of(z_ref[0] * words + i * per, per), per)
+        extra_ref[POS_ROW:, i * part : (i + 1) * part] = pos_ref[rows, :].astype(f32)
+    x_ref[words:, :] = extra_ref[...].astype(bf16)
+
+
+def fill_taps(d, taps_ref, weight_ref, widths_ref):
+    depth = weight_ref.shape[0]
+    filters = weight_ref.shape[1] // PLANE
     char_dim = taps_ref.shape[0] // (2 * GROUP)
+    cols = pl.ds(pl.multiple_of(d * filters, filters), filters)
+    tap = lax.broadcasted_iota(jnp.int32, (depth, filters), 0) // char_dim
+    own = jnp.where(tap < widths_ref[:, cols], weight_ref[:, cols].astype(f32), 0.0).astype(bf16)
     taps_ref[...] = jnp.zeros_like(taps_ref)
     for place in range(GROUP):
         taps_ref[
             place * char_dim : place * char_dim + depth, place * filters : (place + 1) * filters
-        ] = weight_ref[...]
+        ] = own
 
 
 def conv_body(char_len, first_masked, words, d_ref, *refs):
     blocks = refs[:PLANE]
-    (weight_ref, last_ref, bias_ref, h_ref, hb_ref, at_ref, x_ref, ba_ref, bb_ref) = refs[
-        PLANE : PLANE + 9
+    (weight_ref, widths_ref, bias_ref, h_ref, hb_ref, at_ref, x_ref, ba_ref, bb_ref, all_extra_ref) = refs[
+        PLANE : PLANE + 10
     ]
-    taps_ref, extra_ref = refs[PLANE + 9 :]
+    taps_ref, extra_ref = refs[PLANE + 10 :]
     d = d_ref[0]
-    filters = weight_ref.shape[1]
+    filters = h_ref.shape[1]
     held = blocks[0].shape[1]
     lanes = taps_ref.shape[0] // 2
-    fill_taps(taps_ref, weight_ref)
+    fill_taps(d, taps_ref, weight_ref, widths_ref)
+    cols = pl.ds(pl.multiple_of(d * filters, filters), filters)
+    bias = bias_ref[:, cols].astype(f32)
     for k in range(PLANE):
         rows = pl.ds(pl.multiple_of((d ^ k) * words, words), words)
         x_ref[rows, :held] = blocks[k][:words, :]
         x_ref[rows, held:] = jnp.zeros((words, x_ref.shape[1] - held), bf16)
-        extra_ref[d ^ k] = blocks[k][words:, : 2 * filters].astype(f32)
+        extra_ref[d ^ k] = blocks[k][words : words + 16, : 2 * filters].astype(f32)
+        all_extra_ref[d ^ k] = blocks[k][words:, :]
     for half, out in ((0, ba_ref), (PLANE // 2, bb_ref)):
         source = extra_ref[half + d // 2]
         out[...] = jnp.where(d % 2 == 0, source[:, :filters], source[:, filters:])
-    last = last_ref[...]
+    last = char_len - widths_ref[:, cols]
 
     def one(step, carry):
         rows = pl.ds(pl.multiple_of(step * words, words), words)
@@ -559,7 +609,7 @@
                 else:
                     where = jnp.where(value > best, at, where)
                     best = jnp.maximum(value, best)
-        pooled = jnp.maximum(best + bias_ref[...], 0.0)
+        pooled = jnp.maximum(best + bias, 0.0)
         h_ref[rows, :] = pooled
         hb_ref[rows, :] = pooled.astype(bf16)
         at_ref[rows, :] = where
@@ -575,8 +625,8 @@
     a = ba_ref[layer : layer + 1, :]
     b = bb_ref[layer : layer + 1, :]
     for k in range(PLANE):
-        a = a + nn(blocks[k][...], w_ref[d ^ k, 0, 0])
-        b = b + nn(blocks[k][...], w_ref[d ^ k, 0, 1])
+        a = a + nn(blocks[k][...], w_ref[d ^ k, 0])
+        b = b + nn(blocks[k][...], w_ref[d ^ k, 1])
     opened = jax.nn.sigmoid(b)
     ra = jnp.maximum(a, 0.0)
     mixed = opened * h_ref[...] + (1.0 - opened) * ra
@@ -590,7 +640,6 @@
     words, filters = hidden.shape
     part = words // 4
     row = pl.BlockSpec((part, filters), lambda i: (i, 0))
-    depth, parts = weights.shape[1:3]
     return pl.pallas_call(
         functools.partial(highway_body, layer),
         grid=(4,),
@@ -598,13 +647,14 @@
         in_specs=[SMEM_SPEC]
         + [row] * PLANE
         + [
-            pl.BlockSpec((PLANE, 1, parts, filters, filters), lambda i: (0, layer, 0, 0, 0)),
+            pl.BlockSpec(weights.shape, lambda i: (0, 0, 0, 0)),
             pl.BlockSpec(bias_a.shape, lambda i: (0, 0)),
             pl.BlockSpec(bias_b.shape, lambda i: (0, 0)),
             row,
         ],
         out_specs=[row] * 4,
         name=f"highway{layer}",
+        cost_estimate=cost(2 * words * filters * PLANE * 2 * filters, 12e6),
         compiler_params=pltpu.CompilerParams(vmem_limit_bytes=58 * 1024 * 1024),
     )(dvec, *blocks, weights, bias_a, bias_b, hidden)
 
@@ -664,7 +714,7 @@
     for i in range(PLANE // 2):
         for odd, out in ((1, send_ref), (0, keep_ref)):
             j = d ^ odd ^ (2 * i)
-            out[i] = (nt(ga, w_ref[j, 0, 0]) + nt(gb, w_ref[j, 0, 1])).astype(out.dtype)
+            out[i] = (nt(ga, w_ref[j, 0]) + nt(gb, w_ref[j, 1])).astype(out.dtype)
 
 
 def highway_back(layer, dvec, d_hidden, opened, ra, hidden, weights):
@@ -673,7 +723,6 @@
     row = pl.BlockSpec((part, filters), lambda i: (i, 0))
     half = PLANE // 2
     blocks = pl.BlockSpec((half, part, filters), lambda i: (0, i, 0))
-    parts = weights.shape[2]
     return pl.pallas_call(
         highway_back_body,
         grid=(4,),
@@ -687,27 +736,25 @@
         ],
         in_specs=[SMEM_SPEC]
         + [row] * 4
-        + [pl.BlockSpec((PLANE, 1, parts, filters, filters), lambda i: (0, layer, 0, 0, 0))],
+        + [pl.BlockSpec(weights.shape, lambda i: (0, 0, 0, 0))],
         out_specs=[row, row, row, pl.BlockSpec((8, 2 * filters), lambda i: (0, 0)), blocks, blocks],
         name=f"highway_back{layer}",
+        cost_estimate=cost(2 * words * filters * PLANE * 2 * filters, 20e6),
         compiler_params=pltpu.CompilerParams(vmem_limit_bytes=58 * 1024 * 1024),
     )(dvec, d_hidden, opened, ra, hidden, weights)
 
 
 def highway_grad_body(d_ref, *refs):
     blocks = refs[:PLANE]
-    ga_ref, gb_ref, sum_ref, out_ref = refs[PLANE:]
+    ga_ref, gb_ref, out_ref = refs[PLANE:]
     d = d_ref[0]
     filters = ga_ref.shape[1]
-    row = jnp.sum(sum_ref[...], axis=0, keepdims=True)
-    pad = out_ref.shape[1] - filters
-    tail = jnp.where(
-        lax.broadcasted_iota(jnp.int32, (pad, 2 * filters), 0) == 0, row, 0.0
-    ).astype(bf16)
     for k in range(PLANE):
-        out_ref[d ^ k, :filters, :filters] = tn(blocks[k][...], ga_ref[...]).astype(bf16)
-        out_ref[d ^ k, :filters, filters:] = tn(blocks[k][...], gb_ref[...]).astype(bf16)
-        out_ref[d ^ k, filters:, :] = tail
+        for side, grad_ref in enumerate((ga_ref, gb_ref)):
+            piece = tn(blocks[k][...], grad_ref[...]).astype(bf16)
+            out_ref[:, d ^ k, :, side * filters : (side + 1) * filters] = piece.reshape(
+                DEPTH, filters // DEPTH, filters
+            )
 
 
 def spread_groups(char_len, filters, grad, at, spread_ref, group):
@@ -720,12 +767,12 @@
     return count
 
 
-def char_back_body(char_len, words, d_ref, h_ref, at_ref, dh_ref, weight_ref, gp_ref, keep_ref, send_ref, taps_ref, spread_ref, chars_ref):
+def char_back_body(char_len, words, d_ref, h_ref, at_ref, dh_ref, weight_ref, widths_ref, gp_ref, keep_ref, send_ref, taps_ref, spread_ref, chars_ref):
     d = d_ref[0]
     filters = h_ref.shape[1]
     lanes = taps_ref.shape[0] // 2
     held = keep_ref.shape[2]
-    fill_taps(taps_ref, weight_ref)
+    fill_taps(d, taps_ref, weight_ref, widths_ref)
     chars_ref[...] = jnp.zeros_like(chars_ref)
 
     def one(step, carry):
@@ -802,9 +849,10 @@
     out_ref[...] = fold
 
 
-def pack_highway_body(carry_ref, gate_ref, out_ref):
-    out_ref[0, :, 0] = carry_ref[...]
-    out_ref[0, :, 1] = gate_ref[...]
+def pack_highway_body(carry_ref, gate_ref, *outs):
+    for layer, out_ref in enumerate(outs):
+        out_ref[0, 0] = carry_ref[layer]
+        out_ref[0, 1] = gate_ref[layer]
 
 
 def pack_highway(weights):
@@ -814,51 +862,90 @@
     return pl.pallas_call(
         pack_highway_body,
         grid=(PLANE,),
-        out_shape=jax.ShapeDtypeStruct((PLANE, layers, 2, rows, own), bf16),
+        out_shape=[jax.ShapeDtypeStruct((PLANE, 2, rows, own), bf16)] * layers,
         in_specs=[
             pl.BlockSpec(block, lambda j: (0, 0, j)),
             pl.BlockSpec(block, lambda j: (0, 0, PLANE + j)),
         ],
-        out_specs=pl.BlockSpec((1, layers, 2, rows, own), lambda j: (j, 0, 0, 0, 0)),
+        out_specs=[pl.BlockSpec((1, 2, rows, own), lambda j: (j, 0, 0, 0))] * layers,
         name="pack_highway",
     )(weights, weights)
 
 
-def pack_encoder_body(qkv_ref, out_ref, inner_ref, outer_ref, small_ref, packed_ref):
+def pack_encoder_body(qkv_ref, out_ref, inner_ref, outer_ref, packed_ref):
     dim = packed_ref.shape[1]
     at = 0
-    for ref in (qkv_ref, out_ref, inner_ref, outer_ref, small_ref):
+    for ref in (qkv_ref, out_ref, inner_ref, outer_ref):
         rows = ref.shape[0]
         for start in range(0, ref.shape[1], dim):
             packed_ref[at : at + rows, :] = ref[:, start : start + dim]
             at += rows
 
 
-def finish_highway_body(flag_ref, whole_ref, third_ref, *refs):
-    mid = flag_ref[0] == 1
-    refs[-1][0] = jnp.where(mid, whole_ref[0].astype(f32), third_ref[0].astype(f32))
-
-
-def finish_highway(layer, layers, flag, total, third, previous):
-    own = total.shape[2] // 2
-    block = pl.BlockSpec((1, own, own), lambda half, j: (j, 0, half))
-    shape = jax.ShapeDtypeStruct((layers, own, 2 * PLANE * own), f32)
-    operands = [flag, total, third]
-    specs = [SMEM_SPEC, block, block]
+def finish_highway_body(blocks_ref, *refs):
+    out_ref = refs[-1]
+    own = out_ref.shape[1]
+    half = out_ref.shape[2] // 2
+    for j in range(PLANE):
+        for side in range(2):
+            at = slice(j * own + side * half, (j + 1) * own + side * half)
+            cols = slice(side * own, (side + 1) * own)
+            out_ref[0, :, at] = blocks_ref[:, j, :, cols].reshape(own, own).astype(f32)
+
+
+def finish_highway(layer, layers, blocks, previous):
+    own = blocks.shape[3] // 2
+    width = 2 * PLANE * own
+    operands = [blocks]
+    specs = [pl.BlockSpec(blocks.shape, lambda i: (0, 0, 0, 0))]
     aliases = {}
     if previous is not None:
         operands.append(previous)
         specs.append(pl.BlockSpec(memory_space=pl.ANY))
-        aliases = {3: 0}
+        aliases = {1: 0}
     return pl.pallas_call(
         finish_highway_body,
-        grid=(2, PLANE),
-        out_shape=shape,
+        grid=(1,),
+        out_shape=jax.ShapeDtypeStruct((layers, own, width), f32),
         in_specs=specs,
-        out_specs=pl.BlockSpec((1, own, own), lambda half, j: (layer, 0, half * PLANE + j)),
+        out_specs=pl.BlockSpec((1, own, width), lambda i: (layer, 0, 0)),
         input_output_aliases=aliases,
         name=f"finish_highway{layer}",
+        compiler_params=pltpu.CompilerParams(vmem_limit_bytes=58 * 1024 * 1024),
     )(*operands)
+
+
+def finish_ends_body(d_ref, *refs):
+    blocks = refs[:PLANE]
+    widths_ref, conv_ref, bias_ref, gates_ref, table_ref, held_ref = refs[PLANE:]
+    d = d_ref[0]
+    own = blocks[0].shape[1]
+    rows = conv_ref.shape[0]
+    lanes = table_ref.shape[1]
+    char_dim = lanes // GROUP
+    tap = lax.broadcasted_iota(jnp.int32, (rows, own), 0) // char_dim
+    for k in range(PLANE):
+        cols = pl.ds(pl.multiple_of((d ^ k) * own, own), own)
+        conv_ref[:, cols] = jnp.where(tap < widths_ref[:, cols], blocks[k][:rows, :], 0.0)
+        bias_ref[:, cols] = blocks[k][rows : rows + 8, :]
+        gates_ref[:, cols] = blocks[k][rows + 8 : rows + 16, :]
+        held_ref[d ^ k] = blocks[k][rows + 16 :, :lanes]
+    total = held_ref[0]
+    for j in range(1, PLANE):
+        total = total + held_ref[j]
+    table_ref[...] = total
+
+
+def finish_encoder_body(d_ref, low_ref, high_ref, *outs):
+    dim = low_ref.shape[1]
+    at = 0
+    for ref in outs:
+        count = ref.shape[0]
+        for left in range(0, ref.shape[1], dim):
+            low = low_ref.shape[0]
+            source = low_ref[at : at + count] if at < low else high_ref[at - low : at - low + count]
+            ref[:, left : left + dim] = source.astype(f32)
+            at += count
 
 
 def normalize(value):
@@ -898,7 +985,9 @@
     w_hbm,
     result_ref,
     d_own_ref,
-    d_send_ref,
+    send1_ref,
+    send2_ref,
+    send3_ref,
     embs_ref,
     gq_ref,
     gk_ref,
@@ -1045,7 +1134,7 @@
         if i == 0:
             d_own_ref[...] = d_res + nt(gq_ref[...], square(0)) + piece
         else:
-            d_send_ref[i - 1] = piece.astype(bf16)
+            (send1_ref, send2_ref, send3_ref)[i - 1][...] = piece.astype(bf16)
 
 
 def encoder_grad_body(
@@ -1061,10 +1150,12 @@
     gup_ref,
     gdown_ref,
     stats_ref,
-    out_hbm,
+    keep_hbm,
+    send_hbm,
     out_ref,
     sems,
 ):
+    d = flag_ref[0]
     words, dim = gq_ref.shape
     part = dim // PLANE
     wide = act_ref.shape[1] // PLANE
@@ -1075,11 +1166,15 @@
         out_ref[:, low:high, :] = value.reshape(PLANE, high - low, dim)
 
     def send(low, high):
-        copy = pltpu.make_async_copy(
-            out_ref.at[:, low:high, :], out_hbm.at[:, low:high, :], sems.at[len(pieces)]
-        )
-        copy.start()
-        pieces.append(copy)
+        for i in range(PLANE // 2):
+            for odd, hbm in ((1, send_hbm), (0, keep_hbm)):
+                copy = pltpu.make_async_copy(
+                    out_ref.at[d ^ odd ^ (2 * i), low:high, :],
+                    hbm.at[i, low:high, :],
+                    sems.at[len(pieces)],
+                )
+                copy.start()
+                pieces.append(copy)
 
     low = (4 + in_parts) * part
     per = dim // wide
@@ -1116,7 +1211,9 @@
     shapes = [
         ((words, dim), bf16),
         ((words, dim), f32),
-        ((DEPTH - 1, words, dim), bf16),
+        ((words, dim), bf16),
+        ((words, dim), bf16),
+        ((words, dim), bf16),
         ((keys, dim), bf16),
         ((words, dim), bf16),
         ((keys, dim), bf16),
@@ -1145,20 +1242,29 @@
             pltpu.SemaphoreType.DMA((4,)),
         ],
         name="encoder",
+        cost_estimate=cost(16e9, 30e6),
         compiler_params=pltpu.CompilerParams(vmem_limit_bytes=58 * 1024 * 1024),
     )(flag, embedded, *others, small, query_segs, key_segs, key_pads, cotangent, weights)
-    result, d_own, d_send = outs[:3]
+    result, d_own = outs[:2]
+    d_embedded = d_own
+    first = None
+    for offset in range(1, DEPTH):
+        piece = swap(outs[1 + offset], "seq", DEPTH, offset)
+        first = piece if first is None else first
+        d_embedded = d_embedded + piece.astype(f32)
+    saved = [tie(outs[5], first), *outs[6:]]
     rows = (4 + in_parts) * part + ff_dim // PLANE + 16
     grads = pl.pallas_call(
         encoder_grad_body,
-        out_shape=jax.ShapeDtypeStruct((PLANE, rows, dim), bf16),
+        out_shape=[jax.ShapeDtypeStruct((PLANE // 2, rows, dim), bf16)] * 2,
         in_specs=[SMEM_SPEC] + [vmem] * 11,
-        out_specs=hbm,
-        scratch_shapes=[VMEM((PLANE, rows, dim), bf16), pltpu.SemaphoreType.DMA((3,))],
+        out_specs=[hbm] * 2,
+        scratch_shapes=[VMEM((PLANE, rows, dim), bf16), pltpu.SemaphoreType.DMA((3 * PLANE,))],
         name="encoder_grad",
+        cost_estimate=cost(6e9, 20e6),
         compiler_params=pltpu.CompilerParams(vmem_limit_bytes=58 * 1024 * 1024),
-    )(flag, *outs[3:])
-    return result, d_own, d_send, grads
+    )(flag, *saved)
+    return result, d_embedded, grads
 
 
 def round_up(value, multiple):
@@ -1207,74 +1313,32 @@
     ids = char_ids.reshape(words, char_len)
     table_rows = round_up(chars, 128)
     table = jnp.pad(jnp.tile(char_table, (1, GROUP)), ((0, table_rows - chars), (0, 0)))
-    extra = jnp.pad(hw_bias, ((0, 16 - depth), (0, held - hw_bias.shape[1])))
     (own_x,) = call(
         functools.partial(lookup_body, char_len),
-        [((words + 16, held), bf16)],
-        dvec,
-        (ids, table, extra),
+        [((words + EXTRA_ROWS, held), bf16)],
+        z.astype(jnp.int32)[None],
+        (ids, table, hw_bias, d_biases, norm_gain, norm_shift, ff_in_bias[None, :], pos_table),
+        [VMEM((EXTRA_ROWS, held), f32)],
         name="lookup",
     )
-    x_blocks = plane_gather(own_x)
-
-    hw_cols = lax.all_to_all(pack_highway(hw_weight), "dp", 0, 0)
-
-    small = jnp.concatenate(
-        [d_biases.reshape(-1), norm_gain.reshape(-1), norm_shift.reshape(-1), ff_in_bias]
-    )
-    small_rows = round_up(small.shape[0], model_dim) // model_dim
-    small = jnp.pad(small, (0, small_rows * model_dim - small.shape[0])).reshape(-1, model_dim)
-    pos_here = lax.dynamic_slice_in_dim(pos_table, z * words, words, 0).reshape(-1, model_dim)
-    pos_rows = pos_here.shape[0]
-    tail_rows = round_up(small_rows + pos_rows, 16)
-    tail = jnp.pad(
-        jnp.concatenate([small, pos_here], axis=0), ((0, tail_rows - small_rows - pos_rows), (0, 0))
-    )
+    hw_weight, qkv_weight, unused = lax.optimization_barrier((hw_weight, qkv_weight, own_x))
+    hw_packed = pack_highway(hw_weight)
+
+    x_blocks = plane_gather(own_x, hw_packed)
+    hw_cols = [lax.all_to_all(tie(hw_packed[0], x_blocks[2]), "dp", 0, 0)]
+
     in_parts = ff_in_weight.shape[1] // model_dim
     weight_rows = (4 + in_parts) * part + ff_dim // PLANE
     packed = pl.pallas_call(
         pack_encoder_body,
-        out_shape=jax.ShapeDtypeStruct((weight_rows + tail_rows, model_dim), bf16),
+        out_shape=jax.ShapeDtypeStruct((weight_rows, model_dim), bf16),
         name="pack_encoder",
-    )(qkv_weight, out_weight, ff_in_weight, ff_out_weight, tail)
-    gathered = lax.all_gather(packed, "dp", axis=0, tiled=False)
-    at = weight_rows
-    small = gathered[:, at : at + small_rows].reshape(PLANE, -1)
-    at += small_rows
-    pos_full = (
-        gathered[:, at : at + pos_rows]
-        .reshape(PLANE, words, part)
-        .transpose(1, 0, 2)
-        .reshape(words, model_dim)
-    )
-
-    def rows_of(start, count):
-        piece = small[:, start : start + count * part].reshape(PLANE, count, part)
-        return piece.transpose(1, 0, 2).reshape(count, model_dim).astype(f32)
-
-    inner_bias = small[:, 11 * part : 11 * part + ff_dim // PLANE].reshape(in_parts, model_dim)
-    small_full = jnp.concatenate(
-        [
-            rows_of(0, 5),
-            rows_of(5 * part, 3),
-            rows_of(8 * part, 3),
-            inner_bias.astype(f32),
-            jnp.zeros((16 - 11 - in_parts, model_dim), f32),
-        ],
-        axis=0,
-    )
-
+    )(qkv_weight, out_weight, ff_in_weight, ff_out_weight)
     widths = filter_widths(filters)
-    tap_mask = jnp.asarray(np.arange(tap_count)[:, None] < widths[None, :])
-    masked_kernel = jnp.where(tap_mask[:, None, :], conv_weight, 0).reshape(
-        tap_count * char_dim, filters
-    )
-    own_kernel = lax.dynamic_slice_in_dim(masked_kernel, d * own, own, 1)
-    last_place = jnp.asarray((char_len - widths)[None, :], jnp.int32)
-    own_last = lax.dynamic_slice_in_dim(last_place, d * own, own, 1)
-    own_bias = lax.dynamic_slice_in_dim(conv_bias.astype(f32)[None, :], d * own, own, 1)
+    widths_row = jnp.asarray(widths[None, :], jnp.int32)
+    taps = conv_weight.reshape(tap_count * char_dim, filters)
     taps_shape = VMEM((2 * lanes, GROUP * own), bf16)
-    hidden0, hidden0_b, top_at, x_all, bias_a, bias_b = call(
+    hidden0, hidden0_b, top_at, x_all, bias_a, bias_b, extras = call(
         functools.partial(conv_body, char_len, char_len - tap_count + 1, words),
         [
             ((all_words, own), f32),
@@ -1283,22 +1347,47 @@
             ((all_words, held + lanes), bf16),
             ((16, own), f32),
             ((16, own), f32),
+            ((PLANE, EXTRA_ROWS, held), bf16),
         ],
         dvec,
-        (*x_blocks, own_kernel, own_last, own_bias),
+        (*x_blocks, taps, widths_row, conv_bias[None, :]),
         [taps_shape, VMEM((PLANE, 16, 2 * own), f32)],
         name="conv",
+        flops=8e9,
     )
 
     hidden, hidden_b = hidden0, hidden0_b
     saved = []
     for layer in range(depth):
-        blocks = plane_gather(hidden_b)
+        blocks = plane_gather(hidden_b, (hw_cols[layer],))
+        if layer + 1 < depth:
+            following, packed = tie((hw_packed[layer + 1], packed), blocks)
+            hw_cols.append(lax.all_to_all(following, "dp", 0, 0))
+        if layer == 0:
+            gathered = lax.all_gather(packed, "dp", axis=0, tiled=False)
         opened, ra, following, following_b = highway(
-            layer, dvec, blocks, hw_cols, bias_a, bias_b, hidden
+            layer, dvec, blocks, hw_cols[layer], bias_a, bias_b, hidden
         )
         saved.append((blocks, opened, ra, hidden))
         hidden, hidden_b = following, following_b
+    vectors = extras[:, VECTOR_ROW : VECTOR_ROW + 11, :part].astype(f32)
+    inner_bias = extras[:, VECTOR_ROW + 11, : ff_dim // PLANE].reshape(in_parts, model_dim)
+    small_full = jnp.concatenate(
+        [
+            vectors.transpose(1, 0, 2).reshape(11, model_dim),
+            inner_bias.astype(f32),
+            jnp.zeros((16 - 11 - in_parts, model_dim), f32),
+        ],
+        axis=0,
+    )
+    per = EXTRA_ROWS - POS_ROW
+    pos_full = (
+        extras[:, POS_ROW:, : (words // per) * part]
+        .reshape(PLANE, per, words // per, part)
+        .transpose(2, 1, 0, 3)
+        .reshape(words, model_dim)
+    )
+
     half = PLANE // 2
     keep, send = call(
         project_body,
@@ -1322,7 +1411,7 @@
         )
 
     key_segs, key_pads = by_offset(segment_ids), by_offset(pad_mask)
-    result, d_own, d_send, enc_grads = encoder(
+    result, d_embedded, (enc_keep, enc_send) = encoder(
         dvec,
         embedded,
         others,
@@ -1333,10 +1422,7 @@
         cotangent.reshape(words, model_dim),
         gathered,
     )
-    d_embedded = d_own
-    for offset in range(1, DEPTH):
-        d_embedded = d_embedded + swap(d_send[offset - 1], "seq", DEPTH, offset).astype(f32)
-    enc_slice = lax.psum_scatter(enc_grads, "dp", scatter_dimension=0, tiled=True)[0]
+    enc_arrived = plane_swap(enc_send, CORE_PARTNER)
     d_summed = normalize_back(d_embedded, normal0, scale0, small_full[5])
     grad_proj = jnp.concatenate(
         [
@@ -1356,22 +1442,40 @@
         (*gp_blocks, proj_weight, hidden_b),
         name="unproject",
     )
-    hw_slices = [None] * depth
+    hw_sums, gate_parts, quarters = {}, {}, {}
+    enc_parts = None
     for layer in reversed(range(depth)):
         blocks, opened, ra, hidden = saved[layer]
         ga, gb, d_carry, sums, keep, send = highway_back(
-            layer, dvec, d_hidden, opened, ra, hidden, hw_cols
+            layer, dvec, d_hidden, opened, ra, hidden, hw_cols[layer]
         )
-        d_hidden = d_carry + plane_reduce(keep, send)
+        parts = plane_parts(keep, send)
+        gate_parts[layer] = jnp.sum(sums, axis=0).reshape(2, own)
         (cols_grad,) = call(
             highway_grad_body,
-            [((PLANE, own + 16, 2 * own), bf16)],
+            [((DEPTH, PLANE, own // DEPTH, 2 * own), bf16)],
             dvec,
-            (*blocks, ga, gb, sums),
+            (*blocks, tie(ga, parts[1]), gb),
             name=f"highway_grad{layer}",
+            flops=2 * all_words * filters * 2 * own,
         )
-        hw_slices[layer] = lax.all_to_all(cols_grad, "dp", 0, 0)
-
+        after = [cols_grad]
+        quarter = lax.psum_scatter(cols_grad, "seq", scatter_dimension=0, tiled=False)
+        quarters[layer] = lax.all_to_all(quarter, "dp", 0, 0)
+        hw_sums[layer] = lax.all_gather(quarters[layer], "seq", axis=0, tiled=False)
+        if enc_parts is None:
+            arrived = tie(enc_arrived, parts[1], cols_grad)
+            enc_parts = [enc_keep[0].astype(f32) + arrived[0].astype(f32)] + [
+                (enc_keep[i].astype(f32) + arrived[i].astype(f32)).astype(bf16)
+                for i in range(1, half)
+            ]
+            enc_rest = [plane_swap(enc_parts[i], 2 * i) for i in range(1, half)]
+            after.append(enc_parts[1])
+        d_hidden = d_carry + plane_total(parts, after)
+    enc_sum = enc_parts[0]
+    for piece in enc_rest[:-1]:
+        enc_sum = enc_sum + tie(piece, d_hidden).astype(f32)
+    d_hidden = tie(d_hidden, enc_sum, *[quarters[other] for other in range(1, depth)])
     grad_pooled, keep, send = call(
         functools.partial(char_back_body, char_len, words),
         [
@@ -1380,15 +1484,17 @@
             ((half, words, held), bf16),
         ],
         dvec,
-        (hidden0, top_at, d_hidden, own_kernel),
+        (hidden0, top_at, d_hidden, taps, widths_row),
         [
             taps_shape,
             VMEM((2 * words, GROUP * own), bf16),
             VMEM((all_words, held + lanes), f32),
         ],
         name="char_back",
-    )
-    char_grads = plane_reduce(keep, send)
+        flops=8e9,
+    )
+    parts = plane_parts(keep, send)
+    grad_pooled = tie(grad_pooled, parts[1])
     (conv_part,) = call(
         functools.partial(conv_grad_body, char_len),
         [((tap_count * char_dim + 8, own), f32)],
@@ -1396,7 +1502,18 @@
         (x_all, top_at, grad_pooled),
         [VMEM((all_words, GROUP * own), bf16), VMEM((2 * lanes, all_words), bf16)],
         name="conv_grad",
-    )
+        flops=8e9,
+    )
+    enc_slice = (tie(enc_sum, conv_part) + enc_rest[-1].astype(f32)).astype(bf16)
+    top_own = lax.dynamic_slice_in_dim(top_sums, d * part, part, 1).astype(bf16)
+    top_own = jnp.pad(top_own, ((0, 0), (0, 128 - part)))
+    top_all = lax.dynamic_update_slice_in_dim(
+        jnp.zeros((seq_len, 128), bf16), top_own[:words], z * words, 0
+    )
+    cut = (4 + in_parts) * part
+    lines = [enc_slice[:cut], enc_slice[cut:], proj_grad, jnp.concatenate([top_all, top_own[words:]], axis=0)]
+    moved = [line_step(value, 0) for value in lines]
+    char_grads = tie(plane_total(parts, (conv_part, enc_slice)), quarters[0])
     fold_rows = round_up(-(-chars // GROUP), 8)
     (table_part,) = call(
         functools.partial(table_grad_body, char_len),
@@ -1404,46 +1521,67 @@
         dvec,
         (ids.T, char_grads),
         name="table_grad",
-    )
+        flops=2e9,
+    )
+    gate_rows = jnp.concatenate([gate_parts[layer] for layer in range(depth)], axis=0)
     ends = jnp.concatenate(
-        [conv_part, jnp.pad(table_part, ((0, 0), (0, own - lanes)))], axis=0
+        [
+            conv_part,
+            jnp.pad(gate_rows, ((0, 8 - 2 * depth), (0, 0))),
+            jnp.pad(table_part, ((0, 0), (0, own - lanes))),
+        ],
+        axis=0,
     )
     ends = ends + swap(ends, "seq", DEPTH, 1)
     ends = ends + swap(ends, "seq", DEPTH, 2)
-    end_blocks = jnp.stack(plane_gather(ends))
-    ordered = [lax.dynamic_index_in_dim(end_blocks, d ^ j, 0, False) for j in range(PLANE)]
+    lines = [value + tie(piece, ends) for value, piece in zip(lines, moved)]
+    moved = [line_step(value, 1) for value in lines]
+    end_blocks = plane_gather(ends)
     conv_rows = tap_count * char_dim
-    conv_total = jnp.concatenate([piece[:conv_rows] for piece in ordered], axis=1)
-    conv_total = jnp.where(
-        tap_mask[:, None, :], conv_total.reshape(tap_count, char_dim, filters), 0.0
-    )
-    conv_bias_total = jnp.concatenate([piece[conv_rows] for piece in ordered])
-    table_total = sum(piece[conv_rows + 8 :, :lanes] for piece in ordered)
+    conv_total, conv_bias_total, gate_sums, table_total = call(
+        finish_ends_body,
+        [
+            ((conv_rows, filters), f32),
+            ((8, filters), f32),
+            ((8, filters), f32),
+            ((fold_rows, lanes), f32),
+        ],
+        dvec,
+        (*end_blocks, widths_row),
+        [VMEM((PLANE, fold_rows, lanes), f32)],
+        name="finish_ends",
+    )
+    conv_total = conv_total.reshape(tap_count, char_dim, filters)
+    conv_bias_total = conv_bias_total[0]
     table_total = (
         table_total.reshape(fold_rows, GROUP, char_dim)
         .transpose(1, 0, 2)
         .reshape(GROUP * fold_rows, char_dim)[:chars]
     )
 
-    top_own = lax.dynamic_slice_in_dim(top_sums, d * part, part, 1).astype(bf16)
-    top_own = jnp.pad(top_own, ((0, 0), (0, 128 - part)))
-    top_all = lax.dynamic_update_slice_in_dim(
-        jnp.zeros((seq_len, 128), bf16), top_own[:words], z * words, 0
-    )
-    top_total = line_sum(jnp.concatenate([top_all, top_own[words:]], axis=0))[:, :part].astype(f32)
+    lines = [value + tie(piece, ends) for value, piece in zip(lines, moved)]
+    moved = [line_step(value, 2) for value in lines]
+    middle = (z == 1) | (z == 2)
+    *enc_total, proj_total, top_total = (
+        jnp.where(middle, value, piece) for value, piece in zip(lines, moved)
+    )
+    top_total = top_total[:, :part].astype(f32)
     pos_total = top_total[:seq_len]
     gain0, shift0, bias0 = top_total[seq_len], top_total[seq_len + 1], top_total[seq_len + 16]
-    proj_total = line_sum(proj_grad).astype(f32)
-    enc_total = line_sum(enc_slice).astype(f32)
-    qkv_total = jnp.concatenate([enc_total[i * part : (i + 1) * part] for i in range(3)], axis=1)
-    out_total = enc_total[3 * part : 4 * part]
-    at = 4 * part
-    inner_total = jnp.concatenate(
-        [enc_total[at + i * part : at + (i + 1) * part] for i in range(in_parts)], axis=1
-    )
-    at += in_parts * part
-    outer_total = enc_total[at : at + ff_dim // PLANE]
-    small_total = enc_total[weight_rows:]
+    proj_total = proj_total.astype(f32)
+    qkv_total, out_total, inner_total, outer_total, small_total = call(
+        finish_encoder_body,
+        [
+            ((part, 3 * model_dim), f32),
+            ((part, model_dim), f32),
+            ((part, ff_dim), f32),
+            ((ff_dim // PLANE, model_dim), f32),
+            ((16, model_dim), f32),
+        ],
+        dvec,
+        enc_total,
+        name="finish_encoder",
+    )
     own_small = lax.dynamic_slice_in_dim(small_total, d * part, part, 1)
     bias_total = jnp.concatenate([bias0[None], own_small[1:5]], axis=0)
     gain_total = jnp.concatenate([gain0[None], own_small[6:8]], axis=0)
@@ -1452,14 +1590,11 @@
         small_total[11 : 11 + in_parts].reshape(-1), d * (ff_dim // PLANE), ff_dim // PLANE, 0
     )
 
-    flag = ((z == 1) | (z == 2)).astype(jnp.int32)[None]
     hw_total, hw_bias_totals = None, [None] * depth
     for layer in reversed(range(depth)):
-        whole_sum, third = line_total(hw_slices[layer])
-        hw_total = finish_highway(layer, depth, flag, whole_sum, third, hw_total)
-        row = jnp.where(flag[0] == 1, whole_sum[:, own], third[:, own])
-        row = row.reshape(PLANE, 2, own).transpose(1, 0, 2).reshape(-1)
-        hw_bias_totals[layer] = lax.dynamic_slice_in_dim(row, d * 2 * own, 2 * own, 0).astype(f32)
+        hw_total = finish_highway(layer, depth, hw_sums[layer], hw_total)
+        row = gate_sums[2 * layer : 2 * layer + 2].reshape(-1)
+        hw_bias_totals[layer] = lax.dynamic_slice_in_dim(row, d * 2 * own, 2 * own, 0)
 
     output = result.reshape(1, words, model_dim)
     return (

time: 780 us -> 711 us (0.912)
  starting transfers between devices: 131 us -> 96.6 us
  waiting for transfers between devices: 390 us -> 364 us
    ppermute x59 -> x63, starting transfers between devices: 90.7 us -> 60.9 us  [swap(): lax.ppermute(value, axis_name, [(at, at ^ offset) for at in range(size)])]
    all_to_all x3 -> x4, waiting for transfers between devices: 18.4 us -> 3.36 us  [the longest x2 3.36 us: plane_shards(): quarters[layer] = lax.all_to_all(quarter, 'dp', 0, 0)]
    pallas_call x4, Pallas kernels: 36.4 us -> 23.6 us  [the longest x1 9.24 us: encoder(): pl.pallas_call(encoder_grad_body, out_shape=[jax.ShapeDtypeStruct((PLANE...]
    ppermute x15 -> x12, waiting for transfers between devices: 108 us -> 100 us  [line_step(): return lax.ppermute(value, 'seq', LINE_STEPS[step])]
    convert_element_type x10 -> x8, other arithmetic: 15.8 us -> 23.5 us  [the longest x4 11.1 us: plane_parts(): (keep[i].astype(f32) + arrived[i].astype(f32)).astype(bf16)]
    pallas_call x9 -> x11, Pallas kernels: 60.3 us -> 67.1 us  [call(): pl.pallas_call(body, out_shape=[jax.ShapeDtypeStruct(s, t) for s, t in ou...]
    ppermute x15 -> x12, starting transfers between devices: 26.5 us -> 20.6 us  [line_step(): return lax.ppermute(value, 'seq', LINE_STEPS[step])]
    add x14 -> x13, other arithmetic: 25.3 us -> 20.2 us  [the longest x8 8.77 us: plane_shards(): lines = [value + tie(piece, ends) for value, piece in zip(lines, moved)]]
  transfers between devices with their start and end apart: 79 -> 84, of which waited for: 40 -> 38; matrix products, arithmetic and copies ran while one was open for 8% -> 10% of each run, Pallas kernels for 15% -> 16%
where the time goes in v2:
time: 711 us; the launch traced here: 704 us
  waiting for transfers between devices  364 us (51%)
  Pallas kernels  150 us (21%)
  starting transfers between devices  96.6 us (14%)
  other arithmetic  54.2 us (8%)
  local copies, waits for them, and re-layouts  23.3 us (3%)
  between operations  14.8 us (2%)
    ppermute x63, waiting for transfers between devices, swap(): lax.ppermute(value, axis_name, [(at, at ^ offset) for at in range(size)])  261 us
    ppermute x12, waiting for transfers between devices, line_step(): return lax.ppermute(value, 'seq', LINE_STEPS[step])  100 us
    pallas_call x11, Pallas kernels, call(): pl.pallas_call(body, out_shape=[jax.ShapeDtypeStruct(s, t) for s, t in ou...  67.1 us
    ppermute x63, starting transfers between devices, swap(): lax.ppermute(value, axis_name, [(at, at ^ offset) for at in range(size)])  60.9 us
    pallas_call x1, Pallas kernels, encoder(): pl.pallas_call(functools.partial(encoder_body, head_count, in_parts), out...  23.9 us
    ppermute x12, starting transfers between devices, line_step(): return lax.ppermute(value, 'seq', LINE_STEPS[step])  20.6 us
    pallas_call x2, Pallas kernels, highway(): pl.pallas_call(functools.partial(highway_body, layer), grid=(4,), out_sha...  16.2 us
    pallas_call x2, Pallas kernels, highway_back(): pl.pallas_call(highway_back_body, grid=(4,), out_shape=[jax.ShapeDtypeStr...  16.1 us
  transfers between devices with their start and end apart: 84, of which 38 were waited for; matrix products, arithmetic and copies ran while one was open for 10% of the time, Pallas kernels for 16%

profile of v2, /device:TPU:0, one launch (start us, length us, event | category | flops | bytes accessed | tf_op | source)
XLA Modules:
  0.0 703.7 jit_solution(15377795192923612502)
XLA Ops:
  36.3 12.1 %conv.1 = (f32[1024,256]{1,0:T(8,128)}, bf16[1024,256]{1,0:T(8,128)(2,1)}, s32[1024,256]{1,0:T(8,128)}, bf16[1024,1024]{1,0:T(8,128)(2,1)}, f32[16,256]{1,0:T(8,...) custom-call(s32[1]{0:T(128)} %bitcast.d_ref.flag_ref, bf16[160,896]{1,0:T(8,128)(2,1)} %lookup.1.refs_0_, ...), custom_call_target="tpu_custom_call" | custom-call | flops 8000000000 | bytes 7974912 | tf_op jit(solution)/shard_map/conv/pallas_call | solution.py:486
  51.8 28.3 %collective-permute-done.10.refs_4_ = bf16[1024,256]{1,0:T(8,128)(2,1)S(1)} collective-permute-done((bf16[1024,256]{1,0:T(8,128)(2,1)}, bf16[1024,256]{1,0:T(8,128)(2,1)S(1)}, u32[]{:S(2)}, u32[]{:S(2)}) %collective-permute-start.10) | collective-permute-done | bytes 524320 | tf_op jit(solution)/shard_map/ppermute | solution.py:412
  87.9 7.8 %highway0.1 = (f32[1024,256]{1,0:T(8,128)}, f32[1024,256]{1,0:T(8,128)}, f32[1024,256]{1,0:T(8,128)}, bf16[1024,256]{1,0:T(8,128)(2,1)}) custom-call(s32[1]{0:T(128)} %bitcast.d_ref.flag_ref, bf16[1024,256]{1,0:T(8,128)(2,1)} %get-tuple-element.112.refs_0_, bf16[1024,256]{1,0:T(8,128)(2,1)} %collective-permute-done.7.refs_1_, ...), custom_call_target="tpu_custom_call" | custom-call | flops 2147483648 | bytes 12000000 | tf_op jit(solution)/shard_map/highway0/pallas_call | solution.py:643
  99.3 54.0 %collective-permute-done.17.refs_4_ = bf16[1024,256]{1,0:T(8,128)(2,1)S(1)} collective-permute-done((bf16[1024,256]{1,0:T(8,128)(2,1)}, bf16[1024,256]{1,0:T(8,128)(2,1)S(1)}, u32[]{:S(2)}, u32[]{:S(2)}) %collective-permute-start.17) | collective-permute-done | bytes 524320 | tf_op jit(solution)/shard_map/ppermute | solution.py:412
  157.3 8.4 %highway1.1 = (f32[1024,256]{1,0:T(8,128)}, f32[1024,256]{1,0:T(8,128)}, f32[1024,256]{1,0:T(8,128)}, bf16[1024,256]{1,0:T(8,128)(2,1)}) custom-call(s32[1]{0:T(128)} %bitcast.d_ref.flag_ref, bf16[1024,256]{1,0:T(8,128)(2,1)} %get-tuple-element.118.refs_0_, bf16[1024,256]{1,0:T(8,128)(2,1)} %collective-permute-done.14.refs_1_, ...), custom_call_target="tpu_custom_call" | custom-call | flops 2147483648 | bytes 12000000 | tf_op jit(solution)/shard_map/highway1/pallas_call | solution.py:643
  178.6 7.1 %collective-permute-done.24 = bf16[128,768]{1,0:T(8,128)(2,1)S(1)} collective-permute-done((bf16[128,768]{1,0:T(8,128)(2,1)S(1)}, bf16[128,768]{1,0:T(8,128)(2,1)S(1)}, u32[]{:S(2)}, u32[]{:S(2)}) %collective-permute-start.24) | collective-permute-done | bytes 196640 | tf_op jit(solution)/shard_map/ppermute | solution.py:412
  205.3 9.0 %collective-permute-done.26.e2_ref = bf16[128,768]{1,0:T(8,128)(2,1)S(1)} collective-permute-done((bf16[128,768]{1,0:T(8,128)(2,1)S(1)}, bf16[128,768]{1,0:T(8,128)(2,1)S(1)}, u32[]{:S(2)}, u32[]{:S(2)}) %collective-permute-start.26) | collective-permute-done | bytes 196640 | tf_op jit(solution)/shard_map/ppermute | solution.py:412
  215.0 23.9 %encoder.1 = (bf16[128,768]{1,0:T(8,128)(2,1)}, f32[128,768]{1,0:T(8,128)}, bf16[128,768]{1,0:T(8,128)(2,1)}, bf16[128,768]{1,0:T(8,128)(2,1)}, bf16[128,768]{1,...) custom-call(s32[1]{0:T(128)} %bitcast.d_ref.flag_ref, ...), custom_call_target="tpu_custom_call" | custom-call | flops 16000000000 | bytes 30000000 | tf_op jit(solution)/shard_map/encoder/pallas_call | solution.py:1229
  246.0 9.2 %encoder_grad.1 = (bf16[4,1168,768]{2,1,0:T(8,128)(2,1)}, bf16[4,1168,768]{2,1,0:T(8,128)(2,1)}) custom-call(s32[1]{0:T(128)} %bitcast.d_ref.flag_ref, bf16[512,768]{1,0:T(8,128)(2,1)} %get-tuple-element.145.embs_ref, bf16[128,768]{1,0:T(8,128)(2,1)} %get-tuple-element.146.gq_ref, bf16[512,768]{1,0:T(8,128)(2,1)} %get-tuple-element.147.gk_ref, ...), custom_call_target="tpu_custom_call" | custom-call | flops 6000000000 | bytes 20000000 | tf_op jit(solution)/shard_map/encoder_grad/pallas_call | solution.py:1257
  265.0 11.7 %collective-permute-done.29 = bf16[128,768]{1,0:T(8,128)(2,1)S(1)} collective-permute-done((bf16[128,768]{1,0:T(8,128)(2,1)S(1)}, bf16[128,768]{1,0:T(8,128)(2,1)S(1)}, u32[]{:S(2)}, u32[]{:S(2)}) %collective-permute-start.29) | collective-permute-done | bytes 196640 | tf_op jit(solution)/shard_map/ppermute | solution.py:412
  297.8 8.1 %highway_back1.1 = (bf16[1024,256]{1,0:T(8,128)(2,1)}, bf16[1024,256]{1,0:T(8,128)(2,1)}, f32[1024,256]{1,0:T(8,128)}, f32[8,512]{1,0:T(8,128)}, f32[4,1024,256]{2,1,0:T(8,128)}, /*index=5*/bf16[4,1024,256]{2,1,0:T(8,128)(2,1)}) custom-call(s32[1]{0:T(128)} %bitcast.d_ref.flag_ref, f32[1024,256]{1,0:T(8,128)} %get-tuple-element.135.dh_ref, ...), custom_call_target="tpu_custom_call" | custom-call | flops 2147483648 | bytes 20000000 | tf_op jit(solution)/shard_map/highway_back1/pallas_call | solution.py:726
  323.9 6.6 fusion.3
  330.4 16.4 %collective-permute-done.42 = bf16[1024,256]{1,0:T(8,128)(2,1)S(1)} collective-permute-done((bf16[1024,256]{1,0:T(8,128)(2,1)}, bf16[1024,256]{1,0:T(8,128)(2,1)S(1)}, u32[]{:S(2)}, u32[]{:S(2)}) %collective-permute-start.42) | collective-permute-done | bytes 524320 | tf_op jit(solution)/shard_map/ppermute | solution.py:412
  349.6 8.0 %highway_back0.1 = (bf16[1024,256]{1,0:T(8,128)(2,1)}, bf16[1024,256]{1,0:T(8,128)(2,1)}, f32[1024,256]{1,0:T(8,128)}, f32[8,512]{1,0:T(8,128)}, f32[4,1024,256]{2,1,0:T(8,128)}, /*index=5*/bf16[4,1024,256]{2,1,0:T(8,128)(2,1)}) custom-call(s32[1]{0:T(128)} %bitcast.d_ref.flag_ref, f32[1024,256]{1,0:T(8,128)} %add_add_fusion.1.dh_ref, ...), custom_call_target="tpu_custom_call" | custom-call | flops 2147483648 | bytes 20000000 | tf_op jit(solution)/shard_map/highway_back0/pallas_call | solution.py:726
  378.9 31.8 %collective-permute-done.46 = bf16[1024,256]{1,0:T(8,128)(2,1)} collective-permute-done((bf16[1024,256]{1,0:T(8,128)(2,1)}, bf16[1024,256]{1,0:T(8,128)(2,1)}, u32[]{:S(2)}, u32[]{:S(2)}) %collective-permute-start.46) | collective-permute-done | bytes 524320 | tf_op jit(solution)/shard_map/ppermute | solution.py:412
  410.8 12.5 %collective-permute-done.45 = bf16[1024,256]{1,0:T(8,128)(2,1)} collective-permute-done((bf16[1024,256]{1,0:T(8,128)(2,1)}, bf16[1024,256]{1,0:T(8,128)(2,1)}, u32[]{:S(2)}, u32[]{:S(2)}) %collective-permute-start.45) | collective-permute-done | bytes 524320 | tf_op jit(solution)/shard_map/ppermute | solution.py:412
  431.9 12.5 %char_back.1 = (bf16[1024,256]{1,0:T(8,128)(2,1)}, f32[4,128,896]{2,1,0:T(8,128)}, bf16[4,128,896]{2,1,0:T(8,128)(2,1)}) custom-call(s32[1]{0:T(128)} %bitcast.d_ref.flag_ref, f32[1024,256]{1,0:T(8,128)} %get-tuple-element.117.refs_11_.h_ref, s32[1024,256]{1,0:T(8,128)} %get-tuple-element.130.at_ref, f32[1024,256]{1,0:T(8,128)} %add_add_fusion.dh_ref, ...), custom_call_target="tpu_custom_call" | custom-call | flops 8000000000 | bytes 6889472 | tf_op jit(solution)/shard_map/char_back/pallas_call | solution.py:486
  454.9 9.9 %conv_grad.1 = f32[120,256]{1,0:T(8,128)} custom-call(s32[1]{0:T(128)} %bitcast.d_ref.flag_ref, bf16[1024,1024]{1,0:T(8,128)(2,1)} %get-tuple-element.129.x_ref, s32[1024,256]{1,0:T(8,128)} %get-tuple-element.130.at_ref, bf16[1024,256]{1,0:T(8,128)(2,1)} %get-tuple-element.175.gp_ref), custom_call_target="tpu_custom_call" | custom-call | flops 8000000000 | bytes 3792896 | tf_op jit(solution)/shard_map/conv_grad/pallas_call | solution.py:486
  468.3 19.3 %collective-permute-done.50 = bf16[1168,768]{1,0:T(8,128)(2,1)} collective-permute-done((bf16[1168,768]{1,0:T(8,128)(2,1)}, bf16[1168,768]{1,0:T(8,128)(2,1)}, u32[]{:S(2)}, u32[]{:S(2)}) %collective-permute-start.50) | collective-permute-done | bytes 1794080 | tf_op jit(solution)/shard_map/ppermute | solution.py:412
  507.0 15.2 %collective-permute-done.54 = f32[168,256]{1,0:T(8,128)S(1)} collective-permute-done((f32[168,256]{1,0:T(8,128)S(1)}, f32[168,256]{1,0:T(8,128)S(1)}, u32[]{:S(2)}, u32[]{:S(2)}) %collective-permute-start.54) | collective-permute-done | bytes 172064 | tf_op jit(solution)/shard_map/ppermute | solution.py:412
  545.0 17.0 %collective-permute-done.66 = bf16[544,128]{1,0:T(8,128)(2,1)S(1)} collective-permute-done((bf16[544,128]{1,0:T(8,128)(2,1)S(1)}, bf16[544,128]{1,0:T(8,128)(2,1)S(1)}, u32[]{:S(2)}, u32[]{:S(2)}) %collective-permute-start.66) | collective-permute-done | bytes 139296 | tf_op jit(solution)/shard_map/ppermute | solution.py:454
  579.2 48.8 %collective-permute-done.68 = bf16[544,128]{1,0:T(8,128)(2,1)} collective-permute-done((bf16[544,128]{1,0:T(8,128)(2,1)S(1)}, bf16[544,128]{1,0:T(8,128)(2,1)}, u32[]{:S(2)}, u32[]{:S(2)}) %collective-permute-start.68) | collective-permute-done | bytes 139296 | tf_op jit(solution)/shard_map/ppermute | solution.py:454
  645.5 23.5 %collective-permute-done.65 = bf16[256,768]{1,0:T(8,128)(2,1)} collective-permute-done((bf16[256,768]{1,0:T(8,128)(2,1)S(1)}, bf16[256,768]{1,0:T(8,128)(2,1)}, u32[]{:S(2)}, u32[]{:S(2)}) %collective-permute-start.65) | collective-permute-done | bytes 393248 | tf_op jit(solution)/shard_map/ppermute | solution.py:454
  670.9 10.8 %collective-permute-done.74 = bf16[400,768]{1,0:T(8,128)(2,1)S(1)} collective-permute-done((bf16[400,768]{1,0:T(8,128)(2,1)S(1)}, bf16[400,768]{1,0:T(8,128)(2,1)S(1)}, u32[]{:S(2)}, u32[]{:S(2)}) %collective-permute-start.74) | collective-permute-done | bytes 614432 | tf_op jit(solution)/shard_map/ppermute | solution.py:454
  (347 shorter events, 277.0 us)
Async XLA Ops:
  27.6 53.0 %all-to-all-start = ((bf16[8,2,256,256]{3,2,1,0:T(8,128)(2,1)}), bf16[8,2,256,256]{3,2,1,0:T(8,128)(2,1)S(1)}, u32[]{:S(2)}, u32[]{:S(2)}) async-start(bf16[8,2,256,256]{3,2,1,0:T(8,128)(2,1)} %get-tuple-element.113), calls=%async_computation | async-start | bytes 4194304 | tf_op jit(solution)/shard_map/all_to_all | solution.py:1328
  32.0 182.3 %all-gather.7.cloned.1.call-start = ((), (), s32[]{:S(2)}) async-start(), calls=%async_computation.8 | async-start | bytes 15925248 | tf_op jit(solution)/shard_map/all_gather | solution.py:1367
  84.3 70.8 %all-to-all-start.1 = ((bf16[8,2,256,256]{3,2,1,0:T(8,128)(2,1)}), bf16[8,2,256,256]{3,2,1,0:T(8,128)(2,1)S(1)}, u32[]{:S(2)}, u32[]{:S(2)}) async-start(bf16[8,2,256,256]{3,2,1,0:T(8,128)(2,1)} %get-tuple-element.120), calls=%async_computation.1 | async-start | bytes 4194304 | tf_op jit(solution)/shard_map/all_to_all | solution.py:1365
  87.9 287.5 %reduce-scatter.3.cloned.1.call-start = ((), (), s32[]{:S(2)}) async-start(), calls=%async_computation.6 | async-start | bytes 2621440 | tf_op jit(solution)/shard_map/reduce_scatter | solution.py:1463
  95.7 57.6 %collective-permute-start.17 = (bf16[1024,256]{1,0:T(8,128)(2,1)}, bf16[1024,256]{1,0:T(8,128)(2,1)S(1)}, u32[]{:S(2)}, u32[]{:S(2)}) collective-permute-start(bf16[1024,256]{1,0:T(8,128)(2,1)} %get-tuple-element.118.refs_0_), channel_id=1, source_target_pairs={{0,16},{4,20},{8,24},{12,28},{16,0},{20,4},{24,8},{28,12},{1,17},{... | collective-permute-start | bytes 1572872 | tf_op jit(solution)/shard_map/ppermute | solution.py:412
  97.7 55.6 %collective-permute-start.19 = (bf16[1024,256]{1,0:T(8,128)(2,1)}, bf16[1024,256]{1,0:T(8,128)(2,1)S(1)}, u32[]{:S(2)}, u32[]{:S(2)}) collective-permute-start(bf16[1024,256]{1,0:T(8,128)(2,1)} %get-tuple-element.118.refs_0_), channel_id=1, source_target_pairs={{0,24},{4,28},{8,16},{12,20},{16,8},{20,12},{24,0},{28,4},{1,25},{... | collective-permute-start | bytes 1572872 | tf_op jit(solution)/shard_map/ppermute | solution.py:412
  99.1 55.9 %collective-permute-start.15 = (bf16[1024,256]{1,0:T(8,128)(2,1)}, bf16[1024,256]{1,0:T(8,128)(2,1)}, u32[]{:S(2)}, u32[]{:S(2)}) collective-permute-start(bf16[1024,256]{1,0:T(8,128)(2,1)} %get-tuple-element.118.refs_0_), channel_id=1, source_target_pairs={{0,8},{4,12},{8,0},{12,4},{16,24},{20,28},{24,16},{28,20},{1,9},{5... | collective-permute-start | bytes 1572872 | tf_op jit(solution)/shard_map/ppermute | solution.py:412
  99.3 55.8 %collective-permute-start.14 = (bf16[1024,256]{1,0:T(8,128)(2,1)}, bf16[1024,256]{1,0:T(8,128)(2,1)}, u32[]{:S(2)}, u32[]{:S(2)}) collective-permute-start(bf16[1024,256]{1,0:T(8,128)(2,1)} %get-tuple-element.118.refs_0_), channel_id=1, source_target_pairs={{0,4},{4,0},{8,12},{12,8},{16,20},{20,16},{24,28},{28,24},{1,5},{5... | collective-permute-start | bytes 1572872 | tf_op jit(solution)/shard_map/ppermute | solution.py:412
  255.2 68.7 %collective-permute-start.39 = (bf16[4,1168,768]{2,1,0:T(8,128)(2,1)}, bf16[4,1168,768]{2,1,0:T(8,128)(2,1)}, u32[]{:S(2)}, u32[]{:S(2)}) collective-permute-start(bf16[4,1168,768]{2,1,0:T(8,128)(2,1)} %get-tuple-element.157), channel_id=1, source_target_pairs={{0,4},{4,0},{8,12},{12,8},{16,20},{20,16},{24,28},{28,24},{1,5},{5... | collective-permute-start | bytes 21528584 | tf_op jit(solution)/shard_map/ppermute | solution.py:412
  320.2 144.5 %reduce-scatter.5.cloned.1.call-start = ((), (), s32[]{:S(2)}) async-start(), calls=%async_computation.7 | async-start | bytes 2621440 | tf_op jit(solution)/shard_map/reduce_scatter | solution.py:1463
  357.6 68.5 %collective-permute-start.47 = (bf16[1168,768]{1,0:T(8,128)(2,1)S(1)}, bf16[1168,768]{1,0:T(8,128)(2,1)}, u32[]{:S(2)}, u32[]{:S(2)}) collective-permute-start(bf16[1168,768]{1,0:T(8,128)(2,1)S(1)} %get-tuple-element.278), channel_id=1, source_target_pairs={{0,8},{4,12},{8,0},{12,4},{16,24},{20,28},{24,16},{28,20},{1,9},{5... | collective-permute-start | bytes 5382152 | tf_op jit(solution)/shard_map/ppermute | solution.py:412
  358.1 68.1 %collective-permute-start.48 = (bf16[1168,768]{1,0:T(8,128)(2,1)}, bf16[1168,768]{1,0:T(8,128)(2,1)}, u32[]{:S(2)}, u32[]{:S(2)}) collective-permute-start(bf16[1168,768]{1,0:T(8,128)(2,1)} %get-tuple-element.277), channel_id=1, source_target_pairs={{0,16},{4,20},{8,24},{12,28},{16,0},{20,4},{24,8},{28,12},{1,17},{... | collective-permute-start | bytes 5382152 | tf_op jit(solution)/shard_map/ppermute | solution.py:412
  372.5 50.8 %collective-permute-start.45 = (bf16[1024,256]{1,0:T(8,128)(2,1)}, bf16[1024,256]{1,0:T(8,128)(2,1)}, u32[]{:S(2)}, u32[]{:S(2)}) collective-permute-start(bf16[1024,256]{1,0:T(8,128)(2,1)} %get-tuple-element.281), channel_id=1, source_target_pairs={{0,16},{4,20},{8,24},{12,28},{16,0},{20,4},{24,8},{28,12},{1,17},{... | collective-permute-start | bytes 1572872 | tf_op jit(solution)/shard_map/ppermute | solution.py:412
  373.7 49.5 %collective-permute-start.44 = (bf16[1024,256]{1,0:T(8,128)(2,1)}, bf16[1024,256]{1,0:T(8,128)(2,1)}, u32[]{:S(2)}, u32[]{:S(2)}) collective-permute-start(bf16[1024,256]{1,0:T(8,128)(2,1)} %get-tuple-element.279), channel_id=1, source_target_pairs={{0,8},{4,12},{8,0},{12,4},{16,24},{20,28},{24,16},{28,20},{1,9},{5... | collective-permute-start | bytes 1572872 | tf_op jit(solution)/shard_map/ppermute | solution.py:412
  375.4 56.5 %all-to-all-start.2 = ((bf16[8,64,512]{2,1,0:T(8,128)(2,1)}), bf16[8,64,512]{2,1,0:T(8,128)(2,1)S(1)}, u32[]{:S(2)}, u32[]{:S(2)}) async-start(bf16[8,64,512]{2,1,0:T(8,128)(2,1)} %bitcast.90), calls=%async_computation.3 | async-start | bytes 1048576 | tf_op jit(solution)/shard_map/all_to_all | solution.py:1464
  378.9 193.1 %all-gather.11.cloned.1.call-start = ((), (), s32[]{:S(2)}) async-start(), calls=%async_computation.10 | async-start | bytes 2621440 | tf_op jit(solution)/shard_map/all_gather | solution.py:1465
  468.3 224.8 %all-gather.9.cloned.1.call-start = ((), (), s32[]{:S(2)}) async-start(), calls=%async_computation.9 | async-start | bytes 2621440 | tf_op jit(solution)/shard_map/all_gather | solution.py:1465
  543.5 84.5 %collective-permute-start.64 = (bf16[256,768]{1,0:T(8,128)(2,1)S(1)}, bf16[256,768]{1,0:T(8,128)(2,1)}, u32[]{:S(2)}, u32[]{:S(2)}) collective-permute-start(bf16[256,768]{1,0:T(8,128)(2,1)S(1)} %add.318), channel_id=1, source_target_pairs={{1,2},{2,1},{5,6},{6,5},{9,10},{10,9},{13,14},{14,13},{17,18},{18,... | collective-permute-start | bytes 1179656 | tf_op jit(solution)/shard_map/ppermute | solution.py:454
  564.0 67.9 %collective-permute-start.73 = (bf16[400,768]{1,0:T(8,128)(2,1)}, bf16[400,768]{1,0:T(8,128)(2,1)S(1)}, u32[]{:S(2)}, u32[]{:S(2)}) collective-permute-start(bf16[400,768]{1,0:T(8,128)(2,1)} %slice_add_fusion), channel_id=1, source_target_pairs={{1,2},{2,1},{5,6},{6,5},{9,10},{10,9},{13,14},{14,13},{17,18},{18,... | collective-permute-start | bytes 1843208 | tf_op jit(solution)/shard_map/ppermute | solution.py:454
  570.6 57.4 %collective-permute-start.68 = (bf16[544,128]{1,0:T(8,128)(2,1)S(1)}, bf16[544,128]{1,0:T(8,128)(2,1)}, u32[]{:S(2)}, u32[]{:S(2)}) collective-permute-start(bf16[544,128]{1,0:T(8,128)(2,1)S(1)} %add.323), channel_id=1, source_target_pairs={{1,0},{2,3},{5,4},{6,7},{9,8},{10,11},{13,12},{14,15},{17,16},{18,... | collective-permute-start | bytes 417800 | tf_op jit(solution)/shard_map/ppermute | solution.py:454
  577.5 56.7 %collective-permute-start.56 = (f32[168,256]{1,0:T(8,128)}, f32[168,256]{1,0:T(8,128)S(1)}, u32[]{:S(2)}, u32[]{:S(2)}) collective-permute-start(f32[168,256]{1,0:T(8,128)} %add.316.refs_0_), channel_id=1, source_target_pairs={{0,4},{4,0},{8,12},{12,8},{16,20},{20,16},{24,28},{28,24},{1,5},{5... | collective-permute-start | bytes 516104 | tf_op jit(solution)/shard_map/ppermute | solution.py:412
  577.6 53.8 %collective-permute-start.61 = (f32[168,256]{1,0:T(8,128)}, f32[168,256]{1,0:T(8,128)}, u32[]{:S(2)}, u32[]{:S(2)}) collective-permute-start(f32[168,256]{1,0:T(8,128)} %add.316.refs_0_), channel_id=1, source_target_pairs={{0,24},{4,28},{8,16},{12,20},{16,8},{20,12},{24,0},{28,4},{1,25},{... | collective-permute-start | bytes 516104 | tf_op jit(solution)/shard_map/ppermute | solution.py:412
  628.0 54.6 %collective-permute-start.71 = (bf16[768,768]{1,0:T(8,128)(2,1)S(1)}, bf16[768,768]{1,0:T(8,128)(2,1)}, u32[]{:S(2)}, u32[]{:S(2)}) collective-permute-start(bf16[768,768]{1,0:T(8,128)(2,1)S(1)} %add.325), channel_id=1, source_target_pairs={{1,0},{2,3},{5,4},{6,7},{9,8},{10,11},{13,12},{14,15},{17,16},{18,... | collective-permute-start | bytes 3538952 | tf_op jit(solution)/shard_map/ppermute | solution.py:454
  635.5 46.2 %collective-permute-start.74 = (bf16[400,768]{1,0:T(8,128)(2,1)S(1)}, bf16[400,768]{1,0:T(8,128)(2,1)S(1)}, u32[]{:S(2)}, u32[]{:S(2)}) collective-permute-start(bf16[400,768]{1,0:T(8,128)(2,1)S(1)} %add.327), channel_id=1, source_target_pairs={{1,0},{2,3},{5,4},{6,7},{9,8},{10,11},{13,12},{14,15},{17,16},{18,... | collective-permute-start | bytes 1843208 | tf_op jit(solution)/shard_map/ppermute | solution.py:454
  (99 other events, 1229.3 us)
Sparse Core Ops, SparseCore 0:
  84.3 126.2 all-gather.6
  320.4 43.2 reduce-scatter.2
  371.9 42.1 reduce-scatter.4
  448.0 46.3 all-gather.10
  538.7 63.3 all-gather.8

commit v3 on v2

--- a/solution.py
+++ b/solution.py
@@ -746,15 +746,20 @@
 
 def highway_grad_body(d_ref, *refs):
     blocks = refs[:PLANE]
-    ga_ref, gb_ref, out_ref = refs[PLANE:]
+    ga_ref, gb_ref = refs[PLANE : PLANE + 2]
+    outs = refs[PLANE + 2 :]
     d = d_ref[0]
     filters = ga_ref.shape[1]
     for k in range(PLANE):
         for side, grad_ref in enumerate((ga_ref, gb_ref)):
+            cols = slice(side * filters, (side + 1) * filters)
             piece = tn(blocks[k][...], grad_ref[...]).astype(bf16)
-            out_ref[:, d ^ k, :, side * filters : (side + 1) * filters] = piece.reshape(
-                DEPTH, filters // DEPTH, filters
-            )
+            if len(outs) == 1:
+                outs[0][:, d ^ k, :, cols] = piece.reshape(DEPTH, filters // DEPTH, filters)
+            else:
+                rows = filters // len(outs)
+                for i, out_ref in enumerate(outs):
+                    out_ref[d ^ k, :, cols] = piece[i * rows : (i + 1) * rows]
 
 
 def spread_groups(char_len, filters, grad, at, spread_ref, group):
@@ -882,29 +887,34 @@
             at += rows
 
 
-def finish_highway_body(blocks_ref, *refs):
+def finish_highway_body(count, *refs):
     out_ref = refs[-1]
-    own = out_ref.shape[1]
     half = out_ref.shape[2] // 2
-    for j in range(PLANE):
-        for side in range(2):
-            at = slice(j * own + side * half, (j + 1) * own + side * half)
-            cols = slice(side * own, (side + 1) * own)
-            out_ref[0, :, at] = blocks_ref[:, j, :, cols].reshape(own, own).astype(f32)
-
-
-def finish_highway(layer, layers, blocks, previous):
-    own = blocks.shape[3] // 2
+    own = half // PLANE
+    low = 0
+    for ref in refs[:count]:
+        rows = out_ref.shape[1] // count
+        for j in range(PLANE):
+            for side in range(2):
+                at = slice(j * own + side * half, (j + 1) * own + side * half)
+                cols = slice(side * own, (side + 1) * own)
+                piece = ref[j, :, cols] if len(ref.shape) == 3 else ref[:, j, :, cols]
+                out_ref[0, low : low + rows, at] = piece.reshape(rows, own).astype(f32)
+        low += rows
+
+
+def finish_highway(layer, layers, pieces, previous):
+    own = pieces[0].shape[-1] // 2
     width = 2 * PLANE * own
-    operands = [blocks]
-    specs = [pl.BlockSpec(blocks.shape, lambda i: (0, 0, 0, 0))]
+    operands = list(pieces)
+    specs = [pl.BlockSpec(x.shape, lambda i, n=x.ndim: (0,) * n) for x in pieces]
     aliases = {}
     if previous is not None:
+        aliases = {len(operands): 0}
         operands.append(previous)
         specs.append(pl.BlockSpec(memory_space=pl.ANY))
-        aliases = {1: 0}
     return pl.pallas_call(
-        finish_highway_body,
+        functools.partial(finish_highway_body, len(pieces)),
         grid=(1,),
         out_shape=jax.ShapeDtypeStruct((layers, own, width), f32),
         in_specs=specs,
@@ -1150,12 +1160,10 @@
     gup_ref,
     gdown_ref,
     stats_ref,
-    keep_hbm,
-    send_hbm,
+    out_hbm,
     out_ref,
     sems,
 ):
-    d = flag_ref[0]
     words, dim = gq_ref.shape
     part = dim // PLANE
     wide = act_ref.shape[1] // PLANE
@@ -1166,15 +1174,11 @@
         out_ref[:, low:high, :] = value.reshape(PLANE, high - low, dim)
 
     def send(low, high):
-        for i in range(PLANE // 2):
-            for odd, hbm in ((1, send_hbm), (0, keep_hbm)):
-                copy = pltpu.make_async_copy(
-                    out_ref.at[d ^ odd ^ (2 * i), low:high, :],
-                    hbm.at[i, low:high, :],
-                    sems.at[len(pieces)],
-                )
-                copy.start()
-                pieces.append(copy)
+        copy = pltpu.make_async_copy(
+            out_ref.at[:, low:high, :], out_hbm.at[:, low:high, :], sems.at[len(pieces)]
+        )
+        copy.start()
+        pieces.append(copy)
 
     low = (4 + in_parts) * part
     per = dim // wide
@@ -1256,15 +1260,15 @@
     rows = (4 + in_parts) * part + ff_dim // PLANE + 16
     grads = pl.pallas_call(
         encoder_grad_body,
-        out_shape=[jax.ShapeDtypeStruct((PLANE // 2, rows, dim), bf16)] * 2,
+        out_shape=jax.ShapeDtypeStruct((PLANE, rows, dim), bf16),
         in_specs=[SMEM_SPEC] + [vmem] * 11,
-        out_specs=[hbm] * 2,
-        scratch_shapes=[VMEM((PLANE, rows, dim), bf16), pltpu.SemaphoreType.DMA((3 * PLANE,))],
+        out_specs=hbm,
+        scratch_shapes=[VMEM((PLANE, rows, dim), bf16), pltpu.SemaphoreType.DMA((3,))],
         name="encoder_grad",
         cost_estimate=cost(6e9, 20e6),
         compiler_params=pltpu.CompilerParams(vmem_limit_bytes=58 * 1024 * 1024),
     )(flag, *saved)
-    return result, d_embedded, grads
+    return result, tie(d_embedded, grads), grads
 
 
 def round_up(value, multiple):
@@ -1411,7 +1415,7 @@
         )
 
     key_segs, key_pads = by_offset(segment_ids), by_offset(pad_mask)
-    result, d_embedded, (enc_keep, enc_send) = encoder(
+    result, d_embedded, enc_grads = encoder(
         dvec,
         embedded,
         others,
@@ -1422,7 +1426,7 @@
         cotangent.reshape(words, model_dim),
         gathered,
     )
-    enc_arrived = plane_swap(enc_send, CORE_PARTNER)
+    enc_slice = lax.psum_scatter(enc_grads, "dp", scatter_dimension=0, tiled=True)[0]
     d_summed = normalize_back(d_embedded, normal0, scale0, small_full[5])
     grad_proj = jnp.concatenate(
         [
@@ -1442,8 +1446,16 @@
         (*gp_blocks, proj_weight, hidden_b),
         name="unproject",
     )
-    hw_sums, gate_parts, quarters = {}, {}, {}
-    enc_parts = None
+    top_own = lax.dynamic_slice_in_dim(top_sums, d * part, part, 1)
+    top_own = jnp.pad(top_own, ((0, 0), (0, 128 - part)))
+    top_all = lax.dynamic_update_slice_in_dim(
+        jnp.zeros((seq_len + 32, 128), f32), top_own[words:], seq_len, 0
+    )
+    top_all = lax.dynamic_update_slice_in_dim(top_all, top_own[:words], z * words, 0).astype(bf16)
+    cut = (4 + in_parts) * part
+    gate_parts = {}
+    middle = (z == 1) | (z == 2)
+    chain = None
     for layer in reversed(range(depth)):
         blocks, opened, ra, hidden = saved[layer]
         ga, gb, d_carry, sums, keep, send = highway_back(
@@ -1451,31 +1463,47 @@
         )
         parts = plane_parts(keep, send)
         gate_parts[layer] = jnp.sum(sums, axis=0).reshape(2, own)
-        (cols_grad,) = call(
+        after = []
+        if layer == 0:
+            enc_slice = tie(enc_slice, parts[1])
+            chain[1] = chain[1] + tie(steps[1], parts[1])
+            steps[1] = line_step(chain[1], 1)
+            after = [chain[1]]
+        shapes = (
+            [((DEPTH, PLANE, own // DEPTH, 2 * own), bf16)]
+            if layer == 0
+            else [((PLANE, own // 2, 2 * own), bf16)] * 2
+        )
+        grads = call(
             highway_grad_body,
-            [((DEPTH, PLANE, own // DEPTH, 2 * own), bf16)],
+            shapes,
             dvec,
-            (*blocks, tie(ga, parts[1]), gb),
+            (*blocks, tie(ga, parts[1], *after), gb),
             name=f"highway_grad{layer}",
             flops=2 * all_words * filters * 2 * own,
         )
-        after = [cols_grad]
-        quarter = lax.psum_scatter(cols_grad, "seq", scatter_dimension=0, tiled=False)
-        quarters[layer] = lax.all_to_all(quarter, "dp", 0, 0)
-        hw_sums[layer] = lax.all_gather(quarters[layer], "seq", axis=0, tiled=False)
-        if enc_parts is None:
-            arrived = tie(enc_arrived, parts[1], cols_grad)
-            enc_parts = [enc_keep[0].astype(f32) + arrived[0].astype(f32)] + [
-                (enc_keep[i].astype(f32) + arrived[i].astype(f32)).astype(bf16)
-                for i in range(1, half)
-            ]
-            enc_rest = [plane_swap(enc_parts[i], 2 * i) for i in range(1, half)]
-            after.append(enc_parts[1])
+        top_all = tie(top_all, parts[1])
+        top_all = top_all + swap(top_all, "seq", DEPTH, 1 if layer else 2)
+        if layer == 0:
+            quarter = lax.psum_scatter(
+                tie(grads[0], enc_slice), "seq", scatter_dimension=0, tiled=False
+            )
+            quarter = lax.all_to_all(quarter, "dp", 0, 0)
+            lowest = lax.all_gather(quarter, "seq", axis=0, tiled=False)
+            chain[0] = chain[0] + tie(steps[0], grads[0])
+            steps[0] = line_step(chain[0], 2)
+            after = [grads[0], top_all, enc_slice, chain[0]]
+        else:
+            chain = list(grads)
+            steps = [line_step(value, 0) for value in chain]
+            chain[0] = chain[0] + tie(steps[0], parts[1])
+            steps[0] = line_step(chain[0], 1)
+            after = [*grads, top_all, chain[0]]
         d_hidden = d_carry + plane_total(parts, after)
-    enc_sum = enc_parts[0]
-    for piece in enc_rest[:-1]:
-        enc_sum = enc_sum + tie(piece, d_hidden).astype(f32)
-    d_hidden = tie(d_hidden, enc_sum, *[quarters[other] for other in range(1, depth)])
+    lines = [enc_slice[:cut], jnp.concatenate([enc_slice[cut:], proj_grad], axis=0)]
+    moved = [line_step(value, 0) for value in lines]
+    d_hidden = tie(d_hidden, *lines)
+
     grad_pooled, keep, send = call(
         functools.partial(char_back_body, char_len, words),
         [
@@ -1494,7 +1522,9 @@
         flops=8e9,
     )
     parts = plane_parts(keep, send)
-    grad_pooled = tie(grad_pooled, parts[1])
+    chain[1] = chain[1] + tie(steps[1], parts[1])
+    steps[1] = line_step(chain[1], 2)
+    grad_pooled = tie(grad_pooled, parts[1], chain[1])
     (conv_part,) = call(
         functools.partial(conv_grad_body, char_len),
         [((tap_count * char_dim + 8, own), f32)],
@@ -1504,16 +1534,9 @@
         name="conv_grad",
         flops=8e9,
     )
-    enc_slice = (tie(enc_sum, conv_part) + enc_rest[-1].astype(f32)).astype(bf16)
-    top_own = lax.dynamic_slice_in_dim(top_sums, d * part, part, 1).astype(bf16)
-    top_own = jnp.pad(top_own, ((0, 0), (0, 128 - part)))
-    top_all = lax.dynamic_update_slice_in_dim(
-        jnp.zeros((seq_len, 128), bf16), top_own[:words], z * words, 0
-    )
-    cut = (4 + in_parts) * part
-    lines = [enc_slice[:cut], enc_slice[cut:], proj_grad, jnp.concatenate([top_all, top_own[words:]], axis=0)]
-    moved = [line_step(value, 0) for value in lines]
-    char_grads = tie(plane_total(parts, (conv_part, enc_slice)), quarters[0])
+    lines = [value + tie(piece, conv_part) for value, piece in zip(lines, moved)]
+    moved = [line_step(value, 1) for value in lines]
+    char_grads = plane_total(parts, (conv_part, *lines))
     fold_rows = round_up(-(-chars // GROUP), 8)
     (table_part,) = call(
         functools.partial(table_grad_body, char_len),
@@ -1534,8 +1557,6 @@
     )
     ends = ends + swap(ends, "seq", DEPTH, 1)
     ends = ends + swap(ends, "seq", DEPTH, 2)
-    lines = [value + tie(piece, ends) for value, piece in zip(lines, moved)]
-    moved = [line_step(value, 1) for value in lines]
     end_blocks = plane_gather(ends)
     conv_rows = tap_count * char_dim
     conv_total, conv_bias_total, gate_sums, table_total = call(
@@ -1561,11 +1582,9 @@
 
     lines = [value + tie(piece, ends) for value, piece in zip(lines, moved)]
     moved = [line_step(value, 2) for value in lines]
-    middle = (z == 1) | (z == 2)
-    *enc_total, proj_total, top_total = (
-        jnp.where(middle, value, piece) for value, piece in zip(lines, moved)
-    )
-    top_total = top_total[:, :part].astype(f32)
+    enc_total = [jnp.where(middle, value, piece) for value, piece in zip(lines, moved)]
+    proj_total = enc_total[1][-own:]
+    top_total = top_all[:, :part].astype(f32)
     pos_total = top_total[:seq_len]
     gain0, shift0, bias0 = top_total[seq_len], top_total[seq_len + 1], top_total[seq_len + 16]
     proj_total = proj_total.astype(f32)
@@ -1590,11 +1609,16 @@
         small_total[11 : 11 + in_parts].reshape(-1), d * (ff_dim // PLANE), ff_dim // PLANE, 0
     )
 
-    hw_total, hw_bias_totals = None, [None] * depth
-    for layer in reversed(range(depth)):
-        hw_total = finish_highway(layer, depth, hw_sums[layer], hw_total)
+    chain = [
+        jnp.where(middle, value, tie(piece, table_part)) for value, piece in zip(chain, steps)
+    ]
+    pieces = [lax.all_to_all(value, "dp", 0, 0) for value in chain]
+    hw_total = finish_highway(1, depth, pieces, None)
+    hw_total = finish_highway(0, depth, [lowest], hw_total)
+    hw_bias_totals = []
+    for layer in range(depth):
         row = gate_sums[2 * layer : 2 * layer + 2].reshape(-1)
-        hw_bias_totals[layer] = lax.dynamic_slice_in_dim(row, d * 2 * own, 2 * own, 0)
+        hw_bias_totals.append(lax.dynamic_slice_in_dim(row, d * 2 * own, 2 * own, 0))
 
     output = result.reshape(1, words, model_dim)
     return (

time: 711 us -> 659 us (0.927)
  waiting for transfers between devices: 364 us -> 304 us
  starting transfers between devices: 96.6 us -> 105 us
    ppermute x12, waiting for transfers between devices: 100 us -> 45.7 us  [line_step(): return lax.ppermute(value, 'seq', LINE_STEPS[step])]
    ppermute x12, starting transfers between devices: 20.6 us -> 31 us  [line_step(): return lax.ppermute(value, 'seq', LINE_STEPS[step])]
    convert_element_type x3 -> x1, other arithmetic: 10.5 us -> 0.02 us  [plane_shards(): top_total = top_all[:, :part].astype(f32)]
    ppermute x63 -> x61, waiting for transfers between devices: 261 us -> 253 us  [swap(): lax.ppermute(value, axis_name, [(at, at ^ offset) for at in range(size)])]
    ppermute x63 -> x61, starting transfers between devices: 60.9 us -> 54.9 us  [swap(): lax.ppermute(value, axis_name, [(at, at ^ offset) for at in range(size)])]
  transfers between devices with their start and end apart: 84 -> 82, of which waited for: 38 -> 35; matrix products, arithmetic and copies ran while one was open for 10% -> 10% of each run, Pallas kernels for 16% -> 17%
where the time goes in v3:
time: 659 us; the launch traced here: 651 us
  waiting for transfers between devices  304 us (46%)
  Pallas kernels  150 us (23%)
  starting transfers between devices  105 us (16%)
  other arithmetic  49.5 us (8%)
  local copies, waits for them, and re-layouts  27.6 us (4%)
  between operations  14.9 us (2%)
    ppermute x61, waiting for transfers between devices, swap(): lax.ppermute(value, axis_name, [(at, at ^ offset) for at in range(size)])  253 us
    pallas_call x11, Pallas kernels, call(): pl.pallas_call(body, out_shape=[jax.ShapeDtypeStruct(s, t) for s, t in ou...  67.5 us
    ppermute x61, starting transfers between devices, swap(): lax.ppermute(value, axis_name, [(at, at ^ offset) for at in range(size)])  54.9 us
    ppermute x12, waiting for transfers between devices, line_step(): return lax.ppermute(value, 'seq', LINE_STEPS[step])  45.7 us
    ppermute x12, starting transfers between devices, line_step(): return lax.ppermute(value, 'seq', LINE_STEPS[step])  31 us
    pallas_call x1, Pallas kernels, encoder(): pl.pallas_call(functools.partial(encoder_body, head_count, in_parts), out...  23.9 us
    pallas_call x2, Pallas kernels, highway_back(): pl.pallas_call(highway_back_body, grid=(4,), out_shape=[jax.ShapeDtypeStr...  16.3 us
    pallas_call x2, Pallas kernels, highway(): pl.pallas_call(functools.partial(highway_body, layer), grid=(4,), out_sha...  16.2 us
  transfers between devices with their start and end apart: 82, of which 35 were waited for; matrix products, arithmetic and copies ran while one was open for 10% of the time, Pallas kernels for 17%

profile of v3, /device:TPU:0, one launch (start us, length us, event | category | flops | bytes accessed | tf_op | source)
XLA Modules:
  0.0 650.7 jit_solution(933278723010123258)
XLA Ops:
  37.6 12.1 %conv.1 = (f32[1024,256]{1,0:T(8,128)}, bf16[1024,256]{1,0:T(8,128)(2,1)}, s32[1024,256]{1,0:T(8,128)}, bf16[1024,1024]{1,0:T(8,128)(2,1)}, f32[16,256]{1,0:T(8,...) custom-call(s32[1]{0:T(128)} %bitcast.d_ref.flag_ref, bf16[160,896]{1,0:T(8,128)(2,1)} %lookup.1.refs_0_, ...), custom_call_target="tpu_custom_call" | custom-call | flops 8000000000 | bytes 7974912 | tf_op jit(solution)/shard_map/conv/pallas_call | solution.py:486
  49.7 7.1 %collective-permute-start.12 = (bf16[1024,256]{1,0:T(8,128)(2,1)}, bf16[1024,256]{1,0:T(8,128)(2,1)S(1)}, u32[]{:S(2)}, u32[]{:S(2)}) collective-permute-start(bf16[1024,256]{1,0:T(8,128)(2,1)} %get-tuple-element.114.refs_0_), channel_id=1, source_target_pairs={{0,24},{4,28},{8,16},{12,20},{16,8},{20,12},{24,0},{28,4},{1,25},{... | collective-permute-start | bytes 1572872 | tf_op jit(solution)/shard_map/ppermute | solution.py:412
  58.1 12.2 %collective-permute-done.12.refs_6_ = bf16[1024,256]{1,0:T(8,128)(2,1)S(1)} collective-permute-done((bf16[1024,256]{1,0:T(8,128)(2,1)}, bf16[1024,256]{1,0:T(8,128)(2,1)S(1)}, u32[]{:S(2)}, u32[]{:S(2)}) %collective-permute-start.12) | collective-permute-done | bytes 524320 | tf_op jit(solution)/shard_map/ppermute | solution.py:412
  70.4 10.7 %collective-permute-done.10.refs_4_ = bf16[1024,256]{1,0:T(8,128)(2,1)S(1)} collective-permute-done((bf16[1024,256]{1,0:T(8,128)(2,1)}, bf16[1024,256]{1,0:T(8,128)(2,1)S(1)}, u32[]{:S(2)}, u32[]{:S(2)}) %collective-permute-start.10) | collective-permute-done | bytes 524320 | tf_op jit(solution)/shard_map/ppermute | solution.py:412
  88.5 7.7 %highway0.1 = (f32[1024,256]{1,0:T(8,128)}, f32[1024,256]{1,0:T(8,128)}, f32[1024,256]{1,0:T(8,128)}, bf16[1024,256]{1,0:T(8,128)(2,1)}) custom-call(s32[1]{0:T(128)} %bitcast.d_ref.flag_ref, bf16[1024,256]{1,0:T(8,128)(2,1)} %get-tuple-element.114.refs_0_, bf16[1024,256]{1,0:T(8,128)(2,1)} %collective-permute-done.7.refs_1_, ...), custom_call_target="tpu_custom_call" | custom-call | flops 2147483648 | bytes 12000000 | tf_op jit(solution)/shard_map/highway0/pallas_call | solution.py:643
  99.8 45.8 %collective-permute-done.19.refs_6_ = bf16[1024,256]{1,0:T(8,128)(2,1)S(1)} collective-permute-done((bf16[1024,256]{1,0:T(8,128)(2,1)}, bf16[1024,256]{1,0:T(8,128)(2,1)S(1)}, u32[]{:S(2)}, u32[]{:S(2)}) %collective-permute-start.19) | collective-permute-done | bytes 524320 | tf_op jit(solution)/shard_map/ppermute | solution.py:412
  145.7 7.8 %collective-permute-done.17.refs_4_ = bf16[1024,256]{1,0:T(8,128)(2,1)S(1)} collective-permute-done((bf16[1024,256]{1,0:T(8,128)(2,1)}, bf16[1024,256]{1,0:T(8,128)(2,1)S(1)}, u32[]{:S(2)}, u32[]{:S(2)}) %collective-permute-start.17) | collective-permute-done | bytes 524320 | tf_op jit(solution)/shard_map/ppermute | solution.py:412
  157.9 8.5 %highway1.1 = (f32[1024,256]{1,0:T(8,128)}, f32[1024,256]{1,0:T(8,128)}, f32[1024,256]{1,0:T(8,128)}, bf16[1024,256]{1,0:T(8,128)(2,1)}) custom-call(s32[1]{0:T(128)} %bitcast.d_ref.flag_ref, bf16[1024,256]{1,0:T(8,128)(2,1)} %get-tuple-element.120.refs_0_, bf16[1024,256]{1,0:T(8,128)(2,1)} %collective-permute-done.14.refs_1_, ...), custom_call_target="tpu_custom_call" | custom-call | flops 2147483648 | bytes 12000000 | tf_op jit(solution)/shard_map/highway1/pallas_call | solution.py:643
  178.2 7.6 %collective-permute-done.22 = bf16[128,768]{1,0:T(8,128)(2,1)S(1)} collective-permute-done((bf16[128,768]{1,0:T(8,128)(2,1)S(1)}, bf16[128,768]{1,0:T(8,128)(2,1)S(1)}, u32[]{:S(2)}, u32[]{:S(2)}) %collective-permute-start.22) | collective-permute-done | bytes 196640 | tf_op jit(solution)/shard_map/ppermute | solution.py:412
  185.8 8.9 %collective-permute-done.24 = bf16[128,768]{1,0:T(8,128)(2,1)S(1)} collective-permute-done((bf16[128,768]{1,0:T(8,128)(2,1)S(1)}, bf16[128,768]{1,0:T(8,128)(2,1)S(1)}, u32[]{:S(2)}, u32[]{:S(2)}) %collective-permute-start.24) | collective-permute-done | bytes 196640 | tf_op jit(solution)/shard_map/ppermute | solution.py:412
  205.7 10.1 %collective-permute-done.26.e2_ref = bf16[128,768]{1,0:T(8,128)(2,1)S(1)} collective-permute-done((bf16[128,768]{1,0:T(8,128)(2,1)S(1)}, bf16[128,768]{1,0:T(8,128)(2,1)S(1)}, u32[]{:S(2)}, u32[]{:S(2)}) %collective-permute-start.26) | collective-permute-done | bytes 196640 | tf_op jit(solution)/shard_map/ppermute | solution.py:412
  216.6 23.9 %encoder.1 = (bf16[128,768]{1,0:T(8,128)(2,1)}, f32[128,768]{1,0:T(8,128)}, bf16[128,768]{1,0:T(8,128)(2,1)}, bf16[128,768]{1,0:T(8,128)(2,1)}, bf16[128,768]{1,...) custom-call(s32[1]{0:T(128)} %bitcast.d_ref.flag_ref, ...), custom_call_target="tpu_custom_call" | custom-call | flops 16000000000 | bytes 30000000 | tf_op jit(solution)/shard_map/encoder/pallas_call | solution.py:1233
  246.7 9.1 %encoder_grad.1 = bf16[8,1168,768]{2,1,0:T(8,128)(2,1)} custom-call(s32[1]{0:T(128)} %bitcast.d_ref.flag_ref, bf16[512,768]{1,0:T(8,128)(2,1)} %get-tuple-element.138.embs_ref, bf16[128,768]{1,0:T(8,128)(2,1)} %get-tuple-element.139.gq_ref, bf16[512,768]{1,0:T(8,128)(2,1)} %get-tuple-element.140.gk_ref, bf16[512,768]{1,0:T(8,128)(2,1)} %get-tuple-element.141.gv_ref, ...), custom_call_target="tpu_custom_call" | custom-call | flops 6000000000 | bytes 20000000 | tf_op jit(solution)/shard_map/encoder_grad/pallas_call | solution.py:1261
  259.5 11.7 %collective-permute-done.29 = bf16[128,768]{1,0:T(8,128)(2,1)S(1)} collective-permute-done((bf16[128,768]{1,0:T(8,128)(2,1)S(1)}, bf16[128,768]{1,0:T(8,128)(2,1)S(1)}, u32[]{:S(2)}, u32[]{:S(2)}) %collective-permute-start.29) | collective-permute-done | bytes 196640 | tf_op jit(solution)/shard_map/ppermute | solution.py:412
  292.1 8.2 %highway_back1.1 = (bf16[1024,256]{1,0:T(8,128)(2,1)}, bf16[1024,256]{1,0:T(8,128)(2,1)}, f32[1024,256]{1,0:T(8,128)}, f32[8,512]{1,0:T(8,128)}, f32[4,1024,256]{2,1,0:T(8,128)}, /*index=5*/bf16[4,1024,256]{2,1,0:T(8,128)(2,1)}) custom-call(s32[1]{0:T(128)} %bitcast.d_ref.flag_ref, f32[1024,256]{1,0:T(8,128)} %get-tuple-element.150.dh_ref, ...), custom_call_target="tpu_custom_call" | custom-call | flops 2147483648 | bytes 20000000 | tf_op jit(solution)/shard_map/highway_back1/pallas_call | solution.py:726
  326.7 21.2 %collective-permute-done.39 = bf16[544,128]{1,0:T(8,128)(2,1)S(1)} collective-permute-done((bf16[544,128]{1,0:T(8,128)(2,1)S(1)}, bf16[544,128]{1,0:T(8,128)(2,1)S(1)}, u32[]{:S(2)}, u32[]{:S(2)}) %collective-permute-start.39) | collective-permute-done | bytes 139296 | tf_op jit(solution)/shard_map/ppermute | solution.py:412
  353.3 8.1 %highway_back0.1 = (bf16[1024,256]{1,0:T(8,128)(2,1)}, bf16[1024,256]{1,0:T(8,128)(2,1)}, f32[1024,256]{1,0:T(8,128)}, f32[8,512]{1,0:T(8,128)}, f32[4,1024,256]{2,1,0:T(8,128)}, /*index=5*/bf16[4,1024,256]{2,1,0:T(8,128)(2,1)}) custom-call(s32[1]{0:T(128)} %bitcast.d_ref.flag_ref, f32[1024,256]{1,0:T(8,128)} %add_add_fusion.1.dh_ref, ...), custom_call_target="tpu_custom_call" | custom-call | flops 2147483648 | bytes 20000000 | tf_op jit(solution)/shard_map/highway_back0/pallas_call | solution.py:726
  374.9 13.9 %collective-permute-done.45 = bf16[8,128,512]{2,1,0:T(8,128)(2,1)S(1)} collective-permute-done((bf16[8,128,512]{2,1,0:T(8,128)(2,1)S(1)}, bf16[8,128,512]{2,1,0:T(8,128)(2,1)S(1)}, u32[]{:S(2)}, u32[]{:S(2)}) %collective-permute-start.45) | collective-permute-done | bytes 1048608 | tf_op jit(solution)/shard_map/ppermute | solution.py:454
  400.7 8.3 %collective-permute-done.46 = bf16[544,128]{1,0:T(8,128)(2,1)S(1)} collective-permute-done((bf16[544,128]{1,0:T(8,128)(2,1)S(1)}, bf16[544,128]{1,0:T(8,128)(2,1)S(1)}, u32[]{:S(2)}, u32[]{:S(2)}) %collective-permute-start.46) | collective-permute-done | bytes 139296 | tf_op jit(solution)/shard_map/ppermute | solution.py:412
  414.5 12.3 %char_back.1 = (bf16[1024,256]{1,0:T(8,128)(2,1)}, f32[4,128,896]{2,1,0:T(8,128)}, bf16[4,128,896]{2,1,0:T(8,128)(2,1)}) custom-call(s32[1]{0:T(128)} %bitcast.d_ref.flag_ref, f32[1024,256]{1,0:T(8,128)} %get-tuple-element.119.refs_11_.h_ref, s32[1024,256]{1,0:T(8,128)} %get-tuple-element.132.at_ref, f32[1024,256]{1,0:T(8,128)} %add_add_fusion.dh_ref, ...), custom_call_target="tpu_custom_call" | custom-call | flops 8000000000 | bytes 6889472 | tf_op jit(solution)/shard_map/char_back/pallas_call | solution.py:486
  444.8 9.7 %conv_grad.1 = f32[120,256]{1,0:T(8,128)} custom-call(s32[1]{0:T(128)} %bitcast.d_ref.flag_ref, bf16[1024,1024]{1,0:T(8,128)(2,1)} %get-tuple-element.131.x_ref, s32[1024,256]{1,0:T(8,128)} %get-tuple-element.132.at_ref, bf16[1024,256]{1,0:T(8,128)(2,1)} %get-tuple-element.184.gp_ref), custom_call_target="tpu_custom_call" | custom-call | flops 8000000000 | bytes 3792896 | tf_op jit(solution)/shard_map/conv_grad/pallas_call | solution.py:486
  460.5 23.1 %collective-permute-done.53 = bf16[768,768]{1,0:T(8,128)(2,1)S(1)} collective-permute-done((bf16[768,768]{1,0:T(8,128)(2,1)}, bf16[768,768]{1,0:T(8,128)(2,1)S(1)}, u32[]{:S(2)}, u32[]{:S(2)}) %collective-permute-start.53) | collective-permute-done | bytes 1179680 | tf_op jit(solution)/shard_map/ppermute | solution.py:454
  521.8 57.2 %collective-permute-done.59 = f32[168,256]{1,0:T(8,128)S(1)} collective-permute-done((f32[168,256]{1,0:T(8,128)S(1)}, f32[168,256]{1,0:T(8,128)S(1)}, u32[]{:S(2)}, u32[]{:S(2)}) %collective-permute-start.59) | collective-permute-done | bytes 172064 | tf_op jit(solution)/shard_map/ppermute | solution.py:412
  600.6 8.3 %collective-permute-done.63.refs_4_ = f32[168,256]{1,0:T(8,128)} collective-permute-done((f32[168,256]{1,0:T(8,128)}, f32[168,256]{1,0:T(8,128)}, u32[]{:S(2)}, u32[]{:S(2)}) %collective-permute-start.63) | collective-permute-done | bytes 172064 | tf_op jit(solution)/shard_map/ppermute | solution.py:412
  (372 shorter events, 282.4 us)
Async XLA Ops:
  27.6 53.5 %all-to-all-start = ((bf16[8,2,256,256]{3,2,1,0:T(8,128)(2,1)}), bf16[8,2,256,256]{3,2,1,0:T(8,128)(2,1)S(1)}, u32[]{:S(2)}, u32[]{:S(2)}) async-start(bf16[8,2,256,256]{3,2,1,0:T(8,128)(2,1)} %get-tuple-element.115), calls=%async_computation | async-start | bytes 4194304 | tf_op jit(solution)/shard_map/all_to_all | solution.py:1332
  32.0 183.9 %all-gather.5.cloned.1.call-start = ((), (), s32[]{:S(2)}) async-start(), calls=%async_computation.9 | async-start | bytes 15925248 | tf_op jit(solution)/shard_map/all_gather | solution.py:1371
  84.8 70.8 %all-to-all-start.1 = ((bf16[8,2,256,256]{3,2,1,0:T(8,128)(2,1)}), bf16[8,2,256,256]{3,2,1,0:T(8,128)(2,1)S(1)}, u32[]{:S(2)}, u32[]{:S(2)}) async-start(bf16[8,2,256,256]{3,2,1,0:T(8,128)(2,1)} %get-tuple-element.122), calls=%async_computation.1 | async-start | bytes 4194304 | tf_op jit(solution)/shard_map/all_to_all | solution.py:1369
  88.5 306.8 %reduce-scatter.3.cloned.1.call-start = ((), (), s32[]{:S(2)}) async-start(), calls=%async_computation.7 | async-start | bytes 16146432 | tf_op jit(solution)/shard_map/reduce_scatter | solution.py:1429
  96.3 49.4 %collective-permute-start.19 = (bf16[1024,256]{1,0:T(8,128)(2,1)}, bf16[1024,256]{1,0:T(8,128)(2,1)S(1)}, u32[]{:S(2)}, u32[]{:S(2)}) collective-permute-start(bf16[1024,256]{1,0:T(8,128)(2,1)} %get-tuple-element.120.refs_0_), channel_id=1, source_target_pairs={{0,24},{4,28},{8,16},{12,20},{16,8},{20,12},{24,0},{28,4},{1,25},{... | collective-permute-start | bytes 1572872 | tf_op jit(solution)/shard_map/ppermute | solution.py:412
  99.1 54.3 %collective-permute-start.17 = (bf16[1024,256]{1,0:T(8,128)(2,1)}, bf16[1024,256]{1,0:T(8,128)(2,1)S(1)}, u32[]{:S(2)}, u32[]{:S(2)}) collective-permute-start(bf16[1024,256]{1,0:T(8,128)(2,1)} %get-tuple-element.120.refs_0_), channel_id=1, source_target_pairs={{0,16},{4,20},{8,24},{12,28},{16,0},{20,4},{24,8},{28,12},{1,17},{... | collective-permute-start | bytes 1572872 | tf_op jit(solution)/shard_map/ppermute | solution.py:412
  99.6 56.0 %collective-permute-start.15 = (bf16[1024,256]{1,0:T(8,128)(2,1)}, bf16[1024,256]{1,0:T(8,128)(2,1)}, u32[]{:S(2)}, u32[]{:S(2)}) collective-permute-start(bf16[1024,256]{1,0:T(8,128)(2,1)} %get-tuple-element.120.refs_0_), channel_id=1, source_target_pairs={{0,8},{4,12},{8,0},{12,4},{16,24},{20,28},{24,16},{28,20},{1,9},{5... | collective-permute-start | bytes 1572872 | tf_op jit(solution)/shard_map/ppermute | solution.py:412
  99.8 55.8 %collective-permute-start.14 = (bf16[1024,256]{1,0:T(8,128)(2,1)}, bf16[1024,256]{1,0:T(8,128)(2,1)}, u32[]{:S(2)}, u32[]{:S(2)}) collective-permute-start(bf16[1024,256]{1,0:T(8,128)(2,1)} %get-tuple-element.120.refs_0_), channel_id=1, source_target_pairs={{0,4},{4,0},{8,12},{12,8},{16,20},{20,16},{24,28},{28,24},{1,5},{5... | collective-permute-start | bytes 1572872 | tf_op jit(solution)/shard_map/ppermute | solution.py:412
  255.9 237.1 %reduce-scatter.5.cloned.1.call-start = ((), (), s32[]{:S(2)}) async-start(), calls=%async_computation.8 | async-start | bytes 2621440 | tf_op jit(solution)/shard_map/reduce_scatter | solution.py:1488
  314.9 32.9 %collective-permute-start.40 = (bf16[8,128,512]{2,1,0:T(8,128)(2,1)}, bf16[8,128,512]{2,1,0:T(8,128)(2,1)S(1)}, u32[]{:S(2)}, u32[]{:S(2)}) collective-permute-start(bf16[8,128,512]{2,1,0:T(8,128)(2,1)} %get-tuple-element.159), channel_id=1, source_target_pairs={{0,1},{3,2},{4,5},{7,6},{8,9},{11,10},{12,13},{15,14},{16,17},{19,... | collective-permute-start | bytes 3145736 | tf_op jit(solution)/shard_map/ppermute | solution.py:454
  371.4 40.4 %collective-permute-start.50 = (bf16[1024,256]{1,0:T(8,128)(2,1)}, bf16[1024,256]{1,0:T(8,128)(2,1)}, u32[]{:S(2)}, u32[]{:S(2)}) collective-permute-start(bf16[1024,256]{1,0:T(8,128)(2,1)} %get-tuple-element.280), channel_id=1, source_target_pairs={{0,24},{4,28},{8,16},{12,20},{16,8},{20,12},{24,0},{28,4},{1,25},{... | collective-permute-start | bytes 1572872 | tf_op jit(solution)/shard_map/ppermute | solution.py:412
  372.5 39.3 %collective-permute-start.49 = (bf16[1024,256]{1,0:T(8,128)(2,1)}, bf16[1024,256]{1,0:T(8,128)(2,1)}, u32[]{:S(2)}, u32[]{:S(2)}) collective-permute-start(bf16[1024,256]{1,0:T(8,128)(2,1)} %get-tuple-element.281), channel_id=1, source_target_pairs={{0,16},{4,20},{8,24},{12,28},{16,0},{20,4},{24,8},{28,12},{1,17},{... | collective-permute-start | bytes 1572872 | tf_op jit(solution)/shard_map/ppermute | solution.py:412
  373.9 37.9 %collective-permute-start.48 = (bf16[1024,256]{1,0:T(8,128)(2,1)}, bf16[1024,256]{1,0:T(8,128)(2,1)}, u32[]{:S(2)}, u32[]{:S(2)}) collective-permute-start(bf16[1024,256]{1,0:T(8,128)(2,1)} %get-tuple-element.279), channel_id=1, source_target_pairs={{0,8},{4,12},{8,0},{12,4},{16,24},{20,28},{24,16},{28,20},{1,9},{5... | collective-permute-start | bytes 1572872 | tf_op jit(solution)/shard_map/ppermute | solution.py:412
  429.2 70.8 %collective-permute-start.67 = (bf16[8,128,512]{2,1,0:T(8,128)(2,1)}, bf16[8,128,512]{2,1,0:T(8,128)(2,1)}, u32[]{:S(2)}, u32[]{:S(2)}) collective-permute-start(bf16[8,128,512]{2,1,0:T(8,128)(2,1)} %add.280), channel_id=1, source_target_pairs={{1,0},{2,3},{5,4},{6,7},{9,8},{10,11},{13,12},{14,15},{17,16},{18,... | collective-permute-start | bytes 3145736 | tf_op jit(solution)/shard_map/ppermute | solution.py:454
  437.0 46.5 %collective-permute-start.53 = (bf16[768,768]{1,0:T(8,128)(2,1)}, bf16[768,768]{1,0:T(8,128)(2,1)S(1)}, u32[]{:S(2)}, u32[]{:S(2)}) collective-permute-start(bf16[768,768]{1,0:T(8,128)(2,1)} %slice.204), channel_id=1, source_target_pairs={{0,1},{3,2},{4,5},{7,6},{8,9},{11,10},{12,13},{15,14},{16,17},{19,... | collective-permute-start | bytes 3538952 | tf_op jit(solution)/shard_map/ppermute | solution.py:454
  441.0 51.1 %collective-permute-start.55 = (bf16[128,896]{1,0:T(8,128)(2,1)}, bf16[128,896]{1,0:T(8,128)(2,1)S(1)}, u32[]{:S(2)}, u32[]{:S(2)}) collective-permute-start(bf16[128,896]{1,0:T(8,128)(2,1)} %get-tuple-element.287), channel_id=1, source_target_pairs={{0,8},{4,12},{8,0},{12,4},{16,24},{20,28},{24,16},{28,20},{1,9},{5... | collective-permute-start | bytes 688136 | tf_op jit(solution)/shard_map/ppermute | solution.py:412
  443.5 137.6 %collective-permute-start.68 = (bf16[8,128,512]{2,1,0:T(8,128)(2,1)}, bf16[8,128,512]{2,1,0:T(8,128)(2,1)}, u32[]{:S(2)}, u32[]{:S(2)}) collective-permute-start(bf16[8,128,512]{2,1,0:T(8,128)(2,1)} %add.288), channel_id=1, source_target_pairs={{1,0},{2,3},{5,4},{6,7},{9,8},{10,11},{13,12},{14,15},{17,16},{18,... | collective-permute-start | bytes 3145736 | tf_op jit(solution)/shard_map/ppermute | solution.py:454
  484.7 96.5 %collective-permute-start.69 = (bf16[656,768]{1,0:T(8,128)(2,1)S(1)}, bf16[656,768]{1,0:T(8,128)(2,1)}, u32[]{:S(2)}, u32[]{:S(2)}) collective-permute-start(bf16[656,768]{1,0:T(8,128)(2,1)S(1)} %fusion.14), channel_id=1, source_target_pairs={{1,2},{2,1},{5,6},{6,5},{9,10},{10,9},{13,14},{14,13},{17,18},{18,... | collective-permute-start | bytes 3022856 | tf_op jit(solution)/shard_map/ppermute | solution.py:454
  490.5 103.7 %collective-permute-start.71 = (bf16[768,768]{1,0:T(8,128)(2,1)}, bf16[768,768]{1,0:T(8,128)(2,1)}, u32[]{:S(2)}, u32[]{:S(2)}) collective-permute-start(bf16[768,768]{1,0:T(8,128)(2,1)} %slice_add_fusion), channel_id=1, source_target_pairs={{1,2},{2,1},{5,6},{6,5},{9,10},{10,9},{13,14},{14,13},{17,18},{18,... | collective-permute-start | bytes 3538952 | tf_op jit(solution)/shard_map/ppermute | solution.py:454
  506.3 80.8 %all-to-all-start.3 = ((bf16[8,128,512]{2,1,0:T(8,128)(2,1)}), bf16[8,128,512]{2,1,0:T(8,128)(2,1)S(1)}, u32[]{:S(2)}, u32[]{:S(2)}) async-start(bf16[8,128,512]{2,1,0:T(8,128)(2,1)} %broadcast_select_fusion.2), calls=%async_computation.5 | async-start | bytes 2097152 | tf_op jit(solution)/shard_map/all_to_all | solution.py:1615
  509.9 130.2 %all-gather.7.cloned.1.call-start = ((), (), s32[]{:S(2)}) async-start(), calls=%async_computation.10 | async-start | bytes 2621440 | tf_op jit(solution)/shard_map/all_gather | solution.py:1492
  520.5 58.4 %collective-permute-start.59 = (f32[168,256]{1,0:T(8,128)S(1)}, f32[168,256]{1,0:T(8,128)S(1)}, u32[]{:S(2)}, u32[]{:S(2)}) collective-permute-start(f32[168,256]{1,0:T(8,128)S(1)} %fusion.13), channel_id=1, source_target_pairs={{0,2},{1,3},{2,0},{3,1},{4,6},{5,7},{6,4},{7,5},{8,10},{9,11},{10,... | collective-permute-start | bytes 516104 | tf_op jit(solution)/shard_map/ppermute | solution.py:412
  583.6 40.6 %collective-permute-start.70 = (bf16[656,768]{1,0:T(8,128)(2,1)}, bf16[656,768]{1,0:T(8,128)(2,1)}, u32[]{:S(2)}, u32[]{:S(2)}) collective-permute-start(bf16[656,768]{1,0:T(8,128)(2,1)} %add.301), channel_id=1, source_target_pairs={{1,0},{2,3},{5,4},{6,7},{9,8},{10,11},{13,12},{14,15},{17,16},{18,... | collective-permute-start | bytes 3022856 | tf_op jit(solution)/shard_map/ppermute | solution.py:454
  596.1 34.7 %collective-permute-start.72 = (bf16[768,768]{1,0:T(8,128)(2,1)S(1)}, bf16[768,768]{1,0:T(8,128)(2,1)S(1)}, u32[]{:S(2)}, u32[]{:S(2)}) collective-permute-start(bf16[768,768]{1,0:T(8,128)(2,1)S(1)} %add.302), channel_id=1, source_target_pairs={{1,0},{2,3},{5,4},{6,7},{9,8},{10,11},{13,12},{14,15},{17,16},{18,... | collective-permute-start | bytes 3538952 | tf_op jit(solution)/shard_map/ppermute | solution.py:454
  (111 other events, 1136.9 us)
Sparse Core Ops, SparseCore 0:
  84.9 126.2 all-gather.4
  256.0 115.7 reduce-scatter.2
  395.4 43.9 reduce-scatter.4
  512.0 66.8 all-gather.6

commit v4 on v3

--- a/solution.py
+++ b/solution.py
@@ -436,10 +436,14 @@
     ]
 
 
-def plane_total(parts, after=()):
+def plane_others(parts):
+    return [plane_swap(part, 2 * i) for i, part in enumerate(parts[1:], 1)]
+
+
+def plane_total(parts, after=(), others=None):
     total = tie(parts[0], *after)
-    for i, part in enumerate(parts[1:], 1):
-        total = total + plane_swap(part, 2 * i).astype(f32)
+    for piece in others or plane_others(parts):
+        total = total + piece.astype(f32)
     return total
 
 
@@ -946,16 +950,22 @@
     table_ref[...] = total
 
 
-def finish_encoder_body(d_ref, low_ref, high_ref, *outs):
-    dim = low_ref.shape[1]
+def finish_encoder_body(middle_ref, whole_ref, third_ref, *outs):
+    middle = middle_ref[0] == 1
+    dim = whole_ref.shape[1]
     at = 0
     for ref in outs:
         count = ref.shape[0]
         for left in range(0, ref.shape[1], dim):
-            low = low_ref.shape[0]
-            source = low_ref[at : at + count] if at < low else high_ref[at - low : at - low + count]
-            ref[:, left : left + dim] = source.astype(f32)
+            rows = slice(at, at + count)
+            ref[:, left : left + dim] = jnp.where(
+                middle, whole_ref[rows].astype(f32), third_ref[rows].astype(f32)
+            )
             at += count
+
+
+def corner(value):
+    return value.reshape((-1,) + value.shape[-2:])[0, :16, :128]
 
 
 def normalize(value):
@@ -1448,10 +1458,12 @@
     )
     top_own = lax.dynamic_slice_in_dim(top_sums, d * part, part, 1)
     top_own = jnp.pad(top_own, ((0, 0), (0, 128 - part)))
+    wide_rows = round_up(round_up(seq_len + 32, model_dim // 128) // (model_dim // 128), 16)
     top_all = lax.dynamic_update_slice_in_dim(
-        jnp.zeros((seq_len + 32, 128), f32), top_own[words:], seq_len, 0
+        jnp.zeros((wide_rows * (model_dim // 128), 128), f32), top_own[words:], seq_len, 0
     )
     top_all = lax.dynamic_update_slice_in_dim(top_all, top_own[:words], z * words, 0).astype(bf16)
+    top_all = jnp.concatenate(jnp.split(top_all, model_dim // 128), axis=1)
     cut = (4 + in_parts) * part
     gate_parts = {}
     middle = (z == 1) | (z == 2)
@@ -1463,12 +1475,11 @@
         )
         parts = plane_parts(keep, send)
         gate_parts[layer] = jnp.sum(sums, axis=0).reshape(2, own)
-        after = []
+        others = plane_others(parts)
         if layer == 0:
             enc_slice = tie(enc_slice, parts[1])
-            chain[1] = chain[1] + tie(steps[1], parts[1])
+            chain[1] = chain[1] + tie(steps[1], others[0])
             steps[1] = line_step(chain[1], 1)
-            after = [chain[1]]
         shapes = (
             [((DEPTH, PLANE, own // DEPTH, 2 * own), bf16)]
             if layer == 0
@@ -1478,29 +1489,27 @@
             highway_grad_body,
             shapes,
             dvec,
-            (*blocks, tie(ga, parts[1], *after), gb),
+            (*blocks, tie(ga, parts[1]), gb),
             name=f"highway_grad{layer}",
             flops=2 * all_words * filters * 2 * own,
         )
-        top_all = tie(top_all, parts[1])
-        top_all = top_all + swap(top_all, "seq", DEPTH, 1 if layer else 2)
         if layer == 0:
             quarter = lax.psum_scatter(
                 tie(grads[0], enc_slice), "seq", scatter_dimension=0, tiled=False
             )
             quarter = lax.all_to_all(quarter, "dp", 0, 0)
             lowest = lax.all_gather(quarter, "seq", axis=0, tiled=False)
-            chain[0] = chain[0] + tie(steps[0], grads[0])
+            chain[0] = chain[0] + tie(steps[0], grads[0], others[0])
             steps[0] = line_step(chain[0], 2)
-            after = [grads[0], top_all, enc_slice, chain[0]]
+            after = [grads[0], enc_slice, *chain]
         else:
             chain = list(grads)
             steps = [line_step(value, 0) for value in chain]
             chain[0] = chain[0] + tie(steps[0], parts[1])
             steps[0] = line_step(chain[0], 1)
-            after = [*grads, top_all, chain[0]]
-        d_hidden = d_carry + plane_total(parts, after)
-    lines = [enc_slice[:cut], jnp.concatenate([enc_slice[cut:], proj_grad], axis=0)]
+            after = [*grads, chain[0]]
+        d_hidden = d_carry + plane_total(parts, after, others)
+    lines = [enc_slice[:cut], jnp.concatenate([enc_slice[cut:], proj_grad, top_all], axis=0)]
     moved = [line_step(value, 0) for value in lines]
     d_hidden = tie(d_hidden, *lines)
 
@@ -1582,25 +1591,22 @@
 
     lines = [value + tie(piece, ends) for value, piece in zip(lines, moved)]
     moved = [line_step(value, 2) for value in lines]
-    enc_total = [jnp.where(middle, value, piece) for value, piece in zip(lines, moved)]
-    proj_total = enc_total[1][-own:]
-    top_total = top_all[:, :part].astype(f32)
+    middle_flag = middle.astype(jnp.int32)[None]
+    outer_total, small_total, proj_total, top_total = call(
+        finish_encoder_body,
+        [
+            ((ff_dim // PLANE, model_dim), f32),
+            ((16, model_dim), f32),
+            ((own, model_dim), f32),
+            ((wide_rows, model_dim), f32),
+        ],
+        middle_flag,
+        (lines[1], moved[1]),
+        name="finish_high",
+    )
+    top_total = jnp.concatenate(jnp.split(top_total, model_dim // 128, axis=1))[:, :part]
     pos_total = top_total[:seq_len]
     gain0, shift0, bias0 = top_total[seq_len], top_total[seq_len + 1], top_total[seq_len + 16]
-    proj_total = proj_total.astype(f32)
-    qkv_total, out_total, inner_total, outer_total, small_total = call(
-        finish_encoder_body,
-        [
-            ((part, 3 * model_dim), f32),
-            ((part, model_dim), f32),
-            ((part, ff_dim), f32),
-            ((ff_dim // PLANE, model_dim), f32),
-            ((16, model_dim), f32),
-        ],
-        dvec,
-        enc_total,
-        name="finish_encoder",
-    )
     own_small = lax.dynamic_slice_in_dim(small_total, d * part, part, 1)
     bias_total = jnp.concatenate([bias0[None], own_small[1:5]], axis=0)
     gain_total = jnp.concatenate([gain0[None], own_small[6:8]], axis=0)
@@ -1615,6 +1621,13 @@
     pieces = [lax.all_to_all(value, "dp", 0, 0) for value in chain]
     hw_total = finish_highway(1, depth, pieces, None)
     hw_total = finish_highway(0, depth, [lowest], hw_total)
+    qkv_total, out_total, inner_total = call(
+        finish_encoder_body,
+        [((part, 3 * model_dim), f32), ((part, model_dim), f32), ((part, ff_dim), f32)],
+        middle_flag,
+        (lines[0], tie(moved[0], corner(hw_total), outer_total[:8, :128])),
+        name="finish_low",
+    )
     hw_bias_totals = []
     for layer in range(depth):
         row = gate_sums[2 * layer : 2 * layer + 2].reshape(-1)

time: 659 us -> 629 us (0.954)
  waiting for transfers between devices: 304 us -> 266 us
    ppermute x61 -> x59, waiting for transfers between devices: 253 us -> 188 us  [swap(): lax.ppermute(value, axis_name, [(at, at ^ offset) for at in range(size)])]
    ppermute x12, waiting for transfers between devices: 45.7 us -> 73.8 us  [line_step(): return lax.ppermute(value, 'seq', LINE_STEPS[step])]
    unnamed x113 -> x123, local copies, waits for them, and re-layouts: 12 us -> 14.9 us
    pallas_call x11 -> x12, Pallas kernels: 67.5 us -> 70.1 us  [call(): pl.pallas_call(body, out_shape=[jax.ShapeDtypeStruct(s, t) for s, t in ou...]
    ppermute x61 -> x59, starting transfers between devices: 54.9 us -> 54.2 us  [swap(): lax.ppermute(value, axis_name, [(at, at ^ offset) for at in range(size)])]
  transfers between devices with their start and end apart: 82 -> 80, of which waited for: 35 -> 39; matrix products, arithmetic and copies ran while one was open for 10% -> 11% of each run, Pallas kernels for 17% -> 18%
where the time goes in v4:
time: 629 us; the launch traced here: 621 us
  waiting for transfers between devices  266 us (42%)
  Pallas kernels  153 us (24%)
  starting transfers between devices  110 us (17%)
  other arithmetic  47 us (7%)
  local copies, waits for them, and re-layouts  30.2 us (5%)
  between operations  14.8 us (2%)
    ppermute x59, waiting for transfers between devices, swap(): lax.ppermute(value, axis_name, [(at, at ^ offset) for at in range(size)])  188 us
    ppermute x12, waiting for transfers between devices, line_step(): return lax.ppermute(value, 'seq', LINE_STEPS[step])  73.8 us
    pallas_call x12, Pallas kernels, call(): pl.pallas_call(body, out_shape=[jax.ShapeDtypeStruct(s, t) for s, t in ou...  70.1 us
    ppermute x59, starting transfers between devices, swap(): lax.ppermute(value, axis_name, [(at, at ^ offset) for at in range(size)])  54.2 us
    ppermute x12, starting transfers between devices, line_step(): return lax.ppermute(value, 'seq', LINE_STEPS[step])  36.2 us
    pallas_call x1, Pallas kernels, encoder(): pl.pallas_call(functools.partial(encoder_body, head_count, in_parts), out...  23.9 us
    pallas_call x2, Pallas kernels, highway_back(): pl.pallas_call(highway_back_body, grid=(4,), out_shape=[jax.ShapeDtypeStr...  16.2 us
    pallas_call x2, Pallas kernels, highway(): pl.pallas_call(functools.partial(highway_body, layer), grid=(4,), out_sha...  16.2 us
  transfers between devices with their start and end apart: 80, of which 39 were waited for; matrix products, arithmetic and copies ran while one was open for 11% of the time, Pallas kernels for 18%

profile of v4, /device:TPU:0, one launch (start us, length us, event | category | flops | bytes accessed | tf_op | source)
XLA Modules:
  0.0 621.0 jit_solution(1015996583294518395)
XLA Ops:
  37.6 12.1 %conv.1 = (f32[1024,256]{1,0:T(8,128)}, bf16[1024,256]{1,0:T(8,128)(2,1)}, s32[1024,256]{1,0:T(8,128)}, bf16[1024,1024]{1,0:T(8,128)(2,1)}, f32[16,256]{1,0:T(8,...) custom-call(s32[1]{0:T(128)} %bitcast.d_ref.flag_ref, bf16[160,896]{1,0:T(8,128)(2,1)} %lookup.1.refs_0_, ...), custom_call_target="tpu_custom_call" | custom-call | flops 8000000000 | bytes 7974912 | tf_op jit(solution)/shard_map/conv/pallas_call | solution.py:490
  58.1 12.3 %collective-permute-done.12.refs_6_ = bf16[1024,256]{1,0:T(8,128)(2,1)S(1)} collective-permute-done((bf16[1024,256]{1,0:T(8,128)(2,1)}, bf16[1024,256]{1,0:T(8,128)(2,1)S(1)}, u32[]{:S(2)}, u32[]{:S(2)}) %collective-permute-start.12) | collective-permute-done | bytes 524320 | tf_op jit(solution)/shard_map/ppermute | solution.py:412
  70.4 10.7 %collective-permute-done.10.refs_4_ = bf16[1024,256]{1,0:T(8,128)(2,1)S(1)} collective-permute-done((bf16[1024,256]{1,0:T(8,128)(2,1)}, bf16[1024,256]{1,0:T(8,128)(2,1)S(1)}, u32[]{:S(2)}, u32[]{:S(2)}) %collective-permute-start.10) | collective-permute-done | bytes 524320 | tf_op jit(solution)/shard_map/ppermute | solution.py:412
  88.5 7.7 %highway0.1 = (f32[1024,256]{1,0:T(8,128)}, f32[1024,256]{1,0:T(8,128)}, f32[1024,256]{1,0:T(8,128)}, bf16[1024,256]{1,0:T(8,128)(2,1)}) custom-call(s32[1]{0:T(128)} %bitcast.d_ref.flag_ref, bf16[1024,256]{1,0:T(8,128)(2,1)} %get-tuple-element.114.refs_0_, bf16[1024,256]{1,0:T(8,128)(2,1)} %collective-permute-done.7.refs_1_, ...), custom_call_target="tpu_custom_call" | custom-call | flops 2147483648 | bytes 12000000 | tf_op jit(solution)/shard_map/highway0/pallas_call | solution.py:647
  99.8 45.8 %collective-permute-done.19.refs_6_ = bf16[1024,256]{1,0:T(8,128)(2,1)S(1)} collective-permute-done((bf16[1024,256]{1,0:T(8,128)(2,1)}, bf16[1024,256]{1,0:T(8,128)(2,1)S(1)}, u32[]{:S(2)}, u32[]{:S(2)}) %collective-permute-start.19) | collective-permute-done | bytes 524320 | tf_op jit(solution)/shard_map/ppermute | solution.py:412
  145.7 7.9 %collective-permute-done.17.refs_4_ = bf16[1024,256]{1,0:T(8,128)(2,1)S(1)} collective-permute-done((bf16[1024,256]{1,0:T(8,128)(2,1)}, bf16[1024,256]{1,0:T(8,128)(2,1)S(1)}, u32[]{:S(2)}, u32[]{:S(2)}) %collective-permute-start.17) | collective-permute-done | bytes 524320 | tf_op jit(solution)/shard_map/ppermute | solution.py:412
  157.9 8.4 %highway1.1 = (f32[1024,256]{1,0:T(8,128)}, f32[1024,256]{1,0:T(8,128)}, f32[1024,256]{1,0:T(8,128)}, bf16[1024,256]{1,0:T(8,128)(2,1)}) custom-call(s32[1]{0:T(128)} %bitcast.d_ref.flag_ref, bf16[1024,256]{1,0:T(8,128)(2,1)} %get-tuple-element.120.refs_0_, bf16[1024,256]{1,0:T(8,128)(2,1)} %collective-permute-done.14.refs_1_, ...), custom_call_target="tpu_custom_call" | custom-call | flops 2147483648 | bytes 12000000 | tf_op jit(solution)/shard_map/highway1/pallas_call | solution.py:647
  186.7 9.2 %collective-permute-done.24 = bf16[128,768]{1,0:T(8,128)(2,1)S(1)} collective-permute-done((bf16[128,768]{1,0:T(8,128)(2,1)S(1)}, bf16[128,768]{1,0:T(8,128)(2,1)S(1)}, u32[]{:S(2)}, u32[]{:S(2)}) %collective-permute-start.24) | collective-permute-done | bytes 196640 | tf_op jit(solution)/shard_map/ppermute | solution.py:412
  206.9 10.2 %collective-permute-done.26.e2_ref = bf16[128,768]{1,0:T(8,128)(2,1)S(1)} collective-permute-done((bf16[128,768]{1,0:T(8,128)(2,1)S(1)}, bf16[128,768]{1,0:T(8,128)(2,1)S(1)}, u32[]{:S(2)}, u32[]{:S(2)}) %collective-permute-start.26) | collective-permute-done | bytes 196640 | tf_op jit(solution)/shard_map/ppermute | solution.py:412
  217.9 23.9 %encoder.1 = (bf16[128,768]{1,0:T(8,128)(2,1)}, f32[128,768]{1,0:T(8,128)}, bf16[128,768]{1,0:T(8,128)(2,1)}, bf16[128,768]{1,0:T(8,128)(2,1)}, bf16[128,768]{1,...) custom-call(s32[1]{0:T(128)} %bitcast.d_ref.flag_ref, ...), custom_call_target="tpu_custom_call" | custom-call | flops 16000000000 | bytes 30000000 | tf_op jit(solution)/shard_map/encoder/pallas_call | solution.py:1243
  248.0 9.1 %encoder_grad.1 = bf16[8,1168,768]{2,1,0:T(8,128)(2,1)} custom-call(s32[1]{0:T(128)} %bitcast.d_ref.flag_ref, bf16[512,768]{1,0:T(8,128)(2,1)} %get-tuple-element.138.embs_ref, bf16[128,768]{1,0:T(8,128)(2,1)} %get-tuple-element.139.gq_ref, bf16[512,768]{1,0:T(8,128)(2,1)} %get-tuple-element.140.gk_ref, bf16[512,768]{1,0:T(8,128)(2,1)} %get-tuple-element.141.gv_ref, ...), custom_call_target="tpu_custom_call" | custom-call | flops 6000000000 | bytes 20000000 | tf_op jit(solution)/shard_map/encoder_grad/pallas_call | solution.py:1271
  260.8 11.7 %collective-permute-done.29 = bf16[128,768]{1,0:T(8,128)(2,1)S(1)} collective-permute-done((bf16[128,768]{1,0:T(8,128)(2,1)S(1)}, bf16[128,768]{1,0:T(8,128)(2,1)S(1)}, u32[]{:S(2)}, u32[]{:S(2)}) %collective-permute-start.29) | collective-permute-done | bytes 196640 | tf_op jit(solution)/shard_map/ppermute | solution.py:412
  293.7 8.2 %highway_back1.1 = (bf16[1024,256]{1,0:T(8,128)(2,1)}, bf16[1024,256]{1,0:T(8,128)(2,1)}, f32[1024,256]{1,0:T(8,128)}, f32[8,512]{1,0:T(8,128)}, f32[4,1024,256]{2,1,0:T(8,128)}, /*index=5*/bf16[4,1024,256]{2,1,0:T(8,128)(2,1)}) custom-call(s32[1]{0:T(128)} %bitcast.d_ref.flag_ref, f32[1024,256]{1,0:T(8,128)} %get-tuple-element.150.dh_ref, ...), custom_call_target="tpu_custom_call" | custom-call | flops 2147483648 | bytes 20000000 | tf_op jit(solution)/shard_map/highway_back1/pallas_call | solution.py:730
  326.1 19.3 %collective-permute-done.39 = bf16[8,128,512]{2,1,0:T(8,128)(2,1)S(1)} collective-permute-done((bf16[8,128,512]{2,1,0:T(8,128)(2,1)}, bf16[8,128,512]{2,1,0:T(8,128)(2,1)S(1)}, u32[]{:S(2)}, u32[]{:S(2)}) %collective-permute-start.39) | collective-permute-done | bytes 1048608 | tf_op jit(solution)/shard_map/ppermute | solution.py:458
  351.8 8.0 %highway_back0.1 = (bf16[1024,256]{1,0:T(8,128)(2,1)}, bf16[1024,256]{1,0:T(8,128)(2,1)}, f32[1024,256]{1,0:T(8,128)}, f32[8,512]{1,0:T(8,128)}, f32[4,1024,256]{2,1,0:T(8,128)}, /*index=5*/bf16[4,1024,256]{2,1,0:T(8,128)(2,1)}) custom-call(s32[1]{0:T(128)} %bitcast.d_ref.flag_ref, f32[1024,256]{1,0:T(8,128)} %add_add_fusion.1.dh_ref, ...), custom_call_target="tpu_custom_call" | custom-call | flops 2147483648 | bytes 20000000 | tf_op jit(solution)/shard_map/highway_back0/pallas_call | solution.py:730
  381.0 8.3 %collective-permute-done.46 = bf16[8,128,512]{2,1,0:T(8,128)(2,1)} collective-permute-done((bf16[8,128,512]{2,1,0:T(8,128)(2,1)}, bf16[8,128,512]{2,1,0:T(8,128)(2,1)}, u32[]{:S(2)}, u32[]{:S(2)}) %collective-permute-start.46) | collective-permute-done | bytes 1048608 | tf_op jit(solution)/shard_map/ppermute | solution.py:458
  401.8 12.4 %char_back.1 = (bf16[1024,256]{1,0:T(8,128)(2,1)}, f32[4,128,896]{2,1,0:T(8,128)}, bf16[4,128,896]{2,1,0:T(8,128)(2,1)}) custom-call(s32[1]{0:T(128)} %bitcast.d_ref.flag_ref, f32[1024,256]{1,0:T(8,128)} %get-tuple-element.119.refs_11_.h_ref, s32[1024,256]{1,0:T(8,128)} %get-tuple-element.132.at_ref, f32[1024,256]{1,0:T(8,128)} %add_add_fusion.dh_ref, ...), custom_call_target="tpu_custom_call" | custom-call | flops 8000000000 | bytes 6889472 | tf_op jit(solution)/shard_map/char_back/pallas_call | solution.py:490
  415.8 7.1 %collective-permute-start.52 = (bf16[752,768]{1,0:T(8,128)(2,1)}, bf16[752,768]{1,0:T(8,128)(2,1)}, u32[]{:S(2)}, u32[]{:S(2)}) collective-permute-start(bf16[752,768]{1,0:T(8,128)(2,1)} %pad_maximum_fusion), channel_id=1, source_target_pairs={{0,1},{3,2},{4,5},{7,6},{8,9},{11,10},{12,13},{15,14},{16,17},{19,... | collective-permute-start | bytes 3465224 | tf_op jit(solution)/shard_map/ppermute | solution.py:458
  438.9 9.7 %conv_grad.1 = f32[120,256]{1,0:T(8,128)} custom-call(s32[1]{0:T(128)} %bitcast.d_ref.flag_ref, bf16[1024,1024]{1,0:T(8,128)(2,1)} %get-tuple-element.131.x_ref, s32[1024,256]{1,0:T(8,128)} %get-tuple-element.132.at_ref, bf16[1024,256]{1,0:T(8,128)(2,1)} %get-tuple-element.182.gp_ref), custom_call_target="tpu_custom_call" | custom-call | flops 8000000000 | bytes 3792896 | tf_op jit(solution)/shard_map/conv_grad/pallas_call | solution.py:490
  452.6 20.1 %collective-permute-done.51 = bf16[768,768]{1,0:T(8,128)(2,1)S(1)} collective-permute-done((bf16[768,768]{1,0:T(8,128)(2,1)}, bf16[768,768]{1,0:T(8,128)(2,1)S(1)}, u32[]{:S(2)}, u32[]{:S(2)}) %collective-permute-start.51) | collective-permute-done | bytes 1179680 | tf_op jit(solution)/shard_map/ppermute | solution.py:458
  510.2 7.1 %collective-permute-done.57 = f32[168,256]{1,0:T(8,128)S(1)} collective-permute-done((f32[168,256]{1,0:T(8,128)S(1)}, f32[168,256]{1,0:T(8,128)S(1)}, u32[]{:S(2)}, u32[]{:S(2)}) %collective-permute-start.57) | collective-permute-done | bytes 172064 | tf_op jit(solution)/shard_map/ppermute | solution.py:412
  531.5 16.1 %collective-permute-done.63.refs_6_ = f32[168,256]{1,0:T(8,128)} collective-permute-done((f32[168,256]{1,0:T(8,128)}, f32[168,256]{1,0:T(8,128)}, u32[]{:S(2)}, u32[]{:S(2)}) %collective-permute-start.63) | collective-permute-done | bytes 172064 | tf_op jit(solution)/shard_map/ppermute | solution.py:412
  565.9 16.6 %collective-permute-done.68.third_ref = bf16[752,768]{1,0:T(8,128)(2,1)} collective-permute-done((bf16[752,768]{1,0:T(8,128)(2,1)S(1)}, bf16[752,768]{1,0:T(8,128)(2,1)}, u32[]{:S(2)}, u32[]{:S(2)}) %collective-permute-start.68) | collective-permute-done | bytes 1155104 | tf_op jit(solution)/shard_map/ppermute | solution.py:458
  596.7 9.6 %collective-permute-done.70.third_ref = bf16[768,768]{1,0:T(8,128)(2,1)S(1)} collective-permute-done((bf16[768,768]{1,0:T(8,128)(2,1)S(1)}, bf16[768,768]{1,0:T(8,128)(2,1)S(1)}, u32[]{:S(2)}, u32[]{:S(2)}) %collective-permute-start.70) | collective-permute-done | bytes 1179680 | tf_op jit(solution)/shard_map/ppermute | solution.py:458
  (375 shorter events, 294.6 us)
Async XLA Ops:
  27.6 53.5 %all-to-all-start = ((bf16[8,2,256,256]{3,2,1,0:T(8,128)(2,1)}), bf16[8,2,256,256]{3,2,1,0:T(8,128)(2,1)S(1)}, u32[]{:S(2)}, u32[]{:S(2)}) async-start(bf16[8,2,256,256]{3,2,1,0:T(8,128)(2,1)} %get-tuple-element.115), calls=%async_computation | async-start | bytes 4194304 | tf_op jit(solution)/shard_map/all_to_all | solution.py:1342
  32.0 185.2 %all-gather.5.cloned.1.call-start = ((), (), s32[]{:S(2)}) async-start(), calls=%async_computation.9 | async-start | bytes 15925248 | tf_op jit(solution)/shard_map/all_gather | solution.py:1381
  84.8 70.8 %all-to-all-start.1 = ((bf16[8,2,256,256]{3,2,1,0:T(8,128)(2,1)}), bf16[8,2,256,256]{3,2,1,0:T(8,128)(2,1)S(1)}, u32[]{:S(2)}, u32[]{:S(2)}) async-start(bf16[8,2,256,256]{3,2,1,0:T(8,128)(2,1)} %get-tuple-element.122), calls=%async_computation.1 | async-start | bytes 4194304 | tf_op jit(solution)/shard_map/all_to_all | solution.py:1379
  88.5 292.5 %reduce-scatter.3.cloned.1.call-start = ((), (), s32[]{:S(2)}) async-start(), calls=%async_computation.7 | async-start | bytes 16146432 | tf_op jit(solution)/shard_map/reduce_scatter | solution.py:1439
  96.3 49.4 %collective-permute-start.19 = (bf16[1024,256]{1,0:T(8,128)(2,1)}, bf16[1024,256]{1,0:T(8,128)(2,1)S(1)}, u32[]{:S(2)}, u32[]{:S(2)}) collective-permute-start(bf16[1024,256]{1,0:T(8,128)(2,1)} %get-tuple-element.120.refs_0_), channel_id=1, source_target_pairs={{0,24},{4,28},{8,16},{12,20},{16,8},{20,12},{24,0},{28,4},{1,25},{... | collective-permute-start | bytes 1572872 | tf_op jit(solution)/shard_map/ppermute | solution.py:412
  99.1 54.4 %collective-permute-start.17 = (bf16[1024,256]{1,0:T(8,128)(2,1)}, bf16[1024,256]{1,0:T(8,128)(2,1)S(1)}, u32[]{:S(2)}, u32[]{:S(2)}) collective-permute-start(bf16[1024,256]{1,0:T(8,128)(2,1)} %get-tuple-element.120.refs_0_), channel_id=1, source_target_pairs={{0,16},{4,20},{8,24},{12,28},{16,0},{20,4},{24,8},{28,12},{1,17},{... | collective-permute-start | bytes 1572872 | tf_op jit(solution)/shard_map/ppermute | solution.py:412
  99.7 56.0 %collective-permute-start.15 = (bf16[1024,256]{1,0:T(8,128)(2,1)}, bf16[1024,256]{1,0:T(8,128)(2,1)}, u32[]{:S(2)}, u32[]{:S(2)}) collective-permute-start(bf16[1024,256]{1,0:T(8,128)(2,1)} %get-tuple-element.120.refs_0_), channel_id=1, source_target_pairs={{0,8},{4,12},{8,0},{12,4},{16,24},{20,28},{24,16},{28,20},{1,9},{5... | collective-permute-start | bytes 1572872 | tf_op jit(solution)/shard_map/ppermute | solution.py:412
  99.8 55.8 %collective-permute-start.14 = (bf16[1024,256]{1,0:T(8,128)(2,1)}, bf16[1024,256]{1,0:T(8,128)(2,1)}, u32[]{:S(2)}, u32[]{:S(2)}) collective-permute-start(bf16[1024,256]{1,0:T(8,128)(2,1)} %get-tuple-element.120.refs_0_), channel_id=1, source_target_pairs={{0,4},{4,0},{8,12},{12,8},{16,20},{20,16},{24,28},{28,24},{1,5},{5... | collective-permute-start | bytes 1572872 | tf_op jit(solution)/shard_map/ppermute | solution.py:412
  257.1 223.3 %reduce-scatter.5.cloned.1.call-start = ((), (), s32[]{:S(2)}) async-start(), calls=%async_computation.8 | async-start | bytes 2621440 | tf_op jit(solution)/shard_map/reduce_scatter | solution.py:1497
  315.5 29.9 %collective-permute-start.39 = (bf16[8,128,512]{2,1,0:T(8,128)(2,1)}, bf16[8,128,512]{2,1,0:T(8,128)(2,1)S(1)}, u32[]{:S(2)}, u32[]{:S(2)}) collective-permute-start(bf16[8,128,512]{2,1,0:T(8,128)(2,1)} %get-tuple-element.159), channel_id=1, source_target_pairs={{0,1},{3,2},{4,5},{7,6},{8,9},{11,10},{12,13},{15,14},{16,17},{19,... | collective-permute-start | bytes 3145736 | tf_op jit(solution)/shard_map/ppermute | solution.py:458
  360.9 28.4 %collective-permute-start.46 = (bf16[8,128,512]{2,1,0:T(8,128)(2,1)}, bf16[8,128,512]{2,1,0:T(8,128)(2,1)}, u32[]{:S(2)}, u32[]{:S(2)}) collective-permute-start(bf16[8,128,512]{2,1,0:T(8,128)(2,1)} %get-tuple-element.160), channel_id=1, source_target_pairs={{0,1},{3,2},{4,5},{7,6},{8,9},{11,10},{12,13},{15,14},{16,17},{19,... | collective-permute-start | bytes 3145736 | tf_op jit(solution)/shard_map/ppermute | solution.py:458
  365.5 27.1 %collective-permute-start.44 = (bf16[8,128,512]{2,1,0:T(8,128)(2,1)S(1)}, bf16[8,128,512]{2,1,0:T(8,128)(2,1)}, u32[]{:S(2)}, u32[]{:S(2)}) collective-permute-start(bf16[8,128,512]{2,1,0:T(8,128)(2,1)S(1)} %add.259), channel_id=1, source_target_pairs={{1,2},{2,1},{5,6},{6,5},{9,10},{10,9},{13,14},{14,13},{17,18},{18,... | collective-permute-start | bytes 3145736 | tf_op jit(solution)/shard_map/ppermute | solution.py:458
  415.8 32.7 %collective-permute-start.52 = (bf16[752,768]{1,0:T(8,128)(2,1)}, bf16[752,768]{1,0:T(8,128)(2,1)}, u32[]{:S(2)}, u32[]{:S(2)}) collective-permute-start(bf16[752,768]{1,0:T(8,128)(2,1)} %pad_maximum_fusion), channel_id=1, source_target_pairs={{0,1},{3,2},{4,5},{7,6},{8,9},{11,10},{12,13},{15,14},{16,17},{19,... | collective-permute-start | bytes 3465224 | tf_op jit(solution)/shard_map/ppermute | solution.py:458
  423.7 63.6 %collective-permute-start.65 = (bf16[8,128,512]{2,1,0:T(8,128)(2,1)S(1)}, bf16[8,128,512]{2,1,0:T(8,128)(2,1)}, u32[]{:S(2)}, u32[]{:S(2)}) collective-permute-start(bf16[8,128,512]{2,1,0:T(8,128)(2,1)S(1)} %copy-done.5), channel_id=1, source_target_pairs={{1,0},{2,3},{5,4},{6,7},{9,8},{10,11},{13,12},{14,15},{17,16},{18,... | collective-permute-start | bytes 3145736 | tf_op jit(solution)/shard_map/ppermute | solution.py:458
  425.0 47.6 %collective-permute-start.51 = (bf16[768,768]{1,0:T(8,128)(2,1)}, bf16[768,768]{1,0:T(8,128)(2,1)S(1)}, u32[]{:S(2)}, u32[]{:S(2)}) collective-permute-start(bf16[768,768]{1,0:T(8,128)(2,1)} %slice.209), channel_id=1, source_target_pairs={{0,1},{3,2},{4,5},{7,6},{8,9},{11,10},{12,13},{15,14},{16,17},{19,... | collective-permute-start | bytes 3538952 | tf_op jit(solution)/shard_map/ppermute | solution.py:458
  433.2 46.3 %collective-permute-start.53 = (bf16[128,896]{1,0:T(8,128)(2,1)}, bf16[128,896]{1,0:T(8,128)(2,1)S(1)}, u32[]{:S(2)}, u32[]{:S(2)}) collective-permute-start(bf16[128,896]{1,0:T(8,128)(2,1)} %get-tuple-element.287), channel_id=1, source_target_pairs={{0,8},{4,12},{8,0},{12,4},{16,24},{20,28},{24,16},{28,20},{1,9},{5... | collective-permute-start | bytes 688136 | tf_op jit(solution)/shard_map/ppermute | solution.py:412
  437.5 80.5 %collective-permute-start.66 = (bf16[8,128,512]{2,1,0:T(8,128)(2,1)}, bf16[8,128,512]{2,1,0:T(8,128)(2,1)}, u32[]{:S(2)}, u32[]{:S(2)}) collective-permute-start(bf16[8,128,512]{2,1,0:T(8,128)(2,1)} %add.280), channel_id=1, source_target_pairs={{1,0},{2,3},{5,4},{6,7},{9,8},{10,11},{13,12},{14,15},{17,16},{18,... | collective-permute-start | bytes 3145736 | tf_op jit(solution)/shard_map/ppermute | solution.py:458
  475.3 42.8 %collective-permute-start.67 = (bf16[752,768]{1,0:T(8,128)(2,1)}, bf16[752,768]{1,0:T(8,128)(2,1)}, u32[]{:S(2)}, u32[]{:S(2)}) collective-permute-start(bf16[752,768]{1,0:T(8,128)(2,1)} %fusion.14), channel_id=1, source_target_pairs={{1,2},{2,1},{5,6},{6,5},{9,10},{10,9},{13,14},{14,13},{17,18},{18,... | collective-permute-start | bytes 3465224 | tf_op jit(solution)/shard_map/ppermute | solution.py:458
  494.6 29.1 %all-to-all-start.3 = ((bf16[8,128,512]{2,1,0:T(8,128)(2,1)}), bf16[8,128,512]{2,1,0:T(8,128)(2,1)S(1)}, u32[]{:S(2)}, u32[]{:S(2)}) async-start(bf16[8,128,512]{2,1,0:T(8,128)(2,1)} %broadcast_select_fusion.1), calls=%async_computation.5 | async-start | bytes 2097152 | tf_op jit(solution)/shard_map/all_to_all | solution.py:1621
  498.1 112.2 %all-gather.7.cloned.1.call-start = ((), (), s32[]{:S(2)}) async-start(), calls=%async_computation.10 | async-start | bytes 2621440 | tf_op jit(solution)/shard_map/all_gather | solution.py:1501
  508.6 50.6 %collective-permute-start.69 = (bf16[768,768]{1,0:T(8,128)(2,1)S(1)}, bf16[768,768]{1,0:T(8,128)(2,1)}, u32[]{:S(2)}, u32[]{:S(2)}) collective-permute-start(bf16[768,768]{1,0:T(8,128)(2,1)S(1)} %copy-done.1), channel_id=1, source_target_pairs={{1,2},{2,1},{5,6},{6,5},{9,10},{10,9},{13,14},{14,13},{17,18},{18,... | collective-permute-start | bytes 3538952 | tf_op jit(solution)/shard_map/ppermute | solution.py:458
  520.0 62.5 %collective-permute-start.68 = (bf16[752,768]{1,0:T(8,128)(2,1)S(1)}, bf16[752,768]{1,0:T(8,128)(2,1)}, u32[]{:S(2)}, u32[]{:S(2)}) collective-permute-start(bf16[752,768]{1,0:T(8,128)(2,1)S(1)} %add.293.whole_ref), channel_id=1, source_target_pairs={{1,0},{2,3},{5,4},{6,7},{9,8},{10,11},{13,12},{14,15},{17,16},{18,... | collective-permute-start | bytes 3465224 | tf_op jit(solution)/shard_map/ppermute | solution.py:458
  523.6 38.4 %all-to-all-start.4 = ((bf16[8,128,512]{2,1,0:T(8,128)(2,1)}), bf16[8,128,512]{2,1,0:T(8,128)(2,1)}, u32[]{:S(2)}, u32[]{:S(2)}) async-start(bf16[8,128,512]{2,1,0:T(8,128)(2,1)} %broadcast_select_fusion), calls=%async_computation.6 | async-start | bytes 2097152 | tf_op jit(solution)/shard_map/all_to_all | solution.py:1621
  560.7 45.5 %collective-permute-start.70 = (bf16[768,768]{1,0:T(8,128)(2,1)S(1)}, bf16[768,768]{1,0:T(8,128)(2,1)S(1)}, u32[]{:S(2)}, u32[]{:S(2)}) collective-permute-start(bf16[768,768]{1,0:T(8,128)(2,1)S(1)} %add.294.whole_ref), channel_id=1, source_target_pairs={{1,0},{2,3},{5,4},{6,7},{9,8},{10,11},{13,12},{14,15},{17,16},{18,... | collective-permute-start | bytes 3538952 | tf_op jit(solution)/shard_map/ppermute | solution.py:458
  (109 other events, 1123.8 us)
Sparse Core Ops, SparseCore 0:
  84.9 126.2 all-gather.4
  257.3 116.8 reduce-scatter.2
  381.1 43.4 reduce-scatter.4
  521.4 63.4 all-gather.6
